TPU v7x, 512 devices: a whole 4x8x8 slice. The times are simulated.
512 devices in a mesh: blk: 64 (over z, y_hi, core), split: 8 (over x, y_lo).
Axes of the slice: x: 4, y: 8 (y_hi: 4, y_lo: 2; y = y_hi * 2 + y_lo), z: 8, core: 2. Of those that a mesh axis runs over, the one named last changes fastest.
Arguments:
- user_factors: float32 [131072, 512], P(('blk', 'split')), may hold values from -2 to 2
- item_factors: float32 [8192, 512], P('blk'), may hold values from -2 to 2
- obs_items: int32 [131072, 4, 8], P(('blk', 'split')), may hold values from 0 to 127
- obs_conf: int32 [131072, 4, 8], P(('blk', 'split')), may hold values from 1 to 3
Outputs:
- users_out: float32 [131072, 512], P(('blk', 'split'))
- items_out: float32 [8192, 512], P(('blk', 'split'))
All inputs are finite; a program needn't handle non-finite values.
Results may differ from a plain program's by a relative error of at most 0.0003.
Values sent between devices are 32-bit elements; how exact they have to be, the bound alone decides.
No kernel may reach another device: no remote copies, remote signals or barrier semaphores. Data moves between devices by JAX's collectives and lax.ppermute only.
A program may use at most 64 MiB of HBM per device.

v0:
```python
import jax
import jax.numpy as jnp
from jax import lax
from jax.sharding import PartitionSpec as P

SUBS = 4


LEARN_RATE = 0.0005
CONF_SCALE = 0.5
RIDGE_COEF = 0.01


def passed_along(block, axis, distance):
    devices = range(lax.axis_size(axis))
    route = [((i - distance) % len(devices), i) for i in devices]
    return lax.ppermute(block, axis, route)


def dense_counts(obs_rows, conf_rows, slab_rows):
    columns = lax.broadcasted_iota(jnp.int32, (1, 1, slab_rows), 2)
    hits = jnp.where(
        obs_rows[:, :, None] == columns, conf_rows[:, :, None].astype(jnp.float32), jnp.float32(0.0)
    )
    return jnp.sum(hits, axis=1)


def block_step(user_rows, held, counts):
    scores = lax.dot_general(
        user_rows,
        held,
        (((1,), (1,)), ((), ())),
        precision=lax.Precision.HIGHEST,
        preferred_element_type=jnp.float32,
    )
    target = jnp.where(counts > 0, 1.0, 0.0).astype(jnp.float32)
    weights = 1.0 + CONF_SCALE * counts
    errors = weights * (scores - target)
    grad_user = (
        jnp.dot(errors, held, precision=lax.Precision.HIGHEST, preferred_element_type=jnp.float32)
        + RIDGE_COEF * user_rows
    )
    partial_grad = lax.dot_general(
        errors,
        user_rows,
        (((0,), (0,)), ((), ())),
        precision=lax.Precision.HIGHEST,
        preferred_element_type=jnp.float32,
    )
    return (user_rows - LEARN_RATE * grad_user, partial_grad)


def local(user_factors, item_factors, obs_items, obs_conf):
    slab_rows = item_factors.shape[0]
    share_rows = slab_rows // lax.axis_size("split")
    share_start = lax.axis_index("split") * share_rows
    user_rows = user_factors
    held = item_factors
    for step in range(SUBS):
        counts = dense_counts(obs_items[:, step, :], obs_conf[:, step, :], slab_rows)
        user_rows, partial_grad = block_step(user_rows, held, counts)
        total_grad = lax.psum(partial_grad, "split")
        held = held - LEARN_RATE * (total_grad + RIDGE_COEF * held)
        held = passed_along(held, "blk", -1)
    share_out = lax.dynamic_slice_in_dim(held, share_start, share_rows, 0)
    return (user_rows, share_out)


def solution(mesh):
    in_specs = (
        P(("blk", "split"), None),
        P("blk", None),
        P(("blk", "split"), None, None),
        P(("blk", "split"), None, None),
    )
    out_specs = (P(("blk", "split"), None), P(("blk", "split"), None))
    return jax.shard_map(local, mesh=mesh, in_specs=in_specs, out_specs=out_specs, check_vma=False)
```

profile of v0, /device:TPU:6, one launch (start us, length us, event | category | flops | bytes accessed | tf_op | source)
XLA Modules:
  0.0 401.3 jit_solution(9950264955979071427)
XLA Ops:
  9.0 1.3 select_reduce_fusion.3
  10.9 1.2 fusion.12
  12.4 87.0 %all-reduce.5.cloned.1.call-done = f32[128,512]{1,0:T(8,128)} async-done(((f32[128,512]{1,0:T(8,128)}), f32[128,512]{1,0:T(8,128)}) %all-reduce.5.cloned.1.call-update) | async-done | bytes 262160 | tf_op jit(solution)/shard_map/psum | solution.py:62
  99.4 1.0 multiply_subtract_fusion.3
  100.4 2.6 collective-permute-start
  103.0 1.3 select_reduce_fusion.2
  105.0 4.8 %collective-permute-done = f32[128,512]{1,0:T(8,128)S(1)} collective-permute-done((f32[128,512]{1,0:T(8,128)S(1)}, f32[128,512]{1,0:T(8,128)S(1)}, u32[]{:S(2)}, u32[]{:S(2)}) %collective-permute-start) | collective-permute-done | bytes 262176 | tf_op jit(solution)/shard_map/ppermute | solution.py:17
  110.3 1.2 fusion.13
  111.8 82.3 %all-reduce.7.cloned.1.call-done = f32[128,512]{1,0:T(8,128)} async-done(((f32[128,512]{1,0:T(8,128)}), f32[128,512]{1,0:T(8,128)}) %all-reduce.7.cloned.1.call-update) | async-done | bytes 262160 | tf_op jit(solution)/shard_map/psum | solution.py:62
  194.2 1.0 multiply_subtract_fusion.2
  195.2 2.6 collective-permute-start.1
  197.8 1.3 select_reduce_fusion.1
  199.7 4.8 %collective-permute-done.1 = f32[128,512]{1,0:T(8,128)S(1)} collective-permute-done((f32[128,512]{1,0:T(8,128)S(1)}, f32[128,512]{1,0:T(8,128)S(1)}, u32[]{:S(2)}, u32[]{:S(2)}) %collective-permute-start.1) | collective-permute-done | bytes 262176 | tf_op jit(solution)/shard_map/ppermute | solution.py:17
  205.1 1.2 fusion.14
  206.6 82.3 %all-reduce.9.cloned.1.call-done = f32[128,512]{1,0:T(8,128)} async-done(((f32[128,512]{1,0:T(8,128)}), f32[128,512]{1,0:T(8,128)}) %all-reduce.9.cloned.1.call-update) | async-done | bytes 262160 | tf_op jit(solution)/shard_map/psum | solution.py:62
  288.9 1.0 multiply_subtract_fusion.1
  289.9 2.6 collective-permute-start.2
  292.6 1.3 select_reduce_fusion
  294.5 4.8 %collective-permute-done.2 = f32[128,512]{1,0:T(8,128)S(1)} collective-permute-done((f32[128,512]{1,0:T(8,128)S(1)}, f32[128,512]{1,0:T(8,128)S(1)}, u32[]{:S(2)}, u32[]{:S(2)}) %collective-permute-start.2) | collective-permute-done | bytes 262176 | tf_op jit(solution)/shard_map/ppermute | solution.py:17
  299.9 1.2 fusion.15
  301.1 82.7 %all-reduce.11.cloned.1.call-done = f32[128,512]{1,0:T(8,128)} async-done(((f32[128,512]{1,0:T(8,128)}), f32[128,512]{1,0:T(8,128)}) %all-reduce.11.cloned.1.call-update) | async-done | bytes 262160 | tf_op jit(solution)/shard_map/psum | solution.py:62
  384.7 2.6 collective-permute-start.3
  387.4 1.4 fusion.1
  388.9 5.3 %collective-permute-done.3 = f32[128,512]{1,0:T(8,128)S(1)} collective-permute-done((f32[128,512]{1,0:T(8,128)S(1)}, f32[128,512]{1,0:T(8,128)S(1)}, u32[]{:S(2)}, u32[]{:S(2)}) %collective-permute-start.3) | collective-permute-done | bytes 262176 | tf_op jit(solution)/shard_map/ppermute | solution.py:17
  (31 shorter events, 8.7 us)
Async XLA Ops:
  7.2 3.1 copy-start
  7.2 92.2 %all-reduce.5.cloned.1.call-start = ((), (), s32[]{:S(2)}) async-start(), calls=%async_computation | async-start | bytes 524288 | tf_op jit(solution)/shard_map/psum | solution.py:62
  8.9 1.4 copy-start.1
  12.1 182.1 %all-reduce.7.cloned.1.call-start = ((), (), s32[]{:S(2)}) async-start(), calls=%async_computation.1 | async-start | bytes 524288 | tf_op jit(solution)/shard_map/psum | solution.py:62
  100.4 9.4 %collective-permute-start = (f32[128,512]{1,0:T(8,128)S(1)}, f32[128,512]{1,0:T(8,128)S(1)}, u32[]{:S(2)}, u32[]{:S(2)}) collective-permute-start(f32[128,512]{1,0:T(8,128)S(1)} %multiply_subtract_fusion.3), channel_id=1, source_target_pairs={{8,0},{16,8},{24,16},{32,24},{40,32},{48,40},{56,48},{64,56},{72,6... | collective-permute-start | bytes 786440 | tf_op jit(solution)/shard_map/ppermute | solution.py:17
  111.5 177.4 %all-reduce.9.cloned.1.call-start = ((), (), s32[]{:S(2)}) async-start(), calls=%async_computation.2 | async-start | bytes 524288 | tf_op jit(solution)/shard_map/psum | solution.py:62
  195.2 9.4 %collective-permute-start.1 = (f32[128,512]{1,0:T(8,128)S(1)}, f32[128,512]{1,0:T(8,128)S(1)}, u32[]{:S(2)}, u32[]{:S(2)}) collective-permute-start(f32[128,512]{1,0:T(8,128)S(1)} %multiply_subtract_fusion.2), channel_id=1, source_target_pairs={{8,0},{16,8},{24,16},{32,24},{40,32},{48,40},{56,48},{64,56},{72,6... | collective-permute-start | bytes 786440 | tf_op jit(solution)/shard_map/ppermute | solution.py:17
  206.3 177.4 %all-reduce.11.cloned.1.call-start = ((), (), s32[]{:S(2)}) async-start(), calls=%async_computation.3 | async-start | bytes 524288 | tf_op jit(solution)/shard_map/psum | solution.py:62
  289.9 9.4 %collective-permute-start.2 = (f32[128,512]{1,0:T(8,128)S(1)}, f32[128,512]{1,0:T(8,128)S(1)}, u32[]{:S(2)}, u32[]{:S(2)}) collective-permute-start(f32[128,512]{1,0:T(8,128)S(1)} %multiply_subtract_fusion.1), channel_id=1, source_target_pairs={{8,0},{16,8},{24,16},{32,24},{40,32},{48,40},{56,48},{64,56},{72,6... | collective-permute-start | bytes 786440 | tf_op jit(solution)/shard_map/ppermute | solution.py:17
  384.7 9.4 %collective-permute-start.3 = (f32[128,512]{1,0:T(8,128)S(1)}, f32[128,512]{1,0:T(8,128)S(1)}, u32[]{:S(2)}, u32[]{:S(2)}) collective-permute-start(f32[128,512]{1,0:T(8,128)S(1)} %multiply_subtract_fusion), channel_id=1, source_target_pairs={{8,0},{16,8},{24,16},{32,24},{40,32},{48,40},{56,48},{64,56},{72,6... | collective-permute-start | bytes 786440 | tf_op jit(solution)/shard_map/ppermute | solution.py:17
Sparse Core Ops, SparseCore 0:
  12.2 87.1 all-reduce.4
  111.6 82.4 all-reduce.6
  206.4 82.4 all-reduce.8
  301.2 82.5 all-reduce.10
where the time goes:
time: 405 us; the launch traced here: 401 us
  waiting for transfers between devices  354 us (87%)
  between operations  14 us (3%)
  starting transfers between devices  10.7 us (3%)
  matrix products  10.4 us (3%)
  other arithmetic  9.78 us (2%)
    psum x4, waiting for transfers between devices, local(): total_grad = lax.psum(partial_grad, 'split')  334 us
    ppermute x4, waiting for transfers between devices, passed_along(): return lax.ppermute(block, axis, route)  19.6 us
    ppermute x4, starting transfers between devices, passed_along(): return lax.ppermute(block, axis, route)  10.6 us
  transfers between devices with their start and end apart: 8, of which 8 were waited for; matrix products, arithmetic and copies ran while one was open for 2% of the time, Pallas kernels for 0%

commit v1 on v0

v1 whole, which is shorter than its diff:
```python
import jax
import jax.numpy as jnp
from jax import lax
from jax.experimental import pallas as pl
from jax.experimental.pallas import tpu as pltpu
from jax.sharding import PartitionSpec as P

LEARN_RATE = 0.0005
CONF_SCALE = 0.5
RIDGE_COEF = 0.01
DECAY = 1.0 - LEARN_RATE * RIDGE_COEF
PARAMS = pltpu.CompilerParams(vmem_limit_bytes=8 << 20)

NT = (((1,), (1,)), ((), ()))
NN = (((1,), (0,)), ((), ()))
TN = (((0,), (0,)), ((), ()))


def halves(x):
    high = x.astype(jnp.bfloat16)
    low = (x - high.astype(jnp.float32)).astype(jnp.bfloat16)
    return high, low


def product(a, b, dims):
    def one(p, q):
        return lax.dot_general(p, q, dims, preferred_element_type=jnp.float32)

    return one(a[0], b[0]) + (one(a[0], b[1]) + one(a[1], b[0]))


def grad_kernel(user_ref, held_ref, items_ref, conf_ref, errors_ref, grad_ref):
    slab, users = errors_ref.shape
    rows = lax.broadcasted_iota(jnp.int32, (slab, users), 0)
    counts = jnp.zeros((slab, users), jnp.float32)
    for k in range(items_ref.shape[0]):
        hit = items_ref[k : k + 1, :] == rows
        counts += jnp.where(hit, conf_ref[k : k + 1, :].astype(jnp.float32), 0.0)
    user = halves(user_ref[...])
    scores = product(halves(held_ref[...]), user, NT)
    target = jnp.where(counts > 0.0, 1.0, 0.0)
    errors = (1.0 + CONF_SCALE * counts) * (scores - target)
    errors_ref[...] = errors
    grad_ref[...] = product(halves(errors), user, NN)


def gradient(user, held, items, conf):
    slab, users = held.shape[0], user.shape[0]
    return pl.pallas_call(
        grad_kernel,
        out_shape=(
            jax.ShapeDtypeStruct((slab, users), jnp.float32),
            jax.ShapeDtypeStruct(held.shape, jnp.float32),
        ),
        compiler_params=PARAMS,
        name="gradient",
    )(user, held, items, conf)


def user_kernel(user_ref, errors_ref, held_ref, out_ref):
    step = product(halves(errors_ref[...]), halves(held_ref[...]), TN)
    out_ref[...] = DECAY * user_ref[...] - LEARN_RATE * step


def update_users(user, errors, held):
    return pl.pallas_call(
        user_kernel,
        out_shape=jax.ShapeDtypeStruct(user.shape, jnp.float32),
        compiler_params=PARAMS,
        name="users",
    )(user, errors, held)


def share_kernel(parts_ref, share_ref, out_ref):
    total = parts_ref[0]
    for i in range(1, parts_ref.shape[0]):
        total += parts_ref[i]
    out_ref[...] = DECAY * share_ref[...] - LEARN_RATE * total


def update_share(parts, share):
    return pl.pallas_call(
        share_kernel,
        out_shape=jax.ShapeDtypeStruct(share.shape, jnp.float32),
        compiler_params=PARAMS,
        name="share",
    )(parts, share)


def local(user_factors, item_factors, obs_items, obs_conf):
    slab, rank = item_factors.shape
    n = lax.axis_size("split")
    blocks = lax.axis_size("blk")
    share_rows = slab // n
    back = [((b + 1) % blocks, b) for b in range(blocks)]
    user, held = user_factors, item_factors
    share = lax.dynamic_slice_in_dim(held, lax.axis_index("split") * share_rows, share_rows, 0)
    items = jnp.transpose(obs_items, (1, 2, 0))
    conf = jnp.transpose(obs_conf, (1, 2, 0))
    steps = items.shape[0]
    for step in range(steps):
        errors, grad = gradient(user, held, items[step], conf[step])
        parts = lax.all_to_all(grad.reshape(n, share_rows, rank), "split", 0, 0)
        share = lax.ppermute(update_share(parts, share), "blk", back)
        user = update_users(user, errors, held)
        if step < steps - 1:
            copies = jnp.broadcast_to(share[None], (n, share_rows, rank))
            held = lax.all_to_all(copies, "split", 0, 0).reshape(slab, rank)
    return user, share


def solution(mesh):
    in_specs = (
        P(("blk", "split"), None),
        P("blk", None),
        P(("blk", "split"), None, None),
        P(("blk", "split"), None, None),
    )
    out_specs = (P(("blk", "split"), None), P(("blk", "split"), None))
    return jax.shard_map(local, mesh=mesh, in_specs=in_specs, out_specs=out_specs, check_vma=False)
```

time: 405 us -> 119 us (0.29)
  waiting for transfers between devices: 354 us -> 23.6 us
  starting transfers between devices: 10.7 us -> 51.3 us
  blocking collectives: 0 us -> 29.6 us
  between operations: 14 us -> 0.75 us
  matrix products: 10.4 us -> 0 us
  other arithmetic: 9.78 us -> 0 us
  Pallas kernels: 0 us -> 6.58 us
    psum x4 -> x0, waiting for transfers between devices: 334 us -> none  [local(): total_grad = lax.psum(partial_grad, 'split')]
    all_to_all x0 -> x3, blocking collectives: none -> 29.6 us  [local(): parts = lax.all_to_all(grad.reshape(n, share_rows, rank), 'split', 0, 0)]
    all_to_all x0 -> x4, starting transfers between devices: none -> 26.6 us  [the longest x3 17.3 us: local(): held = lax.all_to_all(copies, 'split', 0, 0).reshape(slab, rank)]
    all_to_all x0 -> x4, waiting for transfers between devices: none -> 18.5 us  [the longest x3 13.6 us: local(): held = lax.all_to_all(copies, 'split', 0, 0).reshape(slab, rank)]
    ppermute x4, waiting for transfers between devices: 19.6 us -> 5.1 us  [local(): share = lax.ppermute(update_share(parts, share), 'blk', back)]
    ppermute x4, starting transfers between devices: 10.6 us -> 24.7 us  [local(): share = lax.ppermute(update_share(parts, share), 'blk', back)]
    dot_general x12 -> x0, matrix products: 10.4 us -> none  [the longest x4 4.64 us: block_step(): lax.dot_general(errors, user_rows, (((0,), (0,)), ((), ())), precision=la...]
    pallas_call x0 -> x12, Pallas kernels: none -> 6.58 us  [the longest x4 4.1 us: gradient(): pl.pallas_call(grad_kernel, out_shape=(jax.ShapeDtypeStruct((slab, users)...]
  transfers between devices with their start and end apart: 8 -> 8, of which waited for: 8 -> 8; matrix products, arithmetic and copies ran while one was open for 2% -> 0% of each run, Pallas kernels for 0% -> 2%
where the time goes in v1:
time: 119 us; the launch traced here: 117 us
  starting transfers between devices  51.3 us (43%)
  blocking collectives  29.6 us (25%)
  waiting for transfers between devices  23.6 us (20%)
  Pallas kernels  6.58 us (6%)
  local copies, waits for them, and re-layouts  5.62 us (5%)
    all_to_all x3, blocking collectives, local(): parts = lax.all_to_all(grad.reshape(n, share_rows, rank), 'split', 0, 0)  29.6 us
    ppermute x4, starting transfers between devices, local(): share = lax.ppermute(update_share(parts, share), 'blk', back)  24.7 us
    all_to_all x3, starting transfers between devices, local(): held = lax.all_to_all(copies, 'split', 0, 0).reshape(slab, rank)  17.3 us
    all_to_all x3, waiting for transfers between devices, local(): held = lax.all_to_all(copies, 'split', 0, 0).reshape(slab, rank)  13.6 us
    all_to_all x1, starting transfers between devices, local(): parts = lax.all_to_all(grad.reshape(n, share_rows, rank), 'split', 0, 0)  9.33 us
    ppermute x4, waiting for transfers between devices, local(): share = lax.ppermute(update_share(parts, share), 'blk', back)  5.1 us
    all_to_all x1, waiting for transfers between devices, local(): parts = lax.all_to_all(grad.reshape(n, share_rows, rank), 'split', 0, 0)  4.88 us
    pallas_call x4, Pallas kernels, gradient(): pl.pallas_call(grad_kernel, out_shape=(jax.ShapeDtypeStruct((slab, users)...  4.1 us
  transfers between devices with their start and end apart: 8, of which 8 were waited for; matrix products, arithmetic and copies ran while one was open for 0% of the time, Pallas kernels for 2%

profile of v1, /device:TPU:6, one launch (start us, length us, event | category | flops | bytes accessed | tf_op | source)
XLA Modules:
  0.0 117.4 jit_solution(14541731156232680961)
XLA Ops:
  1.5 1.0 copy-done
  2.5 0.9 copy-done.2
  3.4 1.6 %gradient.4 = (f32[128,256]{1,0:T(8,128)S(1)}, f32[128,512]{1,0:T(8,128)}) custom-call(f32[256,512]{1,0:T(8,128)S(1)} %copy-done, f32[128,512]{1,0:T(8,128)S(1)} %copy-done.2, s32[8,256]{1,0:T(8,128)S(1)} %get-tuple-element.26.items_ref, s32[8,256]{1,0:T(8,128)S(1)} %get-tuple-element.21.conf_ref), custom_call_target="tpu_custom_call" | custom-call | tf_op jit(solution)/shard_map/gradient/pallas_call | solution.py:49
  5.0 9.3 %all-to-all-start = ((f32[8,16,512]{2,1,0:T(8,128)}), f32[8,16,512]{2,1,0:T(8,128)S(1)}, u32[]{:S(2)}, u32[]{:S(2)}) async-start(f32[8,16,512]{2,1,0:T(8,128)} %bitcast.4), calls=%async_computation | async-start | bytes 524288 | tf_op jit(solution)/shard_map/all_to_all | solution.py:103
  14.4 4.9 %all-to-all-done.parts_ref = f32[8,16,512]{2,1,0:T(8,128)S(1)} async-done(((f32[8,16,512]{2,1,0:T(8,128)}), f32[8,16,512]{2,1,0:T(8,128)S(1)}, u32[]{:S(2)}, u32[]{:S(2)}) %all-to-all-start) | async-done | bytes 262176 | tf_op jit(solution)/shard_map/all_to_all | solution.py:103
  19.3 8.3 %collective-permute-start = (f32[16,512]{1,0:T(8,128)S(1)}, f32[16,512]{1,0:T(8,128)S(1)}, u32[]{:S(2)}, u32[]{:S(2)}) collective-permute-start(f32[16,512]{1,0:T(8,128)S(1)} %share.4), channel_id=1, source_target_pairs={{8,0},{16,8},{24,16},{32,24},{40,32},{48,40},{56,48},{64,56},{72,6... | collective-permute-start | bytes 98312 | tf_op jit(solution)/shard_map/ppermute | solution.py:104
  27.6 1.6 %collective-permute-done.share_ref = f32[16,512]{1,0:T(8,128)S(1)} collective-permute-done((f32[16,512]{1,0:T(8,128)S(1)}, f32[16,512]{1,0:T(8,128)S(1)}, u32[]{:S(2)}, u32[]{:S(2)}) %collective-permute-start) | collective-permute-done | bytes 32800 | tf_op jit(solution)/shard_map/ppermute | solution.py:104
  29.9 5.8 %all-to-all-start.1 = ((f32[8,16,512]{2,1,0:T(8,128)}), f32[8,16,512]{2,1,0:T(8,128)S(1)}, u32[]{:S(2)}, u32[]{:S(2)}) async-start(f32[8,16,512]{2,1,0:T(8,128)} %broadcast_in_dim.6), calls=%async_computation.1 | async-start | bytes 524288 | tf_op jit(solution)/shard_map/all_to_all | solution.py:108
  36.1 4.6 %all-to-all-done.1 = f32[8,16,512]{2,1,0:T(8,128)S(1)} async-done(((f32[8,16,512]{2,1,0:T(8,128)}), f32[8,16,512]{2,1,0:T(8,128)S(1)}, u32[]{:S(2)}, u32[]{:S(2)}) %all-to-all-start.1) | async-done | bytes 262176 | tf_op jit(solution)/shard_map/all_to_all | solution.py:108
  41.6 10.0 %all_to_all.35.parts_ref = f32[8,16,512]{2,1,0:T(8,128)S(1)} all-to-all(f32[8,16,512]{2,1,0:T(8,128)S(1)} %bitcast.31), channel_id=1, replica_groups=mesh['blk'=64,'split'=8] {'split'}, dimensions={0} | all-to-all | bytes 524288 | tf_op jit(solution)/shard_map/all_to_all | solution.py:103
  51.6 5.3 %collective-permute-start.1 = (f32[16,512]{1,0:T(8,128)S(1)}, f32[16,512]{1,0:T(8,128)S(1)}, u32[]{:S(2)}, u32[]{:S(2)}) collective-permute-start(f32[16,512]{1,0:T(8,128)S(1)} %share.5), channel_id=1, source_target_pairs={{8,0},{16,8},{24,16},{32,24},{40,32},{48,40},{56,48},{64,56},{72,6... | collective-permute-start | bytes 98312 | tf_op jit(solution)/shard_map/ppermute | solution.py:104
  56.9 1.6 %collective-permute-done.1.share_ref = f32[16,512]{1,0:T(8,128)S(1)} collective-permute-done((f32[16,512]{1,0:T(8,128)S(1)}, f32[16,512]{1,0:T(8,128)S(1)}, u32[]{:S(2)}, u32[]{:S(2)}) %collective-permute-start.1) | collective-permute-done | bytes 32800 | tf_op jit(solution)/shard_map/ppermute | solution.py:104
  59.2 5.7 %all-to-all-start.3 = ((f32[8,16,512]{2,1,0:T(8,128)}), f32[8,16,512]{2,1,0:T(8,128)S(1)}, u32[]{:S(2)}, u32[]{:S(2)}) async-start(f32[8,16,512]{2,1,0:T(8,128)} %broadcast_in_dim.7), calls=%async_computation.3 | async-start | bytes 524288 | tf_op jit(solution)/shard_map/all_to_all | solution.py:108
  65.3 4.5 %all-to-all-done.3 = f32[8,16,512]{2,1,0:T(8,128)S(1)} async-done(((f32[8,16,512]{2,1,0:T(8,128)}), f32[8,16,512]{2,1,0:T(8,128)S(1)}, u32[]{:S(2)}, u32[]{:S(2)}) %all-to-all-start.3) | async-done | bytes 262176 | tf_op jit(solution)/shard_map/all_to_all | solution.py:108
  69.8 0.8 gradient.6
  70.7 9.8 %all_to_all.36.parts_ref = f32[8,16,512]{2,1,0:T(8,128)S(1)} all-to-all(f32[8,16,512]{2,1,0:T(8,128)S(1)} %bitcast.32), channel_id=1, replica_groups=mesh['blk'=64,'split'=8] {'split'}, dimensions={0} | all-to-all | bytes 524288 | tf_op jit(solution)/shard_map/all_to_all | solution.py:103
  80.5 5.6 %collective-permute-start.2 = (f32[16,512]{1,0:T(8,128)S(1)}, f32[16,512]{1,0:T(8,128)S(1)}, u32[]{:S(2)}, u32[]{:S(2)}) collective-permute-start(f32[16,512]{1,0:T(8,128)S(1)} %share.6), channel_id=1, source_target_pairs={{8,0},{16,8},{24,16},{32,24},{40,32},{48,40},{56,48},{64,56},{72,6... | collective-permute-start | bytes 98312 | tf_op jit(solution)/shard_map/ppermute | solution.py:104
  86.1 1.6 %collective-permute-done.2.share_ref = f32[16,512]{1,0:T(8,128)S(1)} collective-permute-done((f32[16,512]{1,0:T(8,128)S(1)}, f32[16,512]{1,0:T(8,128)S(1)}, u32[]{:S(2)}, u32[]{:S(2)}) %collective-permute-start.2) | collective-permute-done | bytes 32800 | tf_op jit(solution)/shard_map/ppermute | solution.py:104
  88.4 5.7 %all-to-all-start.5 = ((f32[8,16,512]{2,1,0:T(8,128)}), f32[8,16,512]{2,1,0:T(8,128)S(1)}, u32[]{:S(2)}, u32[]{:S(2)}) async-start(f32[8,16,512]{2,1,0:T(8,128)} %broadcast_in_dim.8), calls=%async_computation.5 | async-start | bytes 524288 | tf_op jit(solution)/shard_map/all_to_all | solution.py:108
  94.5 4.5 %all-to-all-done.5 = f32[8,16,512]{2,1,0:T(8,128)S(1)} async-done(((f32[8,16,512]{2,1,0:T(8,128)}), f32[8,16,512]{2,1,0:T(8,128)S(1)}, u32[]{:S(2)}, u32[]{:S(2)}) %all-to-all-start.5) | async-done | bytes 262176 | tf_op jit(solution)/shard_map/all_to_all | solution.py:108
  99.0 0.8 gradient.7
  99.9 9.8 %all_to_all.37.parts_ref = f32[8,16,512]{2,1,0:T(8,128)S(1)} all-to-all(f32[8,16,512]{2,1,0:T(8,128)S(1)} %bitcast.33), channel_id=1, replica_groups=mesh['blk'=64,'split'=8] {'split'}, dimensions={0} | all-to-all | bytes 524288 | tf_op jit(solution)/shard_map/all_to_all | solution.py:103
  109.7 5.5 %collective-permute-start.3 = (f32[16,512]{1,0:T(8,128)S(1)}, f32[16,512]{1,0:T(8,128)S(1)}, u32[]{:S(2)}, u32[]{:S(2)}) collective-permute-start(f32[16,512]{1,0:T(8,128)S(1)} %share.7), channel_id=1, source_target_pairs={{8,0},{16,8},{24,16},{32,24},{40,32},{48,40},{56,48},{64,56},{72,6... | collective-permute-start | bytes 98312 | tf_op jit(solution)/shard_map/ppermute | solution.py:104
  115.2 1.2 %users.7 = f32[256,512]{1,0:T(8,128)} custom-call(f32[256,512]{1,0:T(8,128)S(1)} %users.6.user_ref, f32[128,256]{1,0:T(8,128)S(1)} %get-tuple-element.16.errors_ref, f32[128,512]{1,0:T(8,128)S(1)} %bitcast.30), custom_call_target="tpu_custom_call" | custom-call | tf_op jit(solution)/shard_map/users/pallas_call | solution.py:66
  (21 shorter events, 6.1 us)
Async XLA Ops:
  1.5 1.0 copy-start
  2.5 0.9 copy-start.2
  5.0 9.3 %copy-start.3 = (f32[128,512]{1,0:T(8,128)S(1)}, f32[128,512]{1,0:T(8,128)}, u32[]{:S(2)}) copy-start(f32[128,512]{1,0:T(8,128)} %held_ref.3) | copy-start | bytes 786436
  5.0 14.2 %all-to-all-start = ((f32[8,16,512]{2,1,0:T(8,128)}), f32[8,16,512]{2,1,0:T(8,128)S(1)}, u32[]{:S(2)}, u32[]{:S(2)}) async-start(f32[8,16,512]{2,1,0:T(8,128)} %bitcast.4), calls=%async_computation | async-start | bytes 524288 | tf_op jit(solution)/shard_map/all_to_all | solution.py:103
  14.3 21.4 %copy-start.1 = (f32[256,512]{1,0:T(8,128)S(1)}, f32[256,512]{1,0:T(8,128)}, u32[]{:S(2)}) copy-start(f32[256,512]{1,0:T(8,128)} %user_ref.3) | copy-start | bytes 1572868
  19.3 9.9 %collective-permute-start = (f32[16,512]{1,0:T(8,128)S(1)}, f32[16,512]{1,0:T(8,128)S(1)}, u32[]{:S(2)}, u32[]{:S(2)}) collective-permute-start(f32[16,512]{1,0:T(8,128)S(1)} %share.4), channel_id=1, source_target_pairs={{8,0},{16,8},{24,16},{32,24},{40,32},{48,40},{56,48},{64,56},{72,6... | collective-permute-start | bytes 98312 | tf_op jit(solution)/shard_map/ppermute | solution.py:104
  29.9 10.8 %all-to-all-start.1 = ((f32[8,16,512]{2,1,0:T(8,128)}), f32[8,16,512]{2,1,0:T(8,128)S(1)}, u32[]{:S(2)}, u32[]{:S(2)}) async-start(f32[8,16,512]{2,1,0:T(8,128)} %broadcast_in_dim.6), calls=%async_computation.1 | async-start | bytes 524288 | tf_op jit(solution)/shard_map/all_to_all | solution.py:108
  51.6 6.8 %collective-permute-start.1 = (f32[16,512]{1,0:T(8,128)S(1)}, f32[16,512]{1,0:T(8,128)S(1)}, u32[]{:S(2)}, u32[]{:S(2)}) collective-permute-start(f32[16,512]{1,0:T(8,128)S(1)} %share.5), channel_id=1, source_target_pairs={{8,0},{16,8},{24,16},{32,24},{40,32},{48,40},{56,48},{64,56},{72,6... | collective-permute-start | bytes 98312 | tf_op jit(solution)/shard_map/ppermute | solution.py:104
  59.2 10.6 %all-to-all-start.3 = ((f32[8,16,512]{2,1,0:T(8,128)}), f32[8,16,512]{2,1,0:T(8,128)S(1)}, u32[]{:S(2)}, u32[]{:S(2)}) async-start(f32[8,16,512]{2,1,0:T(8,128)} %broadcast_in_dim.7), calls=%async_computation.3 | async-start | bytes 524288 | tf_op jit(solution)/shard_map/all_to_all | solution.py:108
  80.5 7.2 %collective-permute-start.2 = (f32[16,512]{1,0:T(8,128)S(1)}, f32[16,512]{1,0:T(8,128)S(1)}, u32[]{:S(2)}, u32[]{:S(2)}) collective-permute-start(f32[16,512]{1,0:T(8,128)S(1)} %share.6), channel_id=1, source_target_pairs={{8,0},{16,8},{24,16},{32,24},{40,32},{48,40},{56,48},{64,56},{72,6... | collective-permute-start | bytes 98312 | tf_op jit(solution)/shard_map/ppermute | solution.py:104
  88.4 10.6 %all-to-all-start.5 = ((f32[8,16,512]{2,1,0:T(8,128)}), f32[8,16,512]{2,1,0:T(8,128)S(1)}, u32[]{:S(2)}, u32[]{:S(2)}) async-start(f32[8,16,512]{2,1,0:T(8,128)} %broadcast_in_dim.8), calls=%async_computation.5 | async-start | bytes 524288 | tf_op jit(solution)/shard_map/all_to_all | solution.py:108
  109.7 7.1 %collective-permute-start.3 = (f32[16,512]{1,0:T(8,128)S(1)}, f32[16,512]{1,0:T(8,128)S(1)}, u32[]{:S(2)}, u32[]{:S(2)}) collective-permute-start(f32[16,512]{1,0:T(8,128)S(1)} %share.7), channel_id=1, source_target_pairs={{8,0},{16,8},{24,16},{32,24},{40,32},{48,40},{56,48},{64,56},{72,6... | collective-permute-start | bytes 98312 | tf_op jit(solution)/shard_map/ppermute | solution.py:104

commit v2 on v1

v2 whole, which is shorter than its diff:
```python
import functools

import jax
import jax.numpy as jnp
from jax import lax
from jax.experimental import pallas as pl
from jax.experimental.pallas import tpu as pltpu
from jax.sharding import PartitionSpec as P

LEARN_RATE = 0.0005
CONF_SCALE = 0.5
RIDGE_COEF = 0.01
DECAY = 1.0 - LEARN_RATE * RIDGE_COEF
PARAMS = pltpu.CompilerParams(vmem_limit_bytes=16 << 20)

NT = (((1,), (1,)), ((), ()))
NN = (((1,), (0,)), ((), ()))
TN = (((0,), (0,)), ((), ()))

MATES = (1, 2, 3)
MIRROR = 6


def halves(x):
    high = x.astype(jnp.bfloat16)
    low = (x - high.astype(jnp.float32)).astype(jnp.bfloat16)
    return high, low


def product(a, b, dims):
    def one(p, q):
        return lax.dot_general(p, q, dims, preferred_element_type=jnp.float32)

    return one(a[0], b[0]) + (one(a[0], b[1]) + one(a[1], b[0]))


def errors_of(held, user, items, conf, rows):
    counts = jnp.zeros(rows.shape, jnp.float32)
    for k in range(items.shape[0]):
        counts += jnp.where(items[k : k + 1] == rows, conf[k : k + 1], 0.0)
    target = jnp.where(counts > 0.0, 1.0, 0.0)
    return (1.0 + CONF_SCALE * counts) * (product(held, user, NT) - target)


def iota_rows(slab, users):
    return lax.broadcasted_iota(jnp.int32, (slab, users), 0)


def packed(ref, users, step, obs):
    at = users + (step - 1) * obs
    items = ref[at : at + obs, :users].astype(jnp.int32)
    return items, ref[at : at + obs, users:]


def call(kernel, outs, name):
    return pl.pallas_call(
        kernel,
        out_shape=[jax.ShapeDtypeStruct(o, jnp.float32) for o in outs],
        compiler_params=PARAMS,
        name=name,
    )


def first_kernel(user_ref, held_ref, items_ref, conf_ref, errors_ref, grad_ref):
    user = halves(user_ref[...])
    rows = iota_rows(*errors_ref.shape)
    conf = conf_ref[0].astype(jnp.float32)
    errors = errors_of(halves(held_ref[...]), user, items_ref[0], conf, rows)
    errors_ref[...] = errors
    grad_ref[...] = product(halves(errors), user, NN)


def pack_kernel(user_ref, held_ref, errors_ref, items_ref, conf_ref, out_ref):
    users = user_ref.shape[0]
    steps, obs, _ = items_ref.shape
    step = product(halves(errors_ref[...]), halves(held_ref[...]), TN)
    out_ref[:users, :] = DECAY * user_ref[...] - LEARN_RATE * step
    for s in range(1, steps):
        at = users + (s - 1) * obs
        out_ref[at : at + obs, :users] = items_ref[s].astype(jnp.float32)
        out_ref[at : at + obs, users:] = conf_ref[s].astype(jnp.float32)


def share_kernel(parts_ref, held_ref, out_ref):
    share = out_ref.shape[0]
    total = parts_ref[0]
    for i in range(1, parts_ref.shape[0]):
        total += parts_ref[i]
    at = pl.multiple_of(lax.axis_index("split") * share, share)
    out_ref[...] = DECAY * held_ref[pl.ds(at, share), :] - LEARN_RATE * total


def copies_kernel(share_ref, out_ref):
    for i in range(out_ref.shape[0]):
        out_ref[i] = share_ref[...]


def slab_of(refs):
    held = refs[0][...]
    for ref in refs[1:]:
        held += ref[...]
    return held


def group_kernel(step, obs, pieces, *refs):
    n = len(MATES) + 1
    held_refs, user_refs, pack_refs = refs[:pieces], refs[pieces : pieces + n], refs[pieces + n : pieces + 2 * n]
    errors_ref, same_ref, mirror_ref = refs[pieces + 2 * n :]
    _, slab, users = errors_ref.shape
    held = slab_of(held_refs)
    held_halves = halves(held)
    rows = iota_rows(slab, users)
    total = jnp.zeros(held.shape, jnp.float32)
    for i in range(n):
        user = halves(user_refs[i][:users, :])
        items, conf = packed(pack_refs[i], users, step, obs)
        errors = errors_of(held_halves, user, items, conf, rows)
        errors_ref[i] = errors
        total += product(halves(errors), user, NN)
    mirror = -LEARN_RATE * total
    mirror_ref[...] = mirror
    same_ref[...] = DECAY * held + mirror


def group_users_kernel(pieces, *refs):
    n = len(MATES) + 1
    held_refs, errors_ref, user_refs, out_refs = refs[:pieces], refs[pieces], refs[pieces + 1 : pieces + 1 + n], refs[pieces + 1 + n :]
    held = halves(slab_of(held_refs))
    users = out_refs[0].shape[0]
    for i in range(n):
        step = product(halves(errors_ref[i]), held, TN)
        out_refs[i][...] = DECAY * user_refs[i][:users, :] - LEARN_RATE * step


def last_kernel(step, obs, same_ref, mirror_ref, *refs):
    n = len(MATES) + 1
    user_refs, pack_refs = refs[:n], refs[n : 2 * n]
    out_same_ref, out_mirror_ref = refs[2 * n :]
    share = out_same_ref.shape[0]
    users = user_refs[0].shape[0]
    place = lax.axis_index("split")
    at = [pl.multiple_of(place * share, share), pl.multiple_of((place ^ MIRROR) * share, share)]
    pieces = [same_ref[pl.ds(a, share), :] + mirror_ref[pl.ds(a, share), :] for a in at]
    held = halves(jnp.concatenate(pieces, axis=0))
    inner = iota_rows(2 * share, users)
    rows = jnp.where(inner < share, inner + at[0], inner + (at[1] - share))
    total = jnp.zeros((2 * share, same_ref.shape[1]), jnp.float32)
    for i in range(n):
        user = halves(user_refs[i][...])
        items, conf = packed(pack_refs[i], users, step, obs)
        errors = errors_of(held, user, items, conf, rows)
        total += product(halves(errors), user, NN)
    out_same_ref[...] = DECAY * pieces[0] - LEARN_RATE * total[:share]
    out_mirror_ref[...] = -LEARN_RATE * total[share:]


def sum_kernel(a_ref, b_ref, out_ref):
    out_ref[...] = a_ref[...] + b_ref[...]


def last_users_kernel(step, obs, same_ref, mirror_ref, user_ref, pack_ref, out_ref):
    users = user_ref.shape[0]
    held = halves(same_ref[...] + mirror_ref[...])
    user = user_ref[...]
    items, conf = packed(pack_ref, users, step, obs)
    errors = errors_of(held, halves(user), items, conf, iota_rows(same_ref.shape[0], users))
    out_ref[...] = DECAY * user - LEARN_RATE * product(halves(errors), held, TN)


def local(user_factors, item_factors, obs_items, obs_conf):
    slab, rank = item_factors.shape
    users = user_factors.shape[0]
    _, steps, obs = obs_items.shape
    n = lax.axis_size("split")
    blocks = lax.axis_size("blk")
    share_rows = slab // n
    back = [((b + 1) % blocks, b) for b in range(blocks)]
    back_mirror = [(((b + 1) % blocks) * n + (k ^ MIRROR), b * n + k) for b in range(blocks) for k in range(n)]
    items = jnp.transpose(obs_items, (1, 2, 0))
    conf = jnp.transpose(obs_conf, (1, 2, 0))

    def onward(same, mirror):
        return [lax.ppermute(same, "blk", back), lax.ppermute(mirror, ("blk", "split"), back_mirror)]

    errors, grad = call(first_kernel, [(slab, users), (slab, rank)], "first")(user_factors, item_factors, items, conf)
    parts = lax.all_to_all(grad.reshape(n, share_rows, rank), "split", 0, 0)
    rows = users + (steps - 1) * obs
    (own,) = call(pack_kernel, [(rows, rank)], "pack")(user_factors, item_factors, errors, items, conf)
    packs = [own] + [lax.ppermute(own, "split", [(k, k ^ m) for k in range(n)]) for m in MATES]
    (share,) = call(share_kernel, [(share_rows, rank)], "share")(parts, item_factors)
    share = lax.ppermute(share, "blk", back)
    (copies,) = call(copies_kernel, [(n, share_rows, rank)], "copies")(share)
    held = [lax.all_to_all(copies, "split", 0, 0).reshape(slab, rank)]

    user = packs
    for step in range(1, steps - 1):
        kernel = functools.partial(group_kernel, step, obs, len(held))
        outs = [(len(packs), slab, users), (slab, rank), (slab, rank)]
        errors, same, mirror = call(kernel, outs, "group")(*held, *user, *packs)
        sent = onward(same, mirror)
        kernel = functools.partial(group_users_kernel, len(held))
        user = call(kernel, [(users, rank)] * len(packs), "group_users")(*held, errors, *user)
        held = sent
    kernel = functools.partial(last_kernel, steps - 1, obs)
    same, mirror = call(kernel, [(share_rows, rank)] * 2, "last")(*held, *user, *packs)
    same, mirror = onward(same, mirror)
    kernel = functools.partial(last_users_kernel, steps - 1, obs)
    (user_out,) = call(kernel, [(users, rank)], "last_users")(*held, user[0], packs[0])
    (share_out,) = call(sum_kernel, [(share_rows, rank)], "total")(same, mirror)
    return user_out, share_out


def solution(mesh):
    in_specs = (
        P(("blk", "split"), None),
        P("blk", None),
        P(("blk", "split"), None, None),
        P(("blk", "split"), None, None),
    )
    out_specs = (P(("blk", "split"), None), P(("blk", "split"), None))
    return jax.shard_map(local, mesh=mesh, in_specs=in_specs, out_specs=out_specs, check_vma=False)
```

time: 119 us -> 120 us (level)
  blocking collectives: 29.6 us -> 0 us
  starting transfers between devices: 51.3 us -> 78.5 us
  Pallas kernels: 6.58 us -> 13.7 us
  waiting for transfers between devices: 23.6 us -> 21.5 us
  local copies, waits for them, and re-layouts: 5.62 us -> 3.52 us
    ppermute x4 -> x10, starting transfers between devices: 24.7 us -> 57.5 us  [the longest x3 23.9 us: onward(): lax.ppermute(same, 'blk', back)]
    all_to_all x3 -> x0, blocking collectives: 29.6 us -> none  [local(): parts = lax.all_to_all(grad.reshape(n, share_rows, rank), 'split', 0, 0)]
    ppermute x4 -> x10, waiting for transfers between devices: 5.1 us -> 15.8 us  [the longest x3 10.5 us: onward(): lax.ppermute(mirror, ('blk', 'split'), back_mirror)]
    all_to_all x3 -> x1, waiting for transfers between devices: 13.6 us -> 5.64 us  [local(): held = [lax.all_to_all(copies, 'split', 0, 0).reshape(slab, rank)]]
    pallas_call x12 -> x11, Pallas kernels: 6.58 us -> 13.7 us  [the longest x2 4.44 us: local(): errors, same, mirror = call(kernel, outs, 'group')(*held, *user, *packs)]
    all_to_all x3 -> x1, starting transfers between devices: 17.3 us -> 11.6 us  [local(): held = [lax.all_to_all(copies, 'split', 0, 0).reshape(slab, rank)]]
    all_to_all x1, waiting for transfers between devices: 4.88 us -> 0.01 us  [local(): parts = lax.all_to_all(grad.reshape(n, share_rows, rank), 'split', 0, 0)]
    broadcast_in_dim x3 -> x0, local copies, waits for them, and re-layouts: 2.18 us -> none  [local(): copies = jnp.broadcast_to(share[None], (n, share_rows, rank))]
  transfers between devices with their start and end apart: 8 -> 12, of which waited for: 8 -> 6; matrix products, arithmetic and copies ran while one was open for 0% -> 0% of each run, Pallas kernels for 2% -> 4%
where the time goes in v2:
time: 120 us; the launch traced here: 118 us
  starting transfers between devices  78.5 us (65%)
  waiting for transfers between devices  21.5 us (18%)
  Pallas kernels  13.7 us (11%)
  local copies, waits for them, and re-layouts  3.52 us (3%)
    ppermute x3, starting transfers between devices, onward(): lax.ppermute(same, 'blk', back)  23.9 us
    ppermute x3, starting transfers between devices, onward(): lax.ppermute(mirror, ('blk', 'split'), back_mirror)  16.1 us
    all_to_all x1, starting transfers between devices, local(): held = [lax.all_to_all(copies, 'split', 0, 0).reshape(slab, rank)]  11.6 us
    ppermute x3, waiting for transfers between devices, onward(): lax.ppermute(mirror, ('blk', 'split'), back_mirror)  10.5 us
    all_to_all x1, starting transfers between devices, local(): parts = lax.all_to_all(grad.reshape(n, share_rows, rank), 'split', 0, 0)  9.33 us
    ppermute x3, starting transfers between devices, local(): lax.ppermute(own, 'split', [(k, k ^ m) for k in range(n)])  9.21 us
    ppermute x1, starting transfers between devices, local(): share = lax.ppermute(share, 'blk', back)  8.37 us
    all_to_all x1, waiting for transfers between devices, local(): held = [lax.all_to_all(copies, 'split', 0, 0).reshape(slab, rank)]  5.64 us
  transfers between devices with their start and end apart: 12, of which 6 were waited for; matrix products, arithmetic and copies ran while one was open for 0% of the time, Pallas kernels for 4%

profile of v2, /device:TPU:6, one launch (start us, length us, event | category | flops | bytes accessed | tf_op | source)
XLA Modules:
  0.0 118.0 jit_solution(2091830793710733209)
XLA Ops:
  1.6 1.0 copy-done.2
  4.1 1.6 %first.1 = (f32[128,256]{1,0:T(8,128)S(1)}, f32[128,512]{1,0:T(8,128)}) custom-call(f32[256,512]{1,0:T(8,128)S(1)} %copy-done.2, f32[128,512]{1,0:T(8,128)S(1)} %copy-done, s32[4,8,256]{2,1,0:T(8,128)S(1)} %bitcast.6, s32[4,8,256]{2,1,0:T(8,128)S(1)} %bitcast.8), custom_call_target="tpu_custom_call" | custom-call | tf_op jit(solution)/shard_map/first/pallas_call | solution.py:185
  5.7 9.3 %all-to-all-start = ((f32[8,16,512]{2,1,0:T(8,128)}), f32[8,16,512]{2,1,0:T(8,128)S(1)}, u32[]{:S(2)}, u32[]{:S(2)}) async-start(f32[8,16,512]{2,1,0:T(8,128)} %bitcast.2), calls=%async_computation | async-start | bytes 524288 | tf_op jit(solution)/shard_map/all_to_all | solution.py:186
  15.5 3.4 %collective-permute-start.1 = (f32[280,512]{1,0:T(8,128)S(1)}, f32[280,512]{1,0:T(8,128)S(1)}, u32[]{:S(2)}, u32[]{:S(2)}) collective-permute-start(f32[280,512]{1,0:T(8,128)S(1)} %pack.1.refs_1_.refs_5_.refs_2_.refs_6_.pack_ref.refs_4_), channel_id=1, source_target_pairs={{0,1},{1,0},{2,3},{3,2},{4,5},{5,4},{6,7},{7,6},{8,9},{9,8},{10,11... | collective-permute-start | bytes 1720328 | tf_op jit(solution)/shard_map/ppermute | solution.py:189
  18.9 2.8 %collective-permute-start.2 = (f32[280,512]{1,0:T(8,128)S(1)}, f32[280,512]{1,0:T(8,128)S(1)}, u32[]{:S(2)}, u32[]{:S(2)}) collective-permute-start(f32[280,512]{1,0:T(8,128)S(1)} %pack.1.refs_1_.refs_5_.refs_2_.refs_6_.pack_ref.refs_4_), channel_id=1, source_target_pairs={{0,2},{1,3},{2,0},{3,1},{4,6},{5,7},{6,4},{7,5},{8,10},{9,11},{10,... | collective-permute-start | bytes 1720328 | tf_op jit(solution)/shard_map/ppermute | solution.py:189
  21.6 3.1 %collective-permute-start.3 = (f32[280,512]{1,0:T(8,128)S(1)}, f32[280,512]{1,0:T(8,128)S(1)}, u32[]{:S(2)}, u32[]{:S(2)}) collective-permute-start(f32[280,512]{1,0:T(8,128)S(1)} %pack.1.refs_1_.refs_5_.refs_2_.refs_6_.pack_ref.refs_4_), channel_id=1, source_target_pairs={{0,3},{1,2},{2,1},{3,0},{4,7},{5,6},{6,5},{7,4},{8,11},{9,10},{10,... | collective-permute-start | bytes 1720328 | tf_op jit(solution)/shard_map/ppermute | solution.py:189
  24.8 8.4 %collective-permute-start = (f32[16,512]{1,0:T(8,128)S(1)}, f32[16,512]{1,0:T(8,128)S(1)}, u32[]{:S(2)}, u32[]{:S(2)}) collective-permute-start(f32[16,512]{1,0:T(8,128)S(1)} %share.1), channel_id=1, source_target_pairs={{8,0},{16,8},{24,16},{32,24},{40,32},{48,40},{56,48},{64,56},{72,6... | collective-permute-start | bytes 98312 | tf_op jit(solution)/shard_map/ppermute | solution.py:191
  33.1 1.6 %collective-permute-done.share_ref = f32[16,512]{1,0:T(8,128)S(1)} collective-permute-done((f32[16,512]{1,0:T(8,128)S(1)}, f32[16,512]{1,0:T(8,128)S(1)}, u32[]{:S(2)}, u32[]{:S(2)}) %collective-permute-start) | collective-permute-done | bytes 32800 | tf_op jit(solution)/shard_map/ppermute | solution.py:191
  35.4 11.6 %all-to-all-start.1 = ((f32[8,16,512]{2,1,0:T(8,128)}), f32[8,16,512]{2,1,0:T(8,128)S(1)}, u32[]{:S(2)}, u32[]{:S(2)}) async-start(f32[8,16,512]{2,1,0:T(8,128)} %copies.1), calls=%async_computation.1 | async-start | bytes 524288 | tf_op jit(solution)/shard_map/all_to_all | solution.py:193
  47.1 5.6 %all-to-all-done.1 = f32[8,16,512]{2,1,0:T(8,128)S(1)} async-done(((f32[8,16,512]{2,1,0:T(8,128)}), f32[8,16,512]{2,1,0:T(8,128)S(1)}, u32[]{:S(2)}, u32[]{:S(2)}) %all-to-all-start.1) | async-done | bytes 262176 | tf_op jit(solution)/shard_map/all_to_all | solution.py:193
  52.7 2.2 %group.2 = (f32[4,128,256]{2,1,0:T(8,128)S(1)}, f32[128,512]{1,0:T(8,128)S(1)}, f32[128,512]{1,0:T(8,128)S(1)}) custom-call(f32[128,512]{1,0:T(8,128)S(1)} %bitcast.4, f32[280,512]{1,0:T(8,128)S(1)} %pack.1.refs_1_.refs_5_.refs_2_.refs_6_.pack_ref.refs_4_, f32[280,512]{1,0:T(8,128)S(1)} %collective-permute-done.1.refs_2_.refs_6_.refs_3_.refs_7_.refs_5_, ...), custom_call_target="tpu_custom_call" | custom-call | tf_op jit(solution)/shard_map/group/pallas_call | solution.py:199
  55.0 5.8 %collective-permute-start.4 = (f32[128,512]{1,0:T(8,128)S(1)}, f32[128,512]{1,0:T(8,128)S(1)}, u32[]{:S(2)}, u32[]{:S(2)}) collective-permute-start(f32[128,512]{1,0:T(8,128)S(1)} %get-tuple-element.22), channel_id=1, source_target_pairs={{8,0},{16,8},{24,16},{32,24},{40,32},{48,40},{56,48},{64,56},{72,6... | collective-permute-start | bytes 786440 | tf_op jit(solution)/shard_map/ppermute | solution.py:183
  60.8 10.0 %collective-permute-start.5 = (f32[128,512]{1,0:T(8,128)S(1)}, f32[128,512]{1,0:T(8,128)S(1)}, u32[]{:S(2)}, u32[]{:S(2)}) collective-permute-start(f32[128,512]{1,0:T(8,128)S(1)} %get-tuple-element.23), channel_id=1, source_target_pairs={{14,0},{15,1},{12,2},{13,3},{10,4},{11,5},{8,6},{9,7},{22,8},{23,9... | collective-permute-start | bytes 786440 | tf_op jit(solution)/shard_map/ppermute | solution.py:183
  71.8 5.6 %collective-permute-done.5.refs_1_ = f32[128,512]{1,0:T(8,128)S(1)} collective-permute-done((f32[128,512]{1,0:T(8,128)S(1)}, f32[128,512]{1,0:T(8,128)S(1)}, u32[]{:S(2)}, u32[]{:S(2)}) %collective-permute-start.5) | collective-permute-done | bytes 262176 | tf_op jit(solution)/shard_map/ppermute | solution.py:183
  77.5 2.2 %group.3 = (f32[4,128,256]{2,1,0:T(8,128)S(1)}, f32[128,512]{1,0:T(8,128)S(1)}, f32[128,512]{1,0:T(8,128)S(1)}) custom-call(f32[128,512]{1,0:T(8,128)S(1)} %collective-permute-done.4.refs_0_, f32[128,512]{1,0:T(8,128)S(1)} %collective-permute-done.5.refs_1_, f32[256,512]{1,0:T(8,128)S(1)} %get-tuple-element.25.refs_2_.refs_3_, ...), custom_call_target="tpu_custom_call" | custom-call | tf_op jit(solution)/shard_map/group/pallas_call | solution.py:199
  79.7 8.3 %collective-permute-start.6 = (f32[128,512]{1,0:T(8,128)S(1)}, f32[128,512]{1,0:T(8,128)S(1)}, u32[]{:S(2)}, u32[]{:S(2)}) collective-permute-start(f32[128,512]{1,0:T(8,128)S(1)} %get-tuple-element.29), channel_id=1, source_target_pairs={{8,0},{16,8},{24,16},{32,24},{40,32},{48,40},{56,48},{64,56},{72,6... | collective-permute-start | bytes 786440 | tf_op jit(solution)/shard_map/ppermute | solution.py:183
  88.0 3.7 %collective-permute-start.7 = (f32[128,512]{1,0:T(8,128)S(1)}, f32[128,512]{1,0:T(8,128)S(1)}, u32[]{:S(2)}, u32[]{:S(2)}) collective-permute-start(f32[128,512]{1,0:T(8,128)S(1)} %get-tuple-element.30), channel_id=1, source_target_pairs={{14,0},{15,1},{12,2},{13,3},{10,4},{11,5},{8,6},{9,7},{22,8},{23,9... | collective-permute-start | bytes 786440 | tf_op jit(solution)/shard_map/ppermute | solution.py:183
  92.8 3.7 %collective-permute-done.6.same_ref = f32[128,512]{1,0:T(8,128)S(1)} collective-permute-done((f32[128,512]{1,0:T(8,128)S(1)}, f32[128,512]{1,0:T(8,128)S(1)}, u32[]{:S(2)}, u32[]{:S(2)}) %collective-permute-start.6) | collective-permute-done | bytes 262176 | tf_op jit(solution)/shard_map/ppermute | solution.py:183
  96.5 2.8 %collective-permute-done.7.mirror_ref = f32[128,512]{1,0:T(8,128)S(1)} collective-permute-done((f32[128,512]{1,0:T(8,128)S(1)}, f32[128,512]{1,0:T(8,128)S(1)}, u32[]{:S(2)}, u32[]{:S(2)}) %collective-permute-start.7) | collective-permute-done | bytes 262176 | tf_op jit(solution)/shard_map/ppermute | solution.py:183
  99.3 1.9 %last.1 = (f32[16,512]{1,0:T(8,128)S(1)}, f32[16,512]{1,0:T(8,128)S(1)}) custom-call(f32[128,512]{1,0:T(8,128)S(1)} %collective-permute-done.6.same_ref, f32[128,512]{1,0:T(8,128)S(1)} %collective-permute-done.7.mirror_ref, f32[256,512]{1,0:T(8,128)S(1)} %get-tuple-element.32.user_ref.refs_0_, f32[256,512]{1,0:T(8,128)S(1)} %get-tuple-element.33.refs_1_, ...), custom_call_target="tpu_custom_call" | custom-call | tf_op jit(solution)/shard_map/last/pallas_call | solution.py:205
  101.2 9.7 %collective-permute-start.8 = (f32[16,512]{1,0:T(8,128)S(1)}, f32[16,512]{1,0:T(8,128)S(1)}, u32[]{:S(2)}, u32[]{:S(2)}) collective-permute-start(f32[16,512]{1,0:T(8,128)S(1)} %get-tuple-element.36), channel_id=1, source_target_pairs={{8,0},{16,8},{24,16},{32,24},{40,32},{48,40},{56,48},{64,56},{72,6... | collective-permute-start | bytes 98312 | tf_op jit(solution)/shard_map/ppermute | solution.py:183
  110.9 2.3 %collective-permute-start.9 = (f32[16,512]{1,0:T(8,128)S(1)}, f32[16,512]{1,0:T(8,128)S(1)}, u32[]{:S(2)}, u32[]{:S(2)}) collective-permute-start(f32[16,512]{1,0:T(8,128)S(1)} %get-tuple-element.37), channel_id=1, source_target_pairs={{14,0},{15,1},{12,2},{13,3},{10,4},{11,5},{8,6},{9,7},{22,8},{23,9... | collective-permute-start | bytes 98312 | tf_op jit(solution)/shard_map/ppermute | solution.py:183
  113.3 2.0 %last_users.1 = f32[256,512]{1,0:T(8,128)} custom-call(f32[128,512]{1,0:T(8,128)S(1)} %collective-permute-done.6.same_ref, f32[128,512]{1,0:T(8,128)S(1)} %collective-permute-done.7.mirror_ref, f32[256,512]{1,0:T(8,128)S(1)} %get-tuple-element.32.user_ref.refs_0_, f32[280,512]{1,0:T(8,128)S(1)} %pack.1.refs_1_.refs_5_.refs_2_.refs_6_.pack_ref.refs_4_), custom_call_target="tpu_custom_call" | custom-call | tf_op jit(solution)/shard_map/last_users/pallas_call | solution.py:208
  115.2 2.1 %collective-permute-done.9.b_ref = f32[16,512]{1,0:T(8,128)S(1)} collective-permute-done((f32[16,512]{1,0:T(8,128)S(1)}, f32[16,512]{1,0:T(8,128)S(1)}, u32[]{:S(2)}, u32[]{:S(2)}) %collective-permute-start.9) | collective-permute-done | bytes 32800 | tf_op jit(solution)/shard_map/ppermute | solution.py:183
  (27 shorter events, 6.3 us)
Async XLA Ops:
  0.6 1.0 copy-start
  1.6 1.0 copy-start.2
  2.6 0.8 copy-start.4
  3.4 0.8 copy-start.6
  4.1 10.9 %copy-start.3 = (f32[256,512]{1,0:T(8,128)S(1)}, f32[256,512]{1,0:T(8,128)}, u32[]{:S(2)}) copy-start(f32[256,512]{1,0:T(8,128)} %user_ref.3) | copy-start | bytes 1572868
  5.7 9.3 %copy-start.1 = (f32[128,512]{1,0:T(8,128)S(1)}, f32[128,512]{1,0:T(8,128)}, u32[]{:S(2)}) copy-start(f32[128,512]{1,0:T(8,128)} %held_ref.5) | copy-start | bytes 786436
  5.7 9.3 %copy-start.5 = (s32[256,4,8]{0,2,1:T(8,128)S(1)}, s32[256,4,8]{0,2,1:T(8,128)}, u32[]{:S(2)}) copy-start(s32[256,4,8]{0,2,1:T(8,128)} %param.6) | copy-start | bytes 98308
  5.7 9.4 %copy-start.7 = (s32[256,4,8]{0,2,1:T(8,128)S(1)}, s32[256,4,8]{0,2,1:T(8,128)}, u32[]{:S(2)}) copy-start(s32[256,4,8]{0,2,1:T(8,128)} %param.7) | copy-start | bytes 98308
  5.7 19.0 %all-to-all-start = ((f32[8,16,512]{2,1,0:T(8,128)}), f32[8,16,512]{2,1,0:T(8,128)S(1)}, u32[]{:S(2)}, u32[]{:S(2)}) async-start(f32[8,16,512]{2,1,0:T(8,128)} %bitcast.2), calls=%async_computation | async-start | bytes 524288 | tf_op jit(solution)/shard_map/all_to_all | solution.py:186
  15.5 31.6 %collective-permute-start.1 = (f32[280,512]{1,0:T(8,128)S(1)}, f32[280,512]{1,0:T(8,128)S(1)}, u32[]{:S(2)}, u32[]{:S(2)}) collective-permute-start(f32[280,512]{1,0:T(8,128)S(1)} %pack.1.refs_1_.refs_5_.refs_2_.refs_6_.pack_ref.refs_4_), channel_id=1, source_target_pairs={{0,1},{1,0},{2,3},{3,2},{4,5},{5,4},{6,7},{7,6},{8,9},{9,8},{10,11... | collective-permute-start | bytes 1720328 | tf_op jit(solution)/shard_map/ppermute | solution.py:189
  18.9 28.2 %collective-permute-start.2 = (f32[280,512]{1,0:T(8,128)S(1)}, f32[280,512]{1,0:T(8,128)S(1)}, u32[]{:S(2)}, u32[]{:S(2)}) collective-permute-start(f32[280,512]{1,0:T(8,128)S(1)} %pack.1.refs_1_.refs_5_.refs_2_.refs_6_.pack_ref.refs_4_), channel_id=1, source_target_pairs={{0,2},{1,3},{2,0},{3,1},{4,6},{5,7},{6,4},{7,5},{8,10},{9,11},{10,... | collective-permute-start | bytes 1720328 | tf_op jit(solution)/shard_map/ppermute | solution.py:189
  21.6 25.5 %collective-permute-start.3 = (f32[280,512]{1,0:T(8,128)S(1)}, f32[280,512]{1,0:T(8,128)S(1)}, u32[]{:S(2)}, u32[]{:S(2)}) collective-permute-start(f32[280,512]{1,0:T(8,128)S(1)} %pack.1.refs_1_.refs_5_.refs_2_.refs_6_.pack_ref.refs_4_), channel_id=1, source_target_pairs={{0,3},{1,2},{2,1},{3,0},{4,7},{5,6},{6,5},{7,4},{8,11},{9,10},{10,... | collective-permute-start | bytes 1720328 | tf_op jit(solution)/shard_map/ppermute | solution.py:189
  24.8 9.9 %collective-permute-start = (f32[16,512]{1,0:T(8,128)S(1)}, f32[16,512]{1,0:T(8,128)S(1)}, u32[]{:S(2)}, u32[]{:S(2)}) collective-permute-start(f32[16,512]{1,0:T(8,128)S(1)} %share.1), channel_id=1, source_target_pairs={{8,0},{16,8},{24,16},{32,24},{40,32},{48,40},{56,48},{64,56},{72,6... | collective-permute-start | bytes 98312 | tf_op jit(solution)/shard_map/ppermute | solution.py:191
  35.4 17.3 %all-to-all-start.1 = ((f32[8,16,512]{2,1,0:T(8,128)}), f32[8,16,512]{2,1,0:T(8,128)S(1)}, u32[]{:S(2)}, u32[]{:S(2)}) async-start(f32[8,16,512]{2,1,0:T(8,128)} %copies.1), calls=%async_computation.1 | async-start | bytes 524288 | tf_op jit(solution)/shard_map/all_to_all | solution.py:193
  55.0 16.9 %collective-permute-start.4 = (f32[128,512]{1,0:T(8,128)S(1)}, f32[128,512]{1,0:T(8,128)S(1)}, u32[]{:S(2)}, u32[]{:S(2)}) collective-permute-start(f32[128,512]{1,0:T(8,128)S(1)} %get-tuple-element.22), channel_id=1, source_target_pairs={{8,0},{16,8},{24,16},{32,24},{40,32},{48,40},{56,48},{64,56},{72,6... | collective-permute-start | bytes 786440 | tf_op jit(solution)/shard_map/ppermute | solution.py:183
  60.8 16.7 %collective-permute-start.5 = (f32[128,512]{1,0:T(8,128)S(1)}, f32[128,512]{1,0:T(8,128)S(1)}, u32[]{:S(2)}, u32[]{:S(2)}) collective-permute-start(f32[128,512]{1,0:T(8,128)S(1)} %get-tuple-element.23), channel_id=1, source_target_pairs={{14,0},{15,1},{12,2},{13,3},{10,4},{11,5},{8,6},{9,7},{22,8},{23,9... | collective-permute-start | bytes 786440 | tf_op jit(solution)/shard_map/ppermute | solution.py:183
  79.7 16.8 %collective-permute-start.6 = (f32[128,512]{1,0:T(8,128)S(1)}, f32[128,512]{1,0:T(8,128)S(1)}, u32[]{:S(2)}, u32[]{:S(2)}) collective-permute-start(f32[128,512]{1,0:T(8,128)S(1)} %get-tuple-element.29), channel_id=1, source_target_pairs={{8,0},{16,8},{24,16},{32,24},{40,32},{48,40},{56,48},{64,56},{72,6... | collective-permute-start | bytes 786440 | tf_op jit(solution)/shard_map/ppermute | solution.py:183
  88.0 11.2 %collective-permute-start.7 = (f32[128,512]{1,0:T(8,128)S(1)}, f32[128,512]{1,0:T(8,128)S(1)}, u32[]{:S(2)}, u32[]{:S(2)}) collective-permute-start(f32[128,512]{1,0:T(8,128)S(1)} %get-tuple-element.30), channel_id=1, source_target_pairs={{14,0},{15,1},{12,2},{13,3},{10,4},{11,5},{8,6},{9,7},{22,8},{23,9... | collective-permute-start | bytes 786440 | tf_op jit(solution)/shard_map/ppermute | solution.py:183
  101.2 14.0 %collective-permute-start.8 = (f32[16,512]{1,0:T(8,128)S(1)}, f32[16,512]{1,0:T(8,128)S(1)}, u32[]{:S(2)}, u32[]{:S(2)}) collective-permute-start(f32[16,512]{1,0:T(8,128)S(1)} %get-tuple-element.36), channel_id=1, source_target_pairs={{8,0},{16,8},{24,16},{32,24},{40,32},{48,40},{56,48},{64,56},{72,6... | collective-permute-start | bytes 98312 | tf_op jit(solution)/shard_map/ppermute | solution.py:183
  110.9 6.4 %collective-permute-start.9 = (f32[16,512]{1,0:T(8,128)S(1)}, f32[16,512]{1,0:T(8,128)S(1)}, u32[]{:S(2)}, u32[]{:S(2)}) collective-permute-start(f32[16,512]{1,0:T(8,128)S(1)} %get-tuple-element.37), channel_id=1, source_target_pairs={{14,0},{15,1},{12,2},{13,3},{10,4},{11,5},{8,6},{9,7},{22,8},{23,9... | collective-permute-start | bytes 98312 | tf_op jit(solution)/shard_map/ppermute | solution.py:183

commit v3 on v1

v3 whole, which is shorter than its diff:
```python
import functools

import jax
import jax.numpy as jnp
from jax import lax
from jax.experimental import pallas as pl
from jax.experimental.pallas import tpu as pltpu
from jax.sharding import PartitionSpec as P

LEARN_RATE = 0.0005
CONF_SCALE = 0.5
RIDGE_COEF = 0.01
DECAY = 1.0 - LEARN_RATE * RIDGE_COEF
PARAMS = pltpu.CompilerParams(vmem_limit_bytes=16 << 20)

NT = (((1,), (1,)), ((), ()))
NN = (((1,), (0,)), ((), ()))
TN = (((0,), (0,)), ((), ()))

FIRST, SECOND = 2, 7
HELPERS = ((0, 5), (4, 1), (3, 6))


def halves(x):
    high = x.astype(jnp.bfloat16)
    low = (x - high.astype(jnp.float32)).astype(jnp.bfloat16)
    return high, low


def product(a, b, dims):
    def one(p, q):
        return lax.dot_general(p, q, dims, preferred_element_type=jnp.float32)

    return one(a[0], b[0]) + (one(a[0], b[1]) + one(a[1], b[0]))


def errors_of(held, user, items, conf):
    rows = lax.broadcasted_iota(jnp.int32, (held[0].shape[0], user[0].shape[0]), 0)
    counts = jnp.zeros(rows.shape, jnp.float32)
    for k in range(items.shape[0]):
        counts += jnp.where(items[k : k + 1] == rows, conf[k : k + 1], 0.0)
    target = jnp.where(counts > 0.0, 1.0, 0.0)
    return (1.0 + CONF_SCALE * counts) * (product(held, user, NT) - target)


def packed(ref, users, step, obs):
    at = users + step * obs
    return ref[at : at + obs, :users].astype(jnp.int32), ref[at : at + obs, users:]


def parity():
    return lax.axis_index("blk") & 1


def slab_of(refs):
    held = refs[0][...]
    for ref in refs[1:]:
        held += ref[...]
    return held


def call(kernel, outs, name, params=PARAMS, **kwargs):
    return pl.pallas_call(
        kernel,
        out_shape=[jax.ShapeDtypeStruct(o, jnp.float32) for o in outs],
        compiler_params=params,
        name=name,
        **kwargs,
    )


def pack_kernel(user_ref, held_ref, items_ref, conf_ref, out_ref, slab_ref, items, conf, sems):
    users = user_ref.shape[0]
    steps, obs, _ = items_ref.shape
    copies = [
        pltpu.make_async_copy(items_ref, items, sems.at[0]),
        pltpu.make_async_copy(conf_ref, conf, sems.at[1]),
        pltpu.make_async_copy(user_ref, out_ref.at[pl.ds(0, users), :], sems.at[2]),
        pltpu.make_async_copy(held_ref, slab_ref, sems.at[3]),
    ]
    for copy in copies:
        copy.start()
    copies[0].wait()
    copies[1].wait()
    for s in range(steps):
        at = users + s * obs
        out_ref[at : at + obs, :users] = items[s].astype(jnp.float32)
        out_ref[at : at + obs, users:] = conf[s].astype(jnp.float32)
    copies[2].wait()
    copies[3].wait()


def group_kernel(step, obs, pieces, chunks, *refs):
    held_refs, refs = refs[:pieces], refs[pieces:]
    user_refs, pack_refs, (errors_ref, out_ref) = refs[:chunks], refs[chunks : 2 * chunks], refs[2 * chunks :]
    _, slab, users = errors_ref.shape
    held = slab_of(held_refs)
    held_halves = halves(held)
    total = jnp.zeros(held.shape, jnp.float32)
    for i in range(chunks):
        user = halves(user_refs[i][:users, :])
        errors = errors_of(held_halves, user, *packed(pack_refs[i], users, step, obs))
        errors_ref[i] = errors
        total += product(halves(errors), user, NN)
    keep = jnp.where((lax.axis_index("split") ^ parity()) == FIRST, DECAY, 0.0)
    out_ref[...] = keep * held - LEARN_RATE * total


def users_kernel(pieces, chunks, *refs):
    held_refs, errors_ref, refs = refs[:pieces], refs[pieces], refs[pieces + 1 :]
    user_refs, out_refs = refs[:chunks], refs[chunks:]
    held = halves(slab_of(held_refs))
    users = out_refs[0].shape[0]
    for i in range(chunks):
        step = product(halves(errors_ref[i]), held, TN)
        out_refs[i][...] = DECAY * user_refs[i][:users, :] - LEARN_RATE * step


def share_kernel(parts_ref, out_ref):
    out_ref[...] = parts_ref[FIRST ^ parity()] + parts_ref[SECOND ^ parity()]


def home_kernel(share_ref, own_ref, a_ref, b_ref, c_ref, out_ref, share_out_ref):
    share_out_ref[...] = share_ref[...]
    place = lax.axis_index("split") ^ parity()
    works = (place == FIRST) | (place == SECOND)

    @pl.when(works)
    def _():
        out_ref[...] = own_ref[...]

    @pl.when(jnp.logical_not(works))
    def _():
        out_ref[...] = a_ref[...] + b_ref[...] + c_ref[...]


def local(user_factors, item_factors, obs_items, obs_conf):
    slab, rank = item_factors.shape
    users = user_factors.shape[0]
    _, steps, obs = obs_items.shape
    n = lax.axis_size("split")
    blocks = lax.axis_size("blk")
    share_rows = slab // n
    chunks = 1 + len(HELPERS)
    items = jnp.transpose(obs_items, (1, 2, 0))
    conf = jnp.transpose(obs_conf, (1, 2, 0))
    both = ("blk", "split")

    def at(b, k):
        return b * n + (k ^ (b & 1))

    def fetch(x, helpers):
        pairs = [(at(b, h), at(b, w)) for b in range(blocks) for h, w in zip(helpers, (FIRST, SECOND))]
        return lax.ppermute(x, both, pairs)

    def give(x, helpers):
        pairs = [(at(b, w), at(b, h)) for b in range(blocks) for h, w in zip(helpers, (FIRST, SECOND))]
        return lax.ppermute(x, both, pairs)

    def onward(x):
        same, cross = [], []
        for b in range(blocks):
            for w, v in ((FIRST, SECOND), (SECOND, FIRST)):
                source = at((b + 1) % blocks, w)
                same.append((source, at(b, w)))
                cross.append((source, at(b, v)))
        return [lax.ppermute(x, both, same), lax.ppermute(x, both, cross)]

    hbm = pl.BlockSpec(memory_space=pltpu.HBM)
    own, held = call(
        pack_kernel,
        [(users + steps * obs, rank), (slab, rank)],
        "pack",
        params=None,
        in_specs=[hbm] * 4,
        scratch_shapes=[pltpu.VMEM(items.shape, jnp.int32)] * 2 + [pltpu.SemaphoreType.DMA((4,))],
    )(user_factors, item_factors, items, conf)
    packs = [own] + [fetch(own, helpers) for helpers in HELPERS]
    user, held = packs, [held]
    for step in range(steps):
        kernel = functools.partial(group_kernel, step, obs, len(held), chunks)
        errors, out = call(kernel, [(chunks, slab, users), (slab, rank)], "group")(*held, *user, *packs)
        if step < steps - 1:
            sent = onward(out)
        else:
            parts = lax.all_to_all(out.reshape(n, share_rows, rank), "split", 0, 0)
        kernel = functools.partial(users_kernel, len(held), chunks)
        user = call(kernel, [(users, rank)] * chunks, "users")(*held, errors, *user)
        held = sent
    early = pl.CostEstimate(flops=1 << 36, bytes_accessed=1 << 20, transcendentals=0)
    (share,) = call(share_kernel, [(share_rows, rank)], "share", cost_estimate=early)(parts)
    share = lax.ppermute(share, "blk", [((b + 1) % blocks, b) for b in range(blocks)])
    home = [give(u, helpers) for u, helpers in zip(user[1:], HELPERS)]
    outs = [(users, rank), (share_rows, rank)]
    user_out, share_out = call(home_kernel, outs, "home")(share, user[0], *home)
    return user_out, share_out


def solution(mesh):
    in_specs = (
        P(("blk", "split"), None),
        P("blk", None),
        P(("blk", "split"), None, None),
        P(("blk", "split"), None, None),
    )
    out_specs = (P(("blk", "split"), None), P(("blk", "split"), None))
    return jax.shard_map(local, mesh=mesh, in_specs=in_specs, out_specs=out_specs, check_vma=False)
```

time: 119 us -> 110 us (0.924); the launches traced: 117 us -> 110 us
  blocking collectives: 29.6 us -> 0 us
  starting transfers between devices: 51.3 us -> 79.4 us
  waiting for transfers between devices: 23.6 us -> 8.04 us
  Pallas kernels: 6.58 us -> 17.5 us
  local copies, waits for them, and re-layouts: 5.62 us -> 3.85 us
    all_to_all x4 -> x1, starting transfers between devices: 26.6 us -> 57.8 us  [local(): parts = lax.all_to_all(out.reshape(n, share_rows, rank), 'split', 0, 0)]
    all_to_all x3 -> x0, blocking collectives: 29.6 us -> none  [local(): parts = lax.all_to_all(grad.reshape(n, share_rows, rank), 'split', 0, 0)]
    all_to_all x4 -> x1, waiting for transfers between devices: 18.5 us -> 0.01 us  [local(): parts = lax.all_to_all(out.reshape(n, share_rows, rank), 'split', 0, 0)]
    pallas_call x12 -> x11, Pallas kernels: 6.58 us -> 17.5 us  [the longest x4 9.6 us: local(): call(kernel, [(chunks, slab, users), (slab, rank)], 'group')]
    ppermute x4 -> x13, starting transfers between devices: 24.7 us -> 21.6 us  [the longest x1 9.95 us: local(): lax.ppermute(share, 'blk', [((b + 1) % blocks, b) for b in range(blocks)])]
    ppermute x4 -> x13, waiting for transfers between devices: 5.1 us -> 8.04 us  [the longest x3 6.26 us: fetch(): return lax.ppermute(x, both, pairs)]
    broadcast_in_dim x3 -> x0, local copies, waits for them, and re-layouts: 2.18 us -> none  [local(): copies = jnp.broadcast_to(share[None], (n, share_rows, rank))]
    unnamed x9 -> x10, local copies, waits for them, and re-layouts: 2.61 us -> 3.85 us
  transfers between devices with their start and end apart: 8 -> 14, of which waited for: 8 -> 3; matrix products, arithmetic and copies ran while one was open for 0% -> 0% of each run, Pallas kernels for 2% -> 5%
where the time goes in v3:
time: 110 us
  starting transfers between devices  79.4 us (72%)
  Pallas kernels  17.5 us (16%)
  waiting for transfers between devices  8.04 us (7%)
  local copies, waits for them, and re-layouts  3.85 us (4%)
    all_to_all x1, starting transfers between devices, local(): parts = lax.all_to_all(out.reshape(n, share_rows, rank), 'split', 0, 0)  57.8 us
    ppermute x1, starting transfers between devices, local(): lax.ppermute(share, 'blk', [((b + 1) % blocks, b) for b in range(blocks)])  9.95 us
    pallas_call x4, Pallas kernels, local(): call(kernel, [(chunks, slab, users), (slab, rank)], 'group')  9.6 us
    ppermute x3, waiting for transfers between devices, fetch(): return lax.ppermute(x, both, pairs)  6.26 us
    pallas_call x4, Pallas kernels, local(): user = call(kernel, [(users, rank)] * chunks, 'users')(*held, errors, *user)  4.95 us
    ppermute x3, starting transfers between devices, fetch(): return lax.ppermute(x, both, pairs)  4.91 us
    ppermute x6, starting transfers between devices, onward(): return [lax.ppermute(x, both, same), lax.ppermute(x, both, cross)]  4.06 us
    unnamed x10, local copies, waits for them, and re-layouts  3.85 us
  transfers between devices with their start and end apart: 14, of which 3 were waited for; matrix products, arithmetic and copies ran while one was open for 0% of the time, Pallas kernels for 5%

profile of v3, /device:TPU:6, one launch (start us, length us, event | category | flops | bytes accessed | tf_op | source)
XLA Modules:
  0.0 109.7 jit_solution(12019855092223256941)
XLA Ops:
  0.6 2.1 %pack.1 = (f32[288,512]{1,0:T(8,128)}, f32[128,512]{1,0:T(8,128)}) custom-call(f32[256,512]{1,0:T(8,128)} %user_ref.1, f32[128,512]{1,0:T(8,128)} %held_ref.1, s32[4,8,256]{2,1,0:T(8,128)} %bitcast.3, s32[4,8,256]{2,1,0:T(8,128)} %bitcast.4), custom_call_target="tpu_custom_call" | custom-call | tf_op jit(solution)/shard_map/pack/pallas_call | solution.py:170
  2.7 3.5 %collective-permute-start.2 = (f32[288,512]{1,0:T(8,128)}, f32[288,512]{1,0:T(8,128)S(1)}, u32[]{:S(2)}, u32[]{:S(2)}) collective-permute-start(f32[288,512]{1,0:T(8,128)} %get-tuple-element.29.refs_1_.refs_5_.refs_2_.refs_6_), channel_id=1, source_target_pairs={{3,2},{6,7},{10,11},{15,14},{19,18},{22,23},{26,27},{31,30},{35,34... | collective-permute-start | bytes 1769480 | tf_op jit(solution)/shard_map/ppermute | solution.py:154
  6.2 0.7 collective-permute-start.1
  6.9 0.7 collective-permute-start
  7.7 6.2 %collective-permute-done.2.refs_4_.refs_8_.refs_5_.refs_9_ = f32[288,512]{1,0:T(8,128)S(1)} collective-permute-done((f32[288,512]{1,0:T(8,128)}, f32[288,512]{1,0:T(8,128)S(1)}, u32[]{:S(2)}, u32[]{:S(2)}) %collective-permute-start.2) | collective-permute-done | bytes 589856 | tf_op jit(solution)/shard_map/ppermute | solution.py:154
  13.9 1.1 copy-done
  15.0 0.9 copy-done.2
  15.9 2.2 %group.4 = (f32[4,128,256]{2,1,0:T(8,128)S(1)}, f32[128,512]{1,0:T(8,128)S(1)}) custom-call(f32[128,512]{1,0:T(8,128)S(1)} %copy-done.2, f32[288,512]{1,0:T(8,128)S(1)} %copy-done, f32[288,512]{1,0:T(8,128)S(1)} %collective-permute-done.refs_2_.refs_6_.refs_3_.refs_7_, f32[288,512]{1,0:T(8,128)S(1)} %collective-permute-done.1.refs_3_.refs_7_.refs_4_.refs_8_, ...), custom_call_target="tpu_custom_call" | custom-call | tf_op jit(solution)/shard_map/group/pallas_call | solution.py:182
  19.5 1.0 users.4
  20.6 2.2 %group.5 = (f32[4,128,256]{2,1,0:T(8,128)S(1)}, f32[128,512]{1,0:T(8,128)S(1)}) custom-call(f32[128,512]{1,0:T(8,128)S(1)} %collective-permute-done.3.refs_0_, f32[128,512]{1,0:T(8,128)S(1)} %collective-permute-done.4.refs_1_, f32[256,512]{1,0:T(8,128)S(1)} %get-tuple-element.32.refs_2_.refs_3_, f32[256,512]{1,0:T(8,128)S(1)} %get-tuple-element.33.refs_3_.refs_4_, ...), custom_call_target="tpu_custom_call" | custom-call | tf_op jit(solution)/shard_map/group/pallas_call | solution.py:182
  24.2 1.0 users.5
  25.3 2.2 %group.6 = (f32[4,128,256]{2,1,0:T(8,128)S(1)}, f32[128,512]{1,0:T(8,128)S(1)}) custom-call(f32[128,512]{1,0:T(8,128)S(1)} %collective-permute-done.5.refs_0_, f32[128,512]{1,0:T(8,128)S(1)} %collective-permute-done.6.refs_1_, f32[256,512]{1,0:T(8,128)S(1)} %get-tuple-element.38.refs_2_.refs_3_, f32[256,512]{1,0:T(8,128)S(1)} %get-tuple-element.39.refs_3_.refs_4_, ...), custom_call_target="tpu_custom_call" | custom-call | tf_op jit(solution)/shard_map/group/pallas_call | solution.py:182
  28.9 1.0 users.6
  29.9 2.9 %group.7 = (f32[4,128,256]{2,1,0:T(8,128)S(1)}, f32[128,512]{1,0:T(8,128)}) custom-call(f32[128,512]{1,0:T(8,128)S(1)} %collective-permute-done.7.refs_0_, f32[128,512]{1,0:T(8,128)S(1)} %collective-permute-done.8.refs_1_, f32[256,512]{1,0:T(8,128)S(1)} %get-tuple-element.44.refs_2_.refs_3_, f32[256,512]{1,0:T(8,128)S(1)} %get-tuple-element.45.refs_3_.refs_4_, ...), custom_call_target="tpu_custom_call" | custom-call | tf_op jit(solution)/shard_map/group/pallas_call | solution.py:182
  32.9 0.8 copy-done.3
  33.7 57.8 %all-to-all-start = ((f32[8,16,512]{2,1,0:T(8,128)}), f32[8,16,512]{2,1,0:T(8,128)S(1)}, u32[]{:S(2)}, u32[]{:S(2)}) async-start(f32[8,16,512]{2,1,0:T(8,128)} %bitcast.2), calls=%async_computation | async-start | bytes 524288 | tf_op jit(solution)/shard_map/all_to_all | solution.py:186
  91.4 1.0 copy-done.4
  92.5 1.9 %users.7 = (f32[256,512]{1,0:T(8,128)S(1)}, f32[256,512]{1,0:T(8,128)}, f32[256,512]{1,0:T(8,128)}, f32[256,512]{1,0:T(8,128)}) custom-call(f32[128,512]{1,0:T(8,128)S(1)} %collective-permute-done.7.refs_0_, f32[128,512]{1,0:T(8,128)S(1)} %collective-permute-done.8.refs_1_, f32[4,128,256]{2,1,0:T(8,128)S(1)} %copy-done.4, ...), custom_call_target="tpu_custom_call" | custom-call | tf_op jit(solution)/shard_map/users/pallas_call | solution.py:188
  94.3 0.7 collective-permute-start.10
  95.0 0.7 collective-permute-start.11
  95.7 1.3 %collective-permute-start.12 = (f32[256,512]{1,0:T(8,128)}, f32[256,512]{1,0:T(8,128)S(1)}, u32[]{:S(2)}, u32[]{:S(2)}) collective-permute-start(f32[256,512]{1,0:T(8,128)} %get-tuple-element.53), channel_id=1, source_target_pairs={{2,3},{7,6},{11,10},{14,15},{18,19},{23,22},{27,26},{30,31},{34,35... | collective-permute-start | bytes 1572872 | tf_op jit(solution)/shard_map/ppermute | solution.py:158
  97.1 10.0 %collective-permute-start.9 = (f32[16,512]{1,0:T(8,128)S(1)}, f32[16,512]{1,0:T(8,128)S(1)}, u32[]{:S(2)}, u32[]{:S(2)}) collective-permute-start(f32[16,512]{1,0:T(8,128)S(1)} %share.1), channel_id=1, source_target_pairs={{8,0},{16,8},{24,16},{32,24},{40,32},{48,40},{56,48},{64,56},{72,6... | collective-permute-start | bytes 98312 | tf_op jit(solution)/shard_map/ppermute | solution.py:192
  107.0 1.6 %collective-permute-done.9.share_ref = f32[16,512]{1,0:T(8,128)S(1)} collective-permute-done((f32[16,512]{1,0:T(8,128)S(1)}, f32[16,512]{1,0:T(8,128)S(1)}, u32[]{:S(2)}, u32[]{:S(2)}) %collective-permute-start.9) | collective-permute-done | bytes 32800 | tf_op jit(solution)/shard_map/ppermute | solution.py:192
  108.8 0.9 home.1
  (25 shorter events, 4.3 us)
Async XLA Ops:
  2.7 11.2 %collective-permute-start.2 = (f32[288,512]{1,0:T(8,128)}, f32[288,512]{1,0:T(8,128)S(1)}, u32[]{:S(2)}, u32[]{:S(2)}) collective-permute-start(f32[288,512]{1,0:T(8,128)} %get-tuple-element.29.refs_1_.refs_5_.refs_2_.refs_6_), channel_id=1, source_target_pairs={{3,2},{6,7},{10,11},{15,14},{19,18},{22,23},{26,27},{31,30},{35,34... | collective-permute-start | bytes 1769480 | tf_op jit(solution)/shard_map/ppermute | solution.py:154
  6.2 7.7 %collective-permute-start.1 = (f32[288,512]{1,0:T(8,128)}, f32[288,512]{1,0:T(8,128)S(1)}, u32[]{:S(2)}, u32[]{:S(2)}) collective-permute-start(f32[288,512]{1,0:T(8,128)} %get-tuple-element.29.refs_1_.refs_5_.refs_2_.refs_6_), channel_id=1, source_target_pairs={{4,2},{1,7},{13,11},{8,14},{20,18},{17,23},{29,27},{24,30},{36,34}... | collective-permute-start | bytes 1769480 | tf_op jit(solution)/shard_map/ppermute | solution.py:154
  6.9 7.0 %collective-permute-start = (f32[288,512]{1,0:T(8,128)}, f32[288,512]{1,0:T(8,128)S(1)}, u32[]{:S(2)}, u32[]{:S(2)}) collective-permute-start(f32[288,512]{1,0:T(8,128)} %get-tuple-element.29.refs_1_.refs_5_.refs_2_.refs_6_), channel_id=1, source_target_pairs={{0,2},{5,7},{9,11},{12,14},{16,18},{21,23},{25,27},{28,30},{32,34}... | collective-permute-start | bytes 1769480 | tf_op jit(solution)/shard_map/ppermute | solution.py:154
  13.9 1.1 copy-start
  15.0 0.9 copy-start.2
  18.2 2.4 %collective-permute-start.4 = (f32[128,512]{1,0:T(8,128)S(1)}, f32[128,512]{1,0:T(8,128)S(1)}, u32[]{:S(2)}, u32[]{:S(2)}) collective-permute-start(f32[128,512]{1,0:T(8,128)S(1)} %get-tuple-element.30), channel_id=1, source_target_pairs={{11,7},{14,2},{18,14},{23,11},{27,23},{30,18},{34,30},{39,27},{43,... | collective-permute-start | bytes 786440 | tf_op jit(solution)/shard_map/ppermute | solution.py:167
  18.8 1.7 %collective-permute-start.3 = (f32[128,512]{1,0:T(8,128)S(1)}, f32[128,512]{1,0:T(8,128)S(1)}, u32[]{:S(2)}, u32[]{:S(2)}) collective-permute-start(f32[128,512]{1,0:T(8,128)S(1)} %get-tuple-element.30), channel_id=1, source_target_pairs={{11,2},{14,7},{18,11},{23,14},{27,18},{30,23},{34,27},{39,30},{43,... | collective-permute-start | bytes 786440 | tf_op jit(solution)/shard_map/ppermute | solution.py:167
  22.8 2.4 %collective-permute-start.6 = (f32[128,512]{1,0:T(8,128)S(1)}, f32[128,512]{1,0:T(8,128)S(1)}, u32[]{:S(2)}, u32[]{:S(2)}) collective-permute-start(f32[128,512]{1,0:T(8,128)S(1)} %get-tuple-element.36), channel_id=1, source_target_pairs={{11,7},{14,2},{18,14},{23,11},{27,23},{30,18},{34,30},{39,27},{43,... | collective-permute-start | bytes 786440 | tf_op jit(solution)/shard_map/ppermute | solution.py:167
  23.5 1.8 %collective-permute-start.5 = (f32[128,512]{1,0:T(8,128)S(1)}, f32[128,512]{1,0:T(8,128)S(1)}, u32[]{:S(2)}, u32[]{:S(2)}) collective-permute-start(f32[128,512]{1,0:T(8,128)S(1)} %get-tuple-element.36), channel_id=1, source_target_pairs={{11,2},{14,7},{18,11},{23,14},{27,18},{30,23},{34,27},{39,30},{43,... | collective-permute-start | bytes 786440 | tf_op jit(solution)/shard_map/ppermute | solution.py:167
  24.2 1.1 copy-start.1
  27.5 2.4 %collective-permute-start.8 = (f32[128,512]{1,0:T(8,128)S(1)}, f32[128,512]{1,0:T(8,128)S(1)}, u32[]{:S(2)}, u32[]{:S(2)}) collective-permute-start(f32[128,512]{1,0:T(8,128)S(1)} %get-tuple-element.42), channel_id=1, source_target_pairs={{11,7},{14,2},{18,14},{23,11},{27,23},{30,18},{34,30},{39,27},{43,... | collective-permute-start | bytes 786440 | tf_op jit(solution)/shard_map/ppermute | solution.py:167
  28.2 1.7 %collective-permute-start.7 = (f32[128,512]{1,0:T(8,128)S(1)}, f32[128,512]{1,0:T(8,128)S(1)}, u32[]{:S(2)}, u32[]{:S(2)}) collective-permute-start(f32[128,512]{1,0:T(8,128)S(1)} %get-tuple-element.42), channel_id=1, source_target_pairs={{11,2},{14,7},{18,11},{23,14},{27,18},{30,23},{34,27},{39,30},{43,... | collective-permute-start | bytes 786440 | tf_op jit(solution)/shard_map/ppermute | solution.py:167
  32.9 0.8 copy-start.3
  33.7 63.4 %all-to-all-start = ((f32[8,16,512]{2,1,0:T(8,128)}), f32[8,16,512]{2,1,0:T(8,128)S(1)}, u32[]{:S(2)}, u32[]{:S(2)}) async-start(f32[8,16,512]{2,1,0:T(8,128)} %bitcast.2), calls=%async_computation | async-start | bytes 524288 | tf_op jit(solution)/shard_map/all_to_all | solution.py:186
  91.4 1.0 copy-start.4
  94.3 14.3 %collective-permute-start.10 = (f32[256,512]{1,0:T(8,128)}, f32[256,512]{1,0:T(8,128)S(1)}, u32[]{:S(2)}, u32[]{:S(2)}) collective-permute-start(f32[256,512]{1,0:T(8,128)} %get-tuple-element.51), channel_id=1, source_target_pairs={{2,0},{7,5},{11,9},{14,12},{18,16},{23,21},{27,25},{30,28},{34,32}... | collective-permute-start | bytes 1572872 | tf_op jit(solution)/shard_map/ppermute | solution.py:158
  95.0 13.6 %collective-permute-start.11 = (f32[256,512]{1,0:T(8,128)}, f32[256,512]{1,0:T(8,128)S(1)}, u32[]{:S(2)}, u32[]{:S(2)}) collective-permute-start(f32[256,512]{1,0:T(8,128)} %get-tuple-element.52), channel_id=1, source_target_pairs={{2,4},{7,1},{11,13},{14,8},{18,20},{23,17},{27,29},{30,24},{34,36}... | collective-permute-start | bytes 1572872 | tf_op jit(solution)/shard_map/ppermute | solution.py:158
  95.7 13.1 %collective-permute-start.12 = (f32[256,512]{1,0:T(8,128)}, f32[256,512]{1,0:T(8,128)S(1)}, u32[]{:S(2)}, u32[]{:S(2)}) collective-permute-start(f32[256,512]{1,0:T(8,128)} %get-tuple-element.53), channel_id=1, source_target_pairs={{2,3},{7,6},{11,10},{14,15},{18,19},{23,22},{27,26},{30,31},{34,35... | collective-permute-start | bytes 1572872 | tf_op jit(solution)/shard_map/ppermute | solution.py:158
  97.1 11.5 %collective-permute-start.9 = (f32[16,512]{1,0:T(8,128)S(1)}, f32[16,512]{1,0:T(8,128)S(1)}, u32[]{:S(2)}, u32[]{:S(2)}) collective-permute-start(f32[16,512]{1,0:T(8,128)S(1)} %share.1), channel_id=1, source_target_pairs={{8,0},{16,8},{24,16},{32,24},{40,32},{48,40},{56,48},{64,56},{72,6... | collective-permute-start | bytes 98312 | tf_op jit(solution)/shard_map/ppermute | solution.py:192

commit v4 on v3

v4 whole, which is shorter than its diff:
```python
import functools

import jax
import jax.numpy as jnp
from jax import lax
from jax.experimental import pallas as pl
from jax.experimental.pallas import tpu as pltpu
from jax.sharding import PartitionSpec as P

LEARN_RATE = 0.0005
CONF_SCALE = 0.5
RIDGE_COEF = 0.01
DECAY = 1.0 - LEARN_RATE * RIDGE_COEF
PARAMS = pltpu.CompilerParams(vmem_limit_bytes=16 << 20)

NT = (((1,), (1,)), ((), ()))
NN = (((1,), (0,)), ((), ()))
TN = (((0,), (0,)), ((), ()))

FIRST, SECOND = 2, 7
HELPERS = ((0, 5), (4, 1), (3, 6))


def halves(x):
    high = x.astype(jnp.bfloat16)
    low = (x - high.astype(jnp.float32)).astype(jnp.bfloat16)
    return high, low


def product(a, b, dims):
    def one(p, q):
        return lax.dot_general(p, q, dims, preferred_element_type=jnp.float32)

    return one(a[0], b[0]) + (one(a[0], b[1]) + one(a[1], b[0]))


def errors_of(held, user, items, conf):
    rows = lax.broadcasted_iota(jnp.int32, (held[0].shape[0], user[0].shape[0]), 0)
    counts = jnp.zeros(rows.shape, jnp.float32)
    for k in range(items.shape[0]):
        counts += jnp.where(items[k : k + 1] == rows, conf[k : k + 1], 0.0)
    target = jnp.where(counts > 0.0, 1.0, 0.0)
    return (1.0 + CONF_SCALE * counts) * (product(held, user, NT) - target)


def listed(ref, users, step, obs):
    at = users + step * obs
    return ref[at : at + obs, :users].astype(jnp.int32), ref[at : at + obs, users:]


def parity():
    return lax.axis_index("blk") & 1


def slab_of(refs):
    held = refs[0][...]
    for ref in refs[1:]:
        held += ref[...]
    return held


def call(kernel, outs, name, params=PARAMS, **kwargs):
    return pl.pallas_call(
        kernel,
        out_shape=[jax.ShapeDtypeStruct(o, jnp.float32) for o in outs],
        compiler_params=params,
        name=name,
        **kwargs,
    )


def pack_kernel(user_ref, items_ref, conf_ref, out_ref, items, conf, lists, sems):
    users = user_ref.shape[0]
    steps, obs, _ = items_ref.shape
    body = pltpu.make_async_copy(user_ref, out_ref.at[pl.ds(0, users), :], sems.at[0])
    loads = [
        pltpu.make_async_copy(items_ref, items, sems.at[1]),
        pltpu.make_async_copy(conf_ref, conf, sems.at[2]),
    ]
    for copy in (*loads, body):
        copy.start()
    for copy in loads:
        copy.wait()
    for s in range(steps):
        at = s * obs
        lists[at : at + obs, :users] = items[s].astype(jnp.float32)
        lists[at : at + obs, users:] = conf[s].astype(jnp.float32)
    tail = pltpu.make_async_copy(lists, out_ref.at[pl.ds(users, steps * obs), :], sems.at[3])
    tail.start()
    tail.wait()
    body.wait()


def kept():
    return jnp.where((lax.axis_index("split") ^ parity()) == FIRST, DECAY, 0.0)


def own_kernel(step, obs, held_ref, user_ref, errors_ref, total_ref):
    users = errors_ref.shape[1]
    user = halves(user_ref[:users, :])
    errors = errors_of(halves(held_ref[...]), user, *listed(user_ref, users, step, obs))
    errors_ref[...] = errors
    total_ref[...] = product(halves(errors), user, NN)


def group_kernel(step, obs, pieces, totals, chunks, *refs):
    held_refs, total_refs, refs = refs[:pieces], refs[pieces : pieces + totals], refs[pieces + totals :]
    user_refs, list_refs, out_ref, errors_refs = refs[:chunks], refs[chunks : 2 * chunks], refs[2 * chunks], refs[2 * chunks + 1 :]
    held = slab_of(held_refs)
    held_halves = halves(held)
    total = total_refs[0][...] if totals else jnp.zeros(held.shape, jnp.float32)
    for user_ref, list_ref, errors_ref in zip(user_refs, list_refs, errors_refs):
        users = errors_ref.shape[1]
        user = halves(user_ref[:users, :])
        errors = errors_of(held_halves, user, *listed(list_ref, users, step, obs))
        errors_ref[...] = errors
        total += product(halves(errors), user, NN)
    out_ref[...] = kept() * held - LEARN_RATE * total


def users_kernel(pieces, chunks, *refs):
    held_refs, errors_refs, refs = refs[:pieces], refs[pieces : pieces + chunks], refs[pieces + chunks :]
    user_refs, out_refs = refs[:chunks], refs[chunks:]
    held = halves(slab_of(held_refs))
    for errors_ref, user_ref, out_ref in zip(errors_refs, user_refs, out_refs):
        step = product(halves(errors_ref[...]), held, TN)
        out_ref[...] = DECAY * user_ref[: out_ref.shape[0], :] - LEARN_RATE * step


def last_kernel(step, obs, pieces, chunks, *refs):
    held_refs, refs = refs[:pieces], refs[pieces:]
    user_refs, list_refs, out_ref, new_refs = refs[:chunks], refs[chunks : 2 * chunks], refs[2 * chunks], refs[2 * chunks + 1 :]
    held = slab_of(held_refs)
    held_halves = halves(held)
    total = jnp.zeros(held.shape, jnp.float32)
    for user_ref, list_ref, new_ref in zip(user_refs, list_refs, new_refs):
        user = user_ref[...]
        user_halves = halves(user)
        errors = errors_of(held_halves, user_halves, *listed(list_ref, user_ref.shape[0], step, obs))
        errors = halves(errors)
        total += product(errors, user_halves, NN)
        new_ref[...] = DECAY * user - LEARN_RATE * product(errors, held_halves, TN)
    out_ref[...] = kept() * held - LEARN_RATE * total


def share_kernel(parts_ref, out_ref):
    out_ref[...] = parts_ref[FIRST ^ parity()] + parts_ref[SECOND ^ parity()]


def home_kernel(share_ref, own_ref, a_ref, b_ref, c_ref, out_ref, share_out_ref, sem):
    share_out_ref[...] = share_ref[...]
    place = lax.axis_index("split") ^ parity()
    for ref, places in zip((own_ref, a_ref, b_ref, c_ref), ((FIRST, SECOND), *HELPERS)):

        @pl.when((place == places[0]) | (place == places[1]))
        def _(ref=ref):
            copy = pltpu.make_async_copy(ref, out_ref, sem)
            copy.start()
            copy.wait()


def local(user_factors, item_factors, obs_items, obs_conf):
    slab, rank = item_factors.shape
    users = user_factors.shape[0]
    _, steps, obs = obs_items.shape
    n = lax.axis_size("split")
    blocks = lax.axis_size("blk")
    share_rows = slab // n
    chunks = 1 + len(HELPERS)
    items = jnp.transpose(obs_items, (1, 2, 0))
    conf = jnp.transpose(obs_conf, (1, 2, 0))
    both = ("blk", "split")

    def at(b, k):
        return b * n + (k ^ (b & 1))

    def fetch(x, helpers):
        pairs = [(at(b, h), at(b, w)) for b in range(blocks) for h, w in zip(helpers, (FIRST, SECOND))]
        return lax.ppermute(x, both, pairs)

    def give(x, helpers):
        pairs = [(at(b, w), at(b, h)) for b in range(blocks) for h, w in zip(helpers, (FIRST, SECOND))]
        return lax.ppermute(x, both, pairs)

    def onward(x):
        same, cross = [], []
        for b in range(blocks):
            for w, v in ((FIRST, SECOND), (SECOND, FIRST)):
                source = at((b + 1) % blocks, w)
                same.append((source, at(b, w)))
                cross.append((source, at(b, v)))
        return [lax.ppermute(x, both, same), lax.ppermute(x, both, cross)]

    hbm = pl.BlockSpec(memory_space=pltpu.HBM)
    lists_rows = steps * obs
    (own,) = call(
        pack_kernel,
        [(users + lists_rows, rank)],
        "pack",
        params=None,
        in_specs=[hbm] * 3,
        out_specs=[hbm],
        scratch_shapes=[pltpu.VMEM(items.shape, jnp.int32)] * 2
        + [pltpu.VMEM((lists_rows, rank), jnp.float32), pltpu.SemaphoreType.DMA((4,))],
    )(user_factors, items, conf)
    packs = [own] + [fetch(own, helpers) for helpers in HELPERS]
    user = packs
    held = [item_factors]
    for step in range(steps - 1):
        if step == 0:
            kernel = functools.partial(own_kernel, step, obs)
            own_errors, total = call(kernel, [(slab, users), (slab, rank)], "own")(item_factors, own)
            first, totals = [own_errors], [total]
        else:
            first, totals = [], []
        rest = chunks - len(first)
        kernel = functools.partial(group_kernel, step, obs, len(held), len(totals), rest)
        outs = [(slab, rank)] + [(slab, users)] * rest
        out, *errors = call(kernel, outs, "group")(*held, *totals, *user[-rest:], *packs[-rest:])
        sent = onward(out)
        kernel = functools.partial(users_kernel, len(held), chunks)
        user = call(kernel, [(users, rank)] * chunks, "users")(*held, *first, *errors, *user)
        held = sent
    kernel = functools.partial(last_kernel, steps - 1, obs, len(held), chunks)
    out, *user = call(kernel, [(slab, rank)] + [(users, rank)] * chunks, "last")(*held, *user, *packs)
    parts = lax.all_to_all(out.reshape(n, share_rows, rank), "split", 0, 0)
    early = pl.CostEstimate(flops=1 << 36, bytes_accessed=1 << 20, transcendentals=0)
    (share,) = call(share_kernel, [(share_rows, rank)], "share", cost_estimate=early)(parts)
    share = lax.ppermute(share, "blk", [((b + 1) % blocks, b) for b in range(blocks)])
    home = [give(u, helpers) for u, helpers in zip(user[1:], HELPERS)]
    user_out, share_out = call(
        home_kernel,
        [(users, rank), (share_rows, rank)],
        "home",
        out_specs=[pl.BlockSpec(memory_space=pltpu.HBM), pl.BlockSpec(memory_space=pltpu.VMEM)],
        scratch_shapes=[pltpu.SemaphoreType.DMA],
    )(share, user[0], *home)
    return user_out, share_out


def solution(mesh):
    in_specs = (
        P(("blk", "split"), None),
        P("blk", None),
        P(("blk", "split"), None, None),
        P(("blk", "split"), None, None),
    )
    out_specs = (P(("blk", "split"), None), P(("blk", "split"), None))
    return jax.shard_map(local, mesh=mesh, in_specs=in_specs, out_specs=out_specs, check_vma=False)
```

time: 110 us -> 121 us (1.10)
  Pallas kernels: 17.5 us -> 32.5 us
  local copies, waits for them, and re-layouts: 3.85 us -> 1.07 us
  starting transfers between devices: 79.4 us -> 77.2 us
    pallas_call x10, Pallas kernels: 17.5 us -> 32.5 us  [the longest x1 17 us: local(): call(pack_kernel, [(users + lists_rows, rank)], 'pack', params=None, in_s...]
    unnamed x10 -> x6, local copies, waits for them, and re-layouts: 3.85 us -> 1.07 us
    all_to_all x1, waiting for transfers between devices: 0.01 us -> 2.21 us  [local(): parts = lax.all_to_all(out.reshape(n, share_rows, rank), 'split', 0, 0)]
    ppermute x1, starting transfers between devices: 9.95 us -> 7.77 us  [local(): lax.ppermute(share, 'blk', [((b + 1) % blocks, b) for b in range(blocks)])]
    ppermute x3, waiting for transfers between devices: 6.26 us -> 4.33 us  [fetch(): return lax.ppermute(x, both, pairs)]
  transfers between devices with their start and end apart: 14 -> 14, of which waited for: 3 -> 4; matrix products, arithmetic and copies ran while one was open for 0% -> 0% of each run, Pallas kernels for 5% -> 3%
where the time goes in v4:
time: 121 us; the launch traced here: 120 us
  starting transfers between devices  77.2 us (64%)
  Pallas kernels  32.5 us (27%)
  waiting for transfers between devices  8.24 us (7%)
    all_to_all x1, starting transfers between devices, local(): parts = lax.all_to_all(out.reshape(n, share_rows, rank), 'split', 0, 0)  57.8 us
    pallas_call x1, Pallas kernels, local(): call(pack_kernel, [(users + lists_rows, rank)], 'pack', params=None, in_s...  17 us
    ppermute x1, starting transfers between devices, local(): lax.ppermute(share, 'blk', [((b + 1) % blocks, b) for b in range(blocks)])  7.77 us
    pallas_call x3, Pallas kernels, local(): call(kernel, outs, 'group')(*held, *totals, *user[-rest:], *packs[-rest:])  6.48 us
    ppermute x3, starting transfers between devices, fetch(): return lax.ppermute(x, both, pairs)  4.91 us
    ppermute x3, waiting for transfers between devices, fetch(): return lax.ppermute(x, both, pairs)  4.33 us
    ppermute x6, starting transfers between devices, onward(): return [lax.ppermute(x, both, same), lax.ppermute(x, both, cross)]  4.06 us
    pallas_call x1, Pallas kernels, local(): call(kernel, [(slab, rank)] + [(users, rank)] * chunks, 'last')  3.61 us
  transfers between devices with their start and end apart: 14, of which 4 were waited for; matrix products, arithmetic and copies ran while one was open for 0% of the time, Pallas kernels for 3%

profile of v4, /device:TPU:6, one launch (start us, length us, event | category | flops | bytes accessed | tf_op | source)
XLA Modules:
  0.0 119.9 jit_solution(5300269697286239448)
XLA Ops:
  0.6 17.0 %pack.1.user_ref.refs_5_.refs_6_ = f32[288,512]{1,0:T(8,128)} custom-call(f32[256,512]{1,0:T(8,128)} %user_ref.1, s32[4,8,256]{2,1,0:T(8,128)} %bitcast.3, s32[4,8,256]{2,1,0:T(8,128)} %bitcast.4), custom_call_target="tpu_custom_call" | custom-call | tf_op jit(solution)/shard_map/pack/pallas_call | solution.py:196
  17.7 3.5 %collective-permute-start.2 = (f32[288,512]{1,0:T(8,128)}, f32[288,512]{1,0:T(8,128)S(1)}, u32[]{:S(2)}, u32[]{:S(2)}) collective-permute-start(f32[288,512]{1,0:T(8,128)} %pack.1.user_ref.refs_5_.refs_6_), channel_id=1, source_target_pairs={{3,2},{6,7},{10,11},{15,14},{19,18},{22,23},{26,27},{31,30},{35,34... | collective-permute-start | bytes 1769480 | tf_op jit(solution)/shard_map/ppermute | solution.py:179
  21.2 0.7 collective-permute-start.1
  21.9 0.7 collective-permute-start
  22.6 1.1 copy-done
  23.7 0.8 own.1
  24.5 4.3 %collective-permute-done.2.refs_4_.refs_7_.refs_8_.refs_9_ = f32[288,512]{1,0:T(8,128)S(1)} collective-permute-done((f32[288,512]{1,0:T(8,128)}, f32[288,512]{1,0:T(8,128)S(1)}, u32[]{:S(2)}, u32[]{:S(2)}) %collective-permute-start.2) | collective-permute-done | bytes 589856 | tf_op jit(solution)/shard_map/ppermute | solution.py:179
  28.9 2.0 %group.3 = (f32[128,512]{1,0:T(8,128)S(1)}, f32[128,256]{1,0:T(8,128)S(1)}, f32[128,256]{1,0:T(8,128)S(1)}, f32[128,256]{1,0:T(8,128)S(1)}) custom-call(f32[128,512]{1,0:T(8,128)S(1)} %copy-done.2, f32[128,512]{1,0:T(8,128)S(1)} %get-tuple-element.35.refs_1_, f32[288,512]{1,0:T(8,128)S(1)} %collective-permute-done.refs_2_.refs_5_.refs_6_.refs_7_, ...), custom_call_target="tpu_custom_call" | custom-call | tf_op jit(solution)/shard_map/group/pallas_call | solution.py:219
  30.9 0.7 collective-permute-start.4
  32.3 1.0 users.3
  33.3 2.2 %group.4 = (f32[128,512]{1,0:T(8,128)S(1)}, f32[128,256]{1,0:T(8,128)S(1)}, f32[128,256]{1,0:T(8,128)S(1)}, f32[128,256]{1,0:T(8,128)S(1)}, f32[128,256]{1,0:T(8,128)S(1)}) custom-call(f32[128,512]{1,0:T(8,128)S(1)} %collective-permute-done.3.refs_0_, f32[128,512]{1,0:T(8,128)S(1)} %collective-permute-done.4.refs_1_, ...), custom_call_target="tpu_custom_call" | custom-call | tf_op jit(solution)/shard_map/group/pallas_call | solution.py:219
  36.9 1.0 users.4
  38.0 2.2 %group.5 = (f32[128,512]{1,0:T(8,128)S(1)}, f32[128,256]{1,0:T(8,128)S(1)}, f32[128,256]{1,0:T(8,128)S(1)}, f32[128,256]{1,0:T(8,128)S(1)}, f32[128,256]{1,0:T(8,128)S(1)}) custom-call(f32[128,512]{1,0:T(8,128)S(1)} %collective-permute-done.5.refs_0_, f32[128,512]{1,0:T(8,128)S(1)} %collective-permute-done.6.refs_1_, ...), custom_call_target="tpu_custom_call" | custom-call | tf_op jit(solution)/shard_map/group/pallas_call | solution.py:219
  40.9 0.7 collective-permute-start.7
  41.6 1.0 users.5
  42.7 3.6 %last.1 = (f32[128,512]{1,0:T(8,128)}, f32[256,512]{1,0:T(8,128)S(1)}, f32[256,512]{1,0:T(8,128)}, f32[256,512]{1,0:T(8,128)S(1)}, f32[256,512]{1,0:T(8,128)S(1)}) custom-call(f32[128,512]{1,0:T(8,128)S(1)} %collective-permute-done.7.refs_0_, f32[128,512]{1,0:T(8,128)S(1)} %collective-permute-done.8.refs_1_, f32[256,512]{1,0:T(8,128)S(1)} %get-tuple-element.59.refs_2_, ...), custom_call_target="tpu_custom_call" | custom-call | tf_op jit(solution)/shard_map/last/pallas_call | solution.py:225
  46.3 57.8 %all-to-all-start = ((f32[8,16,512]{2,1,0:T(8,128)}), f32[8,16,512]{2,1,0:T(8,128)S(1)}, u32[]{:S(2)}, u32[]{:S(2)}) async-start(f32[8,16,512]{2,1,0:T(8,128)} %bitcast.2), calls=%async_computation | async-start | bytes 524288 | tf_op jit(solution)/shard_map/all_to_all | solution.py:226
  104.1 0.7 collective-permute-start.10
  104.8 0.7 collective-permute-start.11
  105.5 1.3 %collective-permute-start.12 = (f32[256,512]{1,0:T(8,128)S(1)}, f32[256,512]{1,0:T(8,128)S(1)}, u32[]{:S(2)}, u32[]{:S(2)}) collective-permute-start(f32[256,512]{1,0:T(8,128)S(1)} %get-tuple-element.67), channel_id=1, source_target_pairs={{2,3},{7,6},{11,10},{14,15},{18,19},{23,22},{27,26},{30,31},{34,35... | collective-permute-start | bytes 1572872 | tf_op jit(solution)/shard_map/ppermute | solution.py:183
  106.8 2.2 %all-to-all-done.parts_ref = f32[8,16,512]{2,1,0:T(8,128)S(1)} async-done(((f32[8,16,512]{2,1,0:T(8,128)}), f32[8,16,512]{2,1,0:T(8,128)S(1)}, u32[]{:S(2)}, u32[]{:S(2)}) %all-to-all-start) | async-done | bytes 262176 | tf_op jit(solution)/shard_map/all_to_all | solution.py:226
  109.0 7.8 %collective-permute-start.9 = (f32[16,512]{1,0:T(8,128)S(1)}, f32[16,512]{1,0:T(8,128)S(1)}, u32[]{:S(2)}, u32[]{:S(2)}) collective-permute-start(f32[16,512]{1,0:T(8,128)S(1)} %share.1), channel_id=1, source_target_pairs={{8,0},{16,8},{24,16},{32,24},{40,32},{48,40},{56,48},{64,56},{72,6... | collective-permute-start | bytes 98312 | tf_op jit(solution)/shard_map/ppermute | solution.py:229
  116.8 1.6 %collective-permute-done.9.share_ref = f32[16,512]{1,0:T(8,128)S(1)} collective-permute-done((f32[16,512]{1,0:T(8,128)S(1)}, f32[16,512]{1,0:T(8,128)S(1)}, u32[]{:S(2)}, u32[]{:S(2)}) %collective-permute-start.9) | collective-permute-done | bytes 32800 | tf_op jit(solution)/shard_map/ppermute | solution.py:229
  118.4 1.4 %home.1 = (f32[256,512]{1,0:T(8,128)}, f32[16,512]{1,0:T(8,128)}) custom-call(f32[16,512]{1,0:T(8,128)S(1)} %collective-permute-done.9.share_ref, f32[256,512]{1,0:T(8,128)S(1)} %get-tuple-element.64.own_ref, f32[256,512]{1,0:T(8,128)S(1)} %collective-permute-done.10.a_ref, f32[256,512]{1,0:T(8,128)S(1)} %collective-permute-done.11.b_ref, ...), custom_call_target="tpu_custom_call" | custom-call | tf_op jit(solution)/shard_map/home/pallas_call | solution.py:231
  (21 shorter events, 2.9 us)
Async XLA Ops:
  0.6 22.0 %copy-start.2 = (f32[128,512]{1,0:T(8,128)S(1)}, f32[128,512]{1,0:T(8,128)}, u32[]{:S(2)}) copy-start(f32[128,512]{1,0:T(8,128)} %refs_0_.3) | copy-start | bytes 786436
  17.7 11.2 %collective-permute-start.2 = (f32[288,512]{1,0:T(8,128)}, f32[288,512]{1,0:T(8,128)S(1)}, u32[]{:S(2)}, u32[]{:S(2)}) collective-permute-start(f32[288,512]{1,0:T(8,128)} %pack.1.user_ref.refs_5_.refs_6_), channel_id=1, source_target_pairs={{3,2},{6,7},{10,11},{15,14},{19,18},{22,23},{26,27},{31,30},{35,34... | collective-permute-start | bytes 1769480 | tf_op jit(solution)/shard_map/ppermute | solution.py:179
  21.2 7.7 %collective-permute-start.1 = (f32[288,512]{1,0:T(8,128)}, f32[288,512]{1,0:T(8,128)S(1)}, u32[]{:S(2)}, u32[]{:S(2)}) collective-permute-start(f32[288,512]{1,0:T(8,128)} %pack.1.user_ref.refs_5_.refs_6_), channel_id=1, source_target_pairs={{4,2},{1,7},{13,11},{8,14},{20,18},{17,23},{29,27},{24,30},{36,34}... | collective-permute-start | bytes 1769480 | tf_op jit(solution)/shard_map/ppermute | solution.py:179
  21.9 7.0 %collective-permute-start = (f32[288,512]{1,0:T(8,128)}, f32[288,512]{1,0:T(8,128)S(1)}, u32[]{:S(2)}, u32[]{:S(2)}) collective-permute-start(f32[288,512]{1,0:T(8,128)} %pack.1.user_ref.refs_5_.refs_6_), channel_id=1, source_target_pairs={{0,2},{5,7},{9,11},{12,14},{16,18},{21,23},{25,27},{28,30},{32,34}... | collective-permute-start | bytes 1769480 | tf_op jit(solution)/shard_map/ppermute | solution.py:179
  22.6 1.1 copy-start
  28.9 3.4 %copy-start.1 = (f32[288,512]{1,0:T(8,128)S(1)}, f32[288,512]{1,0:T(8,128)}, u32[]{:S(2)}) copy-start(f32[288,512]{1,0:T(8,128)} %pack.1.user_ref.refs_5_.refs_6_) | copy-start | bytes 1769476
  30.9 2.4 %collective-permute-start.4 = (f32[128,512]{1,0:T(8,128)S(1)}, f32[128,512]{1,0:T(8,128)S(1)}, u32[]{:S(2)}, u32[]{:S(2)}) collective-permute-start(f32[128,512]{1,0:T(8,128)S(1)} %get-tuple-element.36), channel_id=1, source_target_pairs={{11,7},{14,2},{18,14},{23,11},{27,23},{30,18},{34,30},{39,27},{43,... | collective-permute-start | bytes 786440 | tf_op jit(solution)/shard_map/ppermute | solution.py:192
  31.6 1.7 %collective-permute-start.3 = (f32[128,512]{1,0:T(8,128)S(1)}, f32[128,512]{1,0:T(8,128)S(1)}, u32[]{:S(2)}, u32[]{:S(2)}) collective-permute-start(f32[128,512]{1,0:T(8,128)S(1)} %get-tuple-element.36), channel_id=1, source_target_pairs={{11,2},{14,7},{18,11},{23,14},{27,18},{30,23},{34,27},{39,30},{43,... | collective-permute-start | bytes 786440 | tf_op jit(solution)/shard_map/ppermute | solution.py:192
  35.6 2.4 %collective-permute-start.6 = (f32[128,512]{1,0:T(8,128)S(1)}, f32[128,512]{1,0:T(8,128)S(1)}, u32[]{:S(2)}, u32[]{:S(2)}) collective-permute-start(f32[128,512]{1,0:T(8,128)S(1)} %get-tuple-element.45), channel_id=1, source_target_pairs={{11,7},{14,2},{18,14},{23,11},{27,23},{30,18},{34,30},{39,27},{43,... | collective-permute-start | bytes 786440 | tf_op jit(solution)/shard_map/ppermute | solution.py:192
  36.3 1.7 %collective-permute-start.5 = (f32[128,512]{1,0:T(8,128)S(1)}, f32[128,512]{1,0:T(8,128)S(1)}, u32[]{:S(2)}, u32[]{:S(2)}) collective-permute-start(f32[128,512]{1,0:T(8,128)S(1)} %get-tuple-element.45), channel_id=1, source_target_pairs={{11,2},{14,7},{18,11},{23,14},{27,18},{30,23},{34,27},{39,30},{43,... | collective-permute-start | bytes 786440 | tf_op jit(solution)/shard_map/ppermute | solution.py:192
  40.2 2.4 %collective-permute-start.8 = (f32[128,512]{1,0:T(8,128)S(1)}, f32[128,512]{1,0:T(8,128)S(1)}, u32[]{:S(2)}, u32[]{:S(2)}) collective-permute-start(f32[128,512]{1,0:T(8,128)S(1)} %get-tuple-element.54), channel_id=1, source_target_pairs={{11,7},{14,2},{18,14},{23,11},{27,23},{30,18},{34,30},{39,27},{43,... | collective-permute-start | bytes 786440 | tf_op jit(solution)/shard_map/ppermute | solution.py:192
  40.9 1.7 %collective-permute-start.7 = (f32[128,512]{1,0:T(8,128)S(1)}, f32[128,512]{1,0:T(8,128)S(1)}, u32[]{:S(2)}, u32[]{:S(2)}) collective-permute-start(f32[128,512]{1,0:T(8,128)S(1)} %get-tuple-element.54), channel_id=1, source_target_pairs={{11,2},{14,7},{18,11},{23,14},{27,18},{30,23},{34,27},{39,30},{43,... | collective-permute-start | bytes 786440 | tf_op jit(solution)/shard_map/ppermute | solution.py:192
  46.3 62.7 %all-to-all-start = ((f32[8,16,512]{2,1,0:T(8,128)}), f32[8,16,512]{2,1,0:T(8,128)S(1)}, u32[]{:S(2)}, u32[]{:S(2)}) async-start(f32[8,16,512]{2,1,0:T(8,128)} %bitcast.2), calls=%async_computation | async-start | bytes 524288 | tf_op jit(solution)/shard_map/all_to_all | solution.py:226
  104.1 14.3 %collective-permute-start.10 = (f32[256,512]{1,0:T(8,128)}, f32[256,512]{1,0:T(8,128)S(1)}, u32[]{:S(2)}, u32[]{:S(2)}) collective-permute-start(f32[256,512]{1,0:T(8,128)} %get-tuple-element.65), channel_id=1, source_target_pairs={{2,0},{7,5},{11,9},{14,12},{18,16},{23,21},{27,25},{30,28},{34,32}... | collective-permute-start | bytes 1572872 | tf_op jit(solution)/shard_map/ppermute | solution.py:183
  104.8 13.6 %collective-permute-start.11 = (f32[256,512]{1,0:T(8,128)S(1)}, f32[256,512]{1,0:T(8,128)S(1)}, u32[]{:S(2)}, u32[]{:S(2)}) collective-permute-start(f32[256,512]{1,0:T(8,128)S(1)} %get-tuple-element.66), channel_id=1, source_target_pairs={{2,4},{7,1},{11,13},{14,8},{18,20},{23,17},{27,29},{30,24},{34,36}... | collective-permute-start | bytes 1572872 | tf_op jit(solution)/shard_map/ppermute | solution.py:183
  105.5 13.0 %collective-permute-start.12 = (f32[256,512]{1,0:T(8,128)S(1)}, f32[256,512]{1,0:T(8,128)S(1)}, u32[]{:S(2)}, u32[]{:S(2)}) collective-permute-start(f32[256,512]{1,0:T(8,128)S(1)} %get-tuple-element.67), channel_id=1, source_target_pairs={{2,3},{7,6},{11,10},{14,15},{18,19},{23,22},{27,26},{30,31},{34,35... | collective-permute-start | bytes 1572872 | tf_op jit(solution)/shard_map/ppermute | solution.py:183
  109.0 9.3 %collective-permute-start.9 = (f32[16,512]{1,0:T(8,128)S(1)}, f32[16,512]{1,0:T(8,128)S(1)}, u32[]{:S(2)}, u32[]{:S(2)}) collective-permute-start(f32[16,512]{1,0:T(8,128)S(1)} %share.1), channel_id=1, source_target_pairs={{8,0},{16,8},{24,16},{32,24},{40,32},{48,40},{56,48},{64,56},{72,6... | collective-permute-start | bytes 98312 | tf_op jit(solution)/shard_map/ppermute | solution.py:229

commit v5 on v4

--- a/solution.py
+++ b/solution.py
@@ -18,6 +18,7 @@
 TN = (((0,), (0,)), ((), ()))
 
 FIRST, SECOND = 2, 7
+PIECES = 4
 HELPERS = ((0, 5), (4, 1), (3, 6))
 
 
@@ -69,26 +70,34 @@
     )
 
 
-def pack_kernel(user_ref, items_ref, conf_ref, out_ref, items, conf, lists, sems):
+def pack_kernel(user_ref, items_ref, conf_ref, out_ref, items, conf, pack, load_sems, store_sems):
     users = user_ref.shape[0]
     steps, obs, _ = items_ref.shape
-    body = pltpu.make_async_copy(user_ref, out_ref.at[pl.ds(0, users), :], sems.at[0])
+    rows = steps * obs
+    pieces = load_sems.shape[0] - 2
+    size = users // pieces
     loads = [
-        pltpu.make_async_copy(items_ref, items, sems.at[1]),
-        pltpu.make_async_copy(conf_ref, conf, sems.at[2]),
+        pltpu.make_async_copy(items_ref, items, load_sems.at[pieces]),
+        pltpu.make_async_copy(conf_ref, conf, load_sems.at[pieces + 1]),
     ]
-    for copy in (*loads, body):
+    places = [pl.ds(i * size, size) for i in range(pieces)]
+    bodies = [pltpu.make_async_copy(user_ref.at[p, :], pack.at[p, :], load_sems.at[i]) for i, p in enumerate(places)]
+    places.append(pl.ds(users, rows))
+    stores = [pltpu.make_async_copy(pack.at[p, :], out_ref.at[p, :], store_sems.at[i]) for i, p in enumerate(places)]
+    for copy in (*loads, *bodies):
         copy.start()
     for copy in loads:
         copy.wait()
     for s in range(steps):
-        at = s * obs
-        lists[at : at + obs, :users] = items[s].astype(jnp.float32)
-        lists[at : at + obs, users:] = conf[s].astype(jnp.float32)
-    tail = pltpu.make_async_copy(lists, out_ref.at[pl.ds(users, steps * obs), :], sems.at[3])
-    tail.start()
-    tail.wait()
-    body.wait()
+        at = users + s * obs
+        pack[at : at + obs, :users] = items[s].astype(jnp.float32)
+        pack[at : at + obs, users:] = conf[s].astype(jnp.float32)
+    stores[pieces].start()
+    for i in range(pieces):
+        bodies[i].wait()
+        stores[i].start()
+    for copy in stores:
+        copy.wait()
 
 
 def kept():
@@ -147,16 +156,14 @@
     out_ref[...] = parts_ref[FIRST ^ parity()] + parts_ref[SECOND ^ parity()]
 
 
-def home_kernel(share_ref, own_ref, a_ref, b_ref, c_ref, out_ref, share_out_ref, sem):
+def home_kernel(share_ref, own_ref, a_ref, b_ref, c_ref, out_ref, share_out_ref):
     share_out_ref[...] = share_ref[...]
     place = lax.axis_index("split") ^ parity()
     for ref, places in zip((own_ref, a_ref, b_ref, c_ref), ((FIRST, SECOND), *HELPERS)):
 
         @pl.when((place == places[0]) | (place == places[1]))
         def _(ref=ref):
-            copy = pltpu.make_async_copy(ref, out_ref, sem)
-            copy.start()
-            copy.wait()
+            out_ref[...] = ref[...]
 
 
 def local(user_factors, item_factors, obs_items, obs_conf):
@@ -201,7 +208,8 @@
         in_specs=[hbm] * 3,
         out_specs=[hbm],
         scratch_shapes=[pltpu.VMEM(items.shape, jnp.int32)] * 2
-        + [pltpu.VMEM((lists_rows, rank), jnp.float32), pltpu.SemaphoreType.DMA((4,))],
+        + [pltpu.VMEM((users + lists_rows, rank), jnp.float32)]
+        + [pltpu.SemaphoreType.DMA((PIECES + 2,)), pltpu.SemaphoreType.DMA((PIECES + 1,))],
     )(user_factors, items, conf)
     packs = [own] + [fetch(own, helpers) for helpers in HELPERS]
     user = packs
@@ -228,13 +236,8 @@
     (share,) = call(share_kernel, [(share_rows, rank)], "share", cost_estimate=early)(parts)
     share = lax.ppermute(share, "blk", [((b + 1) % blocks, b) for b in range(blocks)])
     home = [give(u, helpers) for u, helpers in zip(user[1:], HELPERS)]
-    user_out, share_out = call(
-        home_kernel,
-        [(users, rank), (share_rows, rank)],
-        "home",
-        out_specs=[pl.BlockSpec(memory_space=pltpu.HBM), pl.BlockSpec(memory_space=pltpu.VMEM)],
-        scratch_shapes=[pltpu.SemaphoreType.DMA],
-    )(share, user[0], *home)
+    outs = [(users, rank), (share_rows, rank)]
+    user_out, share_out = call(home_kernel, outs, "home")(share, user[0], *home)
     return user_out, share_out
 
 

time: 121 us -> 105 us (0.87)
  Pallas kernels: 32.5 us -> 16.8 us
    pallas_call x1, Pallas kernels: 17 us -> 1.92 us  [local(): call(pack_kernel, [(users + lists_rows, rank)], 'pack', params=None, in_s...]
  transfers between devices with their start and end apart: 14 -> 14, of which waited for: 4 -> 4; matrix products, arithmetic and copies ran while one was open for 0% -> 0% of each run, Pallas kernels for 3% -> 4%
where the time goes in v5:
time: 105 us; the launch traced here: 104 us
  starting transfers between devices  77.2 us (74%)
  Pallas kernels  16.8 us (16%)
  waiting for transfers between devices  8.24 us (8%)
  local copies, waits for them, and re-layouts  1.07 us (1%)
    all_to_all x1, starting transfers between devices, local(): parts = lax.all_to_all(out.reshape(n, share_rows, rank), 'split', 0, 0)  57.8 us
    ppermute x1, starting transfers between devices, local(): lax.ppermute(share, 'blk', [((b + 1) % blocks, b) for b in range(blocks)])  7.77 us
    pallas_call x3, Pallas kernels, local(): call(kernel, outs, 'group')(*held, *totals, *user[-rest:], *packs[-rest:])  6.48 us
    ppermute x3, starting transfers between devices, fetch(): return lax.ppermute(x, both, pairs)  4.91 us
    ppermute x3, waiting for transfers between devices, fetch(): return lax.ppermute(x, both, pairs)  4.33 us
    ppermute x6, starting transfers between devices, onward(): return [lax.ppermute(x, both, same), lax.ppermute(x, both, cross)]  4.06 us
    pallas_call x1, Pallas kernels, local(): call(kernel, [(slab, rank)] + [(users, rank)] * chunks, 'last')  3.61 us
    pallas_call x3, Pallas kernels, local(): call(kernel, [(users, rank)] * chunks, 'users')  3.11 us
  transfers between devices with their start and end apart: 14, of which 4 were waited for; matrix products, arithmetic and copies ran while one was open for 0% of the time, Pallas kernels for 4%

profile of v5, /device:TPU:6, one launch (start us, length us, event | category | flops | bytes accessed | tf_op | source)
XLA Modules:
  0.0 104.2 jit_solution(8944600137511320355)
XLA Ops:
  0.6 1.9 %pack.1.user_ref.refs_5_.refs_6_ = f32[288,512]{1,0:T(8,128)} custom-call(f32[256,512]{1,0:T(8,128)} %user_ref.1, s32[4,8,256]{2,1,0:T(8,128)} %bitcast.3, s32[4,8,256]{2,1,0:T(8,128)} %bitcast.4), custom_call_target="tpu_custom_call" | custom-call | tf_op jit(solution)/shard_map/pack/pallas_call | solution.py:203
  2.6 3.5 %collective-permute-start.2 = (f32[288,512]{1,0:T(8,128)}, f32[288,512]{1,0:T(8,128)S(1)}, u32[]{:S(2)}, u32[]{:S(2)}) collective-permute-start(f32[288,512]{1,0:T(8,128)} %pack.1.user_ref.refs_5_.refs_6_), channel_id=1, source_target_pairs={{3,2},{6,7},{10,11},{15,14},{19,18},{22,23},{26,27},{31,30},{35,34... | collective-permute-start | bytes 1769480 | tf_op jit(solution)/shard_map/ppermute | solution.py:186
  6.1 0.7 collective-permute-start.1
  6.8 0.7 collective-permute-start
  7.5 1.1 %copy-done = f32[288,512]{1,0:T(8,128)S(1)} copy-done((f32[288,512]{1,0:T(8,128)S(1)}, f32[288,512]{1,0:T(8,128)}, u32[]{:S(2)}) %copy-start) | copy-done | bytes 589848
  8.6 0.8 own.1
  9.4 4.3 %collective-permute-done.2.refs_4_.refs_7_.refs_8_.refs_9_ = f32[288,512]{1,0:T(8,128)S(1)} collective-permute-done((f32[288,512]{1,0:T(8,128)}, f32[288,512]{1,0:T(8,128)S(1)}, u32[]{:S(2)}, u32[]{:S(2)}) %collective-permute-start.2) | collective-permute-done | bytes 589856 | tf_op jit(solution)/shard_map/ppermute | solution.py:186
  13.8 2.0 %group.3 = (f32[128,512]{1,0:T(8,128)S(1)}, f32[128,256]{1,0:T(8,128)S(1)}, f32[128,256]{1,0:T(8,128)S(1)}, f32[128,256]{1,0:T(8,128)S(1)}) custom-call(f32[128,512]{1,0:T(8,128)S(1)} %copy-done.2, f32[128,512]{1,0:T(8,128)S(1)} %get-tuple-element.35.refs_1_, f32[288,512]{1,0:T(8,128)S(1)} %collective-permute-done.refs_2_.refs_5_.refs_6_.refs_7_, ...), custom_call_target="tpu_custom_call" | custom-call | tf_op jit(solution)/shard_map/group/pallas_call | solution.py:227
  15.8 0.7 collective-permute-start.4
  16.5 0.7 collective-permute-start.3
  17.2 1.0 users.3
  18.2 2.2 %group.4 = (f32[128,512]{1,0:T(8,128)S(1)}, f32[128,256]{1,0:T(8,128)S(1)}, f32[128,256]{1,0:T(8,128)S(1)}, f32[128,256]{1,0:T(8,128)S(1)}, f32[128,256]{1,0:T(8,128)S(1)}) custom-call(f32[128,512]{1,0:T(8,128)S(1)} %collective-permute-done.3.refs_0_, f32[128,512]{1,0:T(8,128)S(1)} %collective-permute-done.4.refs_1_, ...), custom_call_target="tpu_custom_call" | custom-call | tf_op jit(solution)/shard_map/group/pallas_call | solution.py:227
  21.8 1.0 users.4
  22.9 2.2 %group.5 = (f32[128,512]{1,0:T(8,128)S(1)}, f32[128,256]{1,0:T(8,128)S(1)}, f32[128,256]{1,0:T(8,128)S(1)}, f32[128,256]{1,0:T(8,128)S(1)}, f32[128,256]{1,0:T(8,128)S(1)}) custom-call(f32[128,512]{1,0:T(8,128)S(1)} %collective-permute-done.5.refs_0_, f32[128,512]{1,0:T(8,128)S(1)} %collective-permute-done.6.refs_1_, ...), custom_call_target="tpu_custom_call" | custom-call | tf_op jit(solution)/shard_map/group/pallas_call | solution.py:227
  26.5 1.0 users.5
  27.6 3.6 %last.1 = (f32[128,512]{1,0:T(8,128)}, f32[256,512]{1,0:T(8,128)S(1)}, f32[256,512]{1,0:T(8,128)}, f32[256,512]{1,0:T(8,128)S(1)}, f32[256,512]{1,0:T(8,128)S(1)}) custom-call(f32[128,512]{1,0:T(8,128)S(1)} %collective-permute-done.7.refs_0_, f32[128,512]{1,0:T(8,128)S(1)} %collective-permute-done.8.refs_1_, f32[256,512]{1,0:T(8,128)S(1)} %get-tuple-element.59.refs_2_, ...), custom_call_target="tpu_custom_call" | custom-call | tf_op jit(solution)/shard_map/last/pallas_call | solution.py:233
  31.2 57.8 %all-to-all-start = ((f32[8,16,512]{2,1,0:T(8,128)}), f32[8,16,512]{2,1,0:T(8,128)S(1)}, u32[]{:S(2)}, u32[]{:S(2)}) async-start(f32[8,16,512]{2,1,0:T(8,128)} %bitcast.2), calls=%async_computation | async-start | bytes 524288 | tf_op jit(solution)/shard_map/all_to_all | solution.py:234
  89.0 0.7 collective-permute-start.10
  89.7 0.7 collective-permute-start.11
  90.4 1.3 %collective-permute-start.12 = (f32[256,512]{1,0:T(8,128)S(1)}, f32[256,512]{1,0:T(8,128)S(1)}, u32[]{:S(2)}, u32[]{:S(2)}) collective-permute-start(f32[256,512]{1,0:T(8,128)S(1)} %get-tuple-element.67), channel_id=1, source_target_pairs={{2,3},{7,6},{11,10},{14,15},{18,19},{23,22},{27,26},{30,31},{34,35... | collective-permute-start | bytes 1572872 | tf_op jit(solution)/shard_map/ppermute | solution.py:190
  91.7 2.2 %all-to-all-done.parts_ref = f32[8,16,512]{2,1,0:T(8,128)S(1)} async-done(((f32[8,16,512]{2,1,0:T(8,128)}), f32[8,16,512]{2,1,0:T(8,128)S(1)}, u32[]{:S(2)}, u32[]{:S(2)}) %all-to-all-start) | async-done | bytes 262176 | tf_op jit(solution)/shard_map/all_to_all | solution.py:234
  93.9 7.8 %collective-permute-start.9 = (f32[16,512]{1,0:T(8,128)S(1)}, f32[16,512]{1,0:T(8,128)S(1)}, u32[]{:S(2)}, u32[]{:S(2)}) collective-permute-start(f32[16,512]{1,0:T(8,128)S(1)} %share.1), channel_id=1, source_target_pairs={{8,0},{16,8},{24,16},{32,24},{40,32},{48,40},{56,48},{64,56},{72,6... | collective-permute-start | bytes 98312 | tf_op jit(solution)/shard_map/ppermute | solution.py:237
  101.7 1.6 %collective-permute-done.9.share_ref = f32[16,512]{1,0:T(8,128)S(1)} collective-permute-done((f32[16,512]{1,0:T(8,128)S(1)}, f32[16,512]{1,0:T(8,128)S(1)}, u32[]{:S(2)}, u32[]{:S(2)}) %collective-permute-start.9) | collective-permute-done | bytes 32800 | tf_op jit(solution)/shard_map/ppermute | solution.py:237
  103.3 0.8 home.1
  (21 shorter events, 2.9 us)
Async XLA Ops:
  0.6 6.9 %copy-start.2 = (f32[128,512]{1,0:T(8,128)S(1)}, f32[128,512]{1,0:T(8,128)}, u32[]{:S(2)}) copy-start(f32[128,512]{1,0:T(8,128)} %refs_0_.3) | copy-start | bytes 786436
  2.6 11.2 %collective-permute-start.2 = (f32[288,512]{1,0:T(8,128)}, f32[288,512]{1,0:T(8,128)S(1)}, u32[]{:S(2)}, u32[]{:S(2)}) collective-permute-start(f32[288,512]{1,0:T(8,128)} %pack.1.user_ref.refs_5_.refs_6_), channel_id=1, source_target_pairs={{3,2},{6,7},{10,11},{15,14},{19,18},{22,23},{26,27},{31,30},{35,34... | collective-permute-start | bytes 1769480 | tf_op jit(solution)/shard_map/ppermute | solution.py:186
  6.1 7.7 %collective-permute-start.1 = (f32[288,512]{1,0:T(8,128)}, f32[288,512]{1,0:T(8,128)S(1)}, u32[]{:S(2)}, u32[]{:S(2)}) collective-permute-start(f32[288,512]{1,0:T(8,128)} %pack.1.user_ref.refs_5_.refs_6_), channel_id=1, source_target_pairs={{4,2},{1,7},{13,11},{8,14},{20,18},{17,23},{29,27},{24,30},{36,34}... | collective-permute-start | bytes 1769480 | tf_op jit(solution)/shard_map/ppermute | solution.py:186
  6.8 7.0 %collective-permute-start = (f32[288,512]{1,0:T(8,128)}, f32[288,512]{1,0:T(8,128)S(1)}, u32[]{:S(2)}, u32[]{:S(2)}) collective-permute-start(f32[288,512]{1,0:T(8,128)} %pack.1.user_ref.refs_5_.refs_6_), channel_id=1, source_target_pairs={{0,2},{5,7},{9,11},{12,14},{16,18},{21,23},{25,27},{28,30},{32,34}... | collective-permute-start | bytes 1769480 | tf_op jit(solution)/shard_map/ppermute | solution.py:186
  7.5 1.1 %copy-start = (f32[288,512]{1,0:T(8,128)S(1)}, f32[288,512]{1,0:T(8,128)}, u32[]{:S(2)}) copy-start(f32[288,512]{1,0:T(8,128)} %pack.1.user_ref.refs_5_.refs_6_) | copy-start | bytes 1769476
  13.8 3.4 %copy-start.1 = (f32[288,512]{1,0:T(8,128)S(1)}, f32[288,512]{1,0:T(8,128)}, u32[]{:S(2)}) copy-start(f32[288,512]{1,0:T(8,128)} %pack.1.user_ref.refs_5_.refs_6_) | copy-start | bytes 1769476
  15.8 2.4 %collective-permute-start.4 = (f32[128,512]{1,0:T(8,128)S(1)}, f32[128,512]{1,0:T(8,128)S(1)}, u32[]{:S(2)}, u32[]{:S(2)}) collective-permute-start(f32[128,512]{1,0:T(8,128)S(1)} %get-tuple-element.36), channel_id=1, source_target_pairs={{11,7},{14,2},{18,14},{23,11},{27,23},{30,18},{34,30},{39,27},{43,... | collective-permute-start | bytes 786440 | tf_op jit(solution)/shard_map/ppermute | solution.py:199
  16.5 1.7 %collective-permute-start.3 = (f32[128,512]{1,0:T(8,128)S(1)}, f32[128,512]{1,0:T(8,128)S(1)}, u32[]{:S(2)}, u32[]{:S(2)}) collective-permute-start(f32[128,512]{1,0:T(8,128)S(1)} %get-tuple-element.36), channel_id=1, source_target_pairs={{11,2},{14,7},{18,11},{23,14},{27,18},{30,23},{34,27},{39,30},{43,... | collective-permute-start | bytes 786440 | tf_op jit(solution)/shard_map/ppermute | solution.py:199
  20.5 2.4 %collective-permute-start.6 = (f32[128,512]{1,0:T(8,128)S(1)}, f32[128,512]{1,0:T(8,128)S(1)}, u32[]{:S(2)}, u32[]{:S(2)}) collective-permute-start(f32[128,512]{1,0:T(8,128)S(1)} %get-tuple-element.45), channel_id=1, source_target_pairs={{11,7},{14,2},{18,14},{23,11},{27,23},{30,18},{34,30},{39,27},{43,... | collective-permute-start | bytes 786440 | tf_op jit(solution)/shard_map/ppermute | solution.py:199
  21.2 1.7 %collective-permute-start.5 = (f32[128,512]{1,0:T(8,128)S(1)}, f32[128,512]{1,0:T(8,128)S(1)}, u32[]{:S(2)}, u32[]{:S(2)}) collective-permute-start(f32[128,512]{1,0:T(8,128)S(1)} %get-tuple-element.45), channel_id=1, source_target_pairs={{11,2},{14,7},{18,11},{23,14},{27,18},{30,23},{34,27},{39,30},{43,... | collective-permute-start | bytes 786440 | tf_op jit(solution)/shard_map/ppermute | solution.py:199
  25.1 2.4 %collective-permute-start.8 = (f32[128,512]{1,0:T(8,128)S(1)}, f32[128,512]{1,0:T(8,128)S(1)}, u32[]{:S(2)}, u32[]{:S(2)}) collective-permute-start(f32[128,512]{1,0:T(8,128)S(1)} %get-tuple-element.54), channel_id=1, source_target_pairs={{11,7},{14,2},{18,14},{23,11},{27,23},{30,18},{34,30},{39,27},{43,... | collective-permute-start | bytes 786440 | tf_op jit(solution)/shard_map/ppermute | solution.py:199
  25.8 1.7 %collective-permute-start.7 = (f32[128,512]{1,0:T(8,128)S(1)}, f32[128,512]{1,0:T(8,128)S(1)}, u32[]{:S(2)}, u32[]{:S(2)}) collective-permute-start(f32[128,512]{1,0:T(8,128)S(1)} %get-tuple-element.54), channel_id=1, source_target_pairs={{11,2},{14,7},{18,11},{23,14},{27,18},{30,23},{34,27},{39,30},{43,... | collective-permute-start | bytes 786440 | tf_op jit(solution)/shard_map/ppermute | solution.py:199
  31.2 62.7 %all-to-all-start = ((f32[8,16,512]{2,1,0:T(8,128)}), f32[8,16,512]{2,1,0:T(8,128)S(1)}, u32[]{:S(2)}, u32[]{:S(2)}) async-start(f32[8,16,512]{2,1,0:T(8,128)} %bitcast.2), calls=%async_computation | async-start | bytes 524288 | tf_op jit(solution)/shard_map/all_to_all | solution.py:234
  89.0 14.3 %collective-permute-start.10 = (f32[256,512]{1,0:T(8,128)}, f32[256,512]{1,0:T(8,128)S(1)}, u32[]{:S(2)}, u32[]{:S(2)}) collective-permute-start(f32[256,512]{1,0:T(8,128)} %get-tuple-element.65), channel_id=1, source_target_pairs={{2,0},{7,5},{11,9},{14,12},{18,16},{23,21},{27,25},{30,28},{34,32}... | collective-permute-start | bytes 1572872 | tf_op jit(solution)/shard_map/ppermute | solution.py:190
  89.7 13.6 %collective-permute-start.11 = (f32[256,512]{1,0:T(8,128)S(1)}, f32[256,512]{1,0:T(8,128)S(1)}, u32[]{:S(2)}, u32[]{:S(2)}) collective-permute-start(f32[256,512]{1,0:T(8,128)S(1)} %get-tuple-element.66), channel_id=1, source_target_pairs={{2,4},{7,1},{11,13},{14,8},{18,20},{23,17},{27,29},{30,24},{34,36}... | collective-permute-start | bytes 1572872 | tf_op jit(solution)/shard_map/ppermute | solution.py:190
  90.4 13.0 %collective-permute-start.12 = (f32[256,512]{1,0:T(8,128)S(1)}, f32[256,512]{1,0:T(8,128)S(1)}, u32[]{:S(2)}, u32[]{:S(2)}) collective-permute-start(f32[256,512]{1,0:T(8,128)S(1)} %get-tuple-element.67), channel_id=1, source_target_pairs={{2,3},{7,6},{11,10},{14,15},{18,19},{23,22},{27,26},{30,31},{34,35... | collective-permute-start | bytes 1572872 | tf_op jit(solution)/shard_map/ppermute | solution.py:190
  93.9 9.3 %collective-permute-start.9 = (f32[16,512]{1,0:T(8,128)S(1)}, f32[16,512]{1,0:T(8,128)S(1)}, u32[]{:S(2)}, u32[]{:S(2)}) collective-permute-start(f32[16,512]{1,0:T(8,128)S(1)} %share.1), channel_id=1, source_target_pairs={{8,0},{16,8},{24,16},{32,24},{40,32},{48,40},{56,48},{64,56},{72,6... | collective-permute-start | bytes 98312 | tf_op jit(solution)/shard_map/ppermute | solution.py:237

commit v6 on v3

v6 whole, which is shorter than its diff:
```python
import functools

import jax
import jax.numpy as jnp
from jax import lax
from jax.experimental import pallas as pl
from jax.experimental.pallas import tpu as pltpu
from jax.sharding import PartitionSpec as P

LEARN_RATE = 0.0005
CONF_SCALE = 0.5
RIDGE_COEF = 0.01
DECAY = 1.0 - LEARN_RATE * RIDGE_COEF
PARAMS = pltpu.CompilerParams(vmem_limit_bytes=16 << 20)

NT = (((1,), (1,)), ((), ()))
NN = (((1,), (0,)), ((), ()))
TN = (((0,), (0,)), ((), ()))

FIRST, SECOND = 2, 7
HELPERS = ((0, 5), (4, 1), (3, 6))


def halves(x):
    high = x.astype(jnp.bfloat16)
    low = (x - high.astype(jnp.float32)).astype(jnp.bfloat16)
    return high, low


def product(a, b, dims):
    def one(p, q):
        return lax.dot_general(p, q, dims, preferred_element_type=jnp.float32)

    return one(a[0], b[0]) + (one(a[0], b[1]) + one(a[1], b[0]))


def weigh(items, conf, slab):
    rows = lax.broadcasted_iota(jnp.int32, (slab, items.shape[1]), 0)
    counts = jnp.zeros(rows.shape, jnp.float32)
    for k in range(items.shape[0]):
        counts += jnp.where(items[k : k + 1] == rows, conf[k : k + 1], 0.0)
    weights = 1.0 + CONF_SCALE * counts
    return weights, jnp.where(counts > 0.0, weights, 0.0)


def listed(ref, users, step, obs):
    at = users + step * obs
    return ref[at : at + obs, :users].astype(jnp.int32), ref[at : at + obs, users:]


def parity():
    return lax.axis_index("blk") & 1


def slab_of(refs):
    held = refs[0][...]
    for ref in refs[1:]:
        held += ref[...]
    return held


def call(kernel, outs, name, params=PARAMS, **kwargs):
    return pl.pallas_call(
        kernel,
        out_shape=[jax.ShapeDtypeStruct(shape, dtype) for shape, dtype in outs],
        compiler_params=params,
        name=name,
        **kwargs,
    )


def kept():
    return jnp.where((lax.axis_index("split") ^ parity()) == FIRST, DECAY, 0.0)


def first_kernel(user_hbm, held_hbm, items_hbm, conf_hbm, part_hbm, pack_hbm, user_ref, held_ref, items, conf, part, pack, sems):
    users = user_ref.shape[0]
    slab = held_ref.shape[0]
    steps, obs, _ = items.shape
    pairs = ((items_hbm, items), (conf_hbm, conf), (held_hbm, held_ref), (user_hbm, user_ref))
    loads = [pltpu.make_async_copy(source, target, sems.at[i]) for i, (source, target) in enumerate(pairs)]
    for copy in loads:
        copy.start()
    loads[0].wait()
    loads[1].wait()
    for s in range(steps):
        at = users + s * obs
        pack[at : at + obs, :users] = items[s].astype(jnp.float32)
        pack[at : at + obs, users:] = conf[s].astype(jnp.float32)
    weights, targets = weigh(items[0], conf[0].astype(jnp.float32), slab)
    loads[2].wait()
    loads[3].wait()
    held = held_ref[...]
    held_halves = halves(held)
    user = halves(user_ref[...])
    errors = halves(weights * product(held_halves, user, NT) - targets)
    part[...] = kept() * held - LEARN_RATE * product(errors, user, NN)
    send_part = pltpu.make_async_copy(part, part_hbm, sems.at[4])
    send_part.start()
    pack[:users, :] = DECAY * user_ref[...] - LEARN_RATE * product(errors, held_halves, TN)
    send_pack = pltpu.make_async_copy(pack, pack_hbm, sems.at[5])
    send_pack.start()
    send_part.wait()
    send_pack.wait()


def sum_kernel(*refs):
    refs[-1][...] = slab_of(refs[:-1])


def prepare_kernel(step, obs, chunks, *refs):
    pack_refs, out_refs = refs[:chunks], refs[chunks:]
    for i, pack_ref in enumerate(pack_refs):
        high_ref, low_ref, weights_ref, targets_ref = out_refs[4 * i : 4 * i + 4]
        users = high_ref.shape[0]
        high_ref[...], low_ref[...] = halves(pack_ref[:users, :])
        weights_ref[...], targets_ref[...] = weigh(*listed(pack_ref, users, step, obs), weights_ref.shape[0])


def group_kernel(pieces, chunks, *refs):
    held_refs, ready_refs, out_ref, errors_refs = refs[:pieces], refs[pieces : pieces + 4 * chunks], refs[pieces + 4 * chunks], refs[pieces + 4 * chunks + 1 :]
    held = slab_of(held_refs)
    held_halves = halves(held)
    total = jnp.zeros(held.shape, jnp.float32)
    for i in range(chunks):
        high_ref, low_ref, weights_ref, targets_ref = ready_refs[4 * i : 4 * i + 4]
        user = high_ref[...], low_ref[...]
        errors = halves(weights_ref[...] * product(held_halves, user, NT) - targets_ref[...])
        errors_refs[2 * i][...], errors_refs[2 * i + 1][...] = errors
        total += product(errors, user, NN)
    out_ref[...] = kept() * held - LEARN_RATE * total


def users_kernel(step, obs, pieces, chunks, *refs):
    held_refs, errors_refs, refs = refs[:pieces], refs[pieces : pieces + 2 * chunks], refs[pieces + 2 * chunks :]
    user_refs, pack_refs, out_refs = refs[:chunks], refs[chunks : 2 * chunks], refs[2 * chunks :]
    held = halves(slab_of(held_refs))
    for i in range(chunks):
        out_ref, high_ref, low_ref, weights_ref, targets_ref = out_refs[5 * i : 5 * i + 5]
        users = out_ref.shape[0]
        move = product((errors_refs[2 * i][...], errors_refs[2 * i + 1][...]), held, TN)
        new = DECAY * user_refs[i][:users, :] - LEARN_RATE * move
        out_ref[...] = new
        high_ref[...], low_ref[...] = halves(new)
        weights_ref[...], targets_ref[...] = weigh(*listed(pack_refs[i], users, step + 1, obs), weights_ref.shape[0])


def last_kernel(pieces, chunks, *refs):
    held_refs, ready_refs, refs = refs[:pieces], refs[pieces : pieces + 4 * chunks], refs[pieces + 4 * chunks :]
    user_refs, out_ref, new_refs = refs[:chunks], refs[chunks], refs[chunks + 1 :]
    held = slab_of(held_refs)
    held_halves = halves(held)
    total = jnp.zeros(held.shape, jnp.float32)
    for i in range(chunks):
        high_ref, low_ref, weights_ref, targets_ref = ready_refs[4 * i : 4 * i + 4]
        user = high_ref[...], low_ref[...]
        errors = halves(weights_ref[...] * product(held_halves, user, NT) - targets_ref[...])
        total += product(errors, user, NN)
        new_refs[i][...] = DECAY * user_refs[i][...] - LEARN_RATE * product(errors, held_halves, TN)
    out_ref[...] = kept() * held - LEARN_RATE * total


def share_kernel(parts_ref, out_ref):
    out_ref[...] = parts_ref[FIRST ^ parity()] + parts_ref[SECOND ^ parity()]


def home_kernel(share_ref, own_ref, a_ref, b_ref, c_ref, out_ref, share_out_ref):
    share_out_ref[...] = share_ref[...]
    place = lax.axis_index("split") ^ parity()
    for ref, places in zip((own_ref, a_ref, b_ref, c_ref), ((FIRST, SECOND), *HELPERS)):

        @pl.when((place == places[0]) | (place == places[1]))
        def _(ref=ref):
            out_ref[...] = ref[...]


def local(user_factors, item_factors, obs_items, obs_conf):
    slab, rank = item_factors.shape
    users = user_factors.shape[0]
    _, steps, obs = obs_items.shape
    n = lax.axis_size("split")
    blocks = lax.axis_size("blk")
    share_rows = slab // n
    chunks = 1 + len(HELPERS)
    items = jnp.transpose(obs_items, (1, 2, 0))
    conf = jnp.transpose(obs_conf, (1, 2, 0))
    both = ("blk", "split")

    def at(b, k):
        return b * n + (k ^ (b & 1))

    def fetch(x, helpers):
        pairs = [(at(b, h), at(b, w)) for b in range(blocks) for h, w in zip(helpers, (FIRST, SECOND))]
        return lax.ppermute(x, both, pairs)

    def give(x, helpers):
        pairs = [(at(b, w), at(b, h)) for b in range(blocks) for h, w in zip(helpers, (FIRST, SECOND))]
        return lax.ppermute(x, both, pairs)

    def onward(x):
        pairs = [(at((b + 1) % blocks, w), at(b, w)) for b in range(blocks) for w in (FIRST, SECOND)]
        same = lax.ppermute(x, both, pairs)
        pairs = [(at(b, w), at(b, v)) for b in range(blocks) for w, v in ((FIRST, SECOND), (SECOND, FIRST))]
        return [same, lax.ppermute(same, both, pairs)]

    f32, bf16 = jnp.float32, jnp.bfloat16
    hbm = pl.BlockSpec(memory_space=pltpu.HBM)
    rows = users + steps * obs
    part, pack = call(
        first_kernel,
        [((slab, rank), f32), ((rows, rank), f32)],
        "first",
        params=None,
        in_specs=[hbm] * 4,
        out_specs=[hbm] * 2,
        scratch_shapes=[pltpu.VMEM(user_factors.shape, f32), pltpu.VMEM(item_factors.shape, f32)]
        + [pltpu.VMEM(items.shape, jnp.int32)] * 2
        + [pltpu.VMEM((slab, rank), f32), pltpu.VMEM((rows, rank), f32), pltpu.SemaphoreType.DMA((6,))],
    )(user_factors, item_factors, items, conf)
    arrived = [part] + [fetch(part, helpers) for helpers in HELPERS]
    packs = [pack] + [fetch(pack, helpers) for helpers in HELPERS]
    (out,) = call(sum_kernel, [((slab, rank), f32)], "sum")(*arrived)
    held = onward(out)
    factors, half, square = ((users, rank), f32), ((users, rank), bf16), ((slab, users), f32)
    pieces = len(held)
    ready = [half, half, square, square]
    kernel = functools.partial(prepare_kernel, 1, obs, chunks)
    ahead = call(kernel, ready * chunks, "prepare")(*packs)
    user = packs
    for step in range(1, steps - 1):
        kernel = functools.partial(group_kernel, pieces, chunks)
        outs = [((slab, rank), f32)] + [((slab, users), bf16)] * (2 * chunks)
        out, *errors = call(kernel, outs, "group")(*held, *ahead)
        sent = onward(out)
        kernel = functools.partial(users_kernel, step, obs, pieces, chunks)
        outs = call(kernel, [factors, *ready] * chunks, "users")(*held, *errors, *user, *packs)
        user = outs[::5]
        ahead = [x for i, x in enumerate(outs) if i % 5]
        held = sent
    kernel = functools.partial(last_kernel, pieces, chunks)
    out, *user = call(kernel, [((slab, rank), f32)] + [factors] * chunks, "last")(*held, *ahead, *user)
    parts = lax.all_to_all(out.reshape(n, share_rows, rank), "split", 0, 0)
    early = pl.CostEstimate(flops=1 << 36, bytes_accessed=1 << 20, transcendentals=0)
    (share,) = call(share_kernel, [((share_rows, rank), f32)], "share", cost_estimate=early)(parts)
    share = lax.ppermute(share, "blk", [((b + 1) % blocks, b) for b in range(blocks)])
    home = [give(u, helpers) for u, helpers in zip(user[1:], HELPERS)]
    outs = [factors, ((share_rows, rank), f32)]
    user_out, share_out = call(home_kernel, outs, "home")(share, user[0], *home)
    return user_out, share_out


def solution(mesh):
    in_specs = (
        P(("blk", "split"), None),
        P("blk", None),
        P(("blk", "split"), None, None),
        P(("blk", "split"), None, None),
    )
    out_specs = (P(("blk", "split"), None), P(("blk", "split"), None))
    return jax.shard_map(local, mesh=mesh, in_specs=in_specs, out_specs=out_specs, check_vma=False)
```

time: 110 us -> 117 us (1.064)
  starting transfers between devices: 79.4 us -> 88.6 us
  local copies, waits for them, and re-layouts: 3.85 us -> 0.95 us
  waiting for transfers between devices: 8.04 us -> 9.48 us
  Pallas kernels: 17.5 us -> 16.1 us
    all_to_all x1, starting transfers between devices: 57.8 us -> 67.3 us  [local(): parts = lax.all_to_all(out.reshape(n, share_rows, rank), 'split', 0, 0)]
    ppermute x1, starting transfers between devices: 9.95 us -> 5.69 us  [local(): lax.ppermute(share, 'blk', [((b + 1) % blocks, b) for b in range(blocks)])]
    ppermute x3 -> x6, starting transfers between devices: 4.91 us -> 8.92 us  [fetch(): return lax.ppermute(x, both, pairs)]
    all_to_all x1, waiting for transfers between devices: 0.01 us -> 3.14 us  [local(): parts = lax.all_to_all(out.reshape(n, share_rows, rank), 'split', 0, 0)]
    unnamed x10 -> x4, local copies, waits for them, and re-layouts: 3.85 us -> 0.95 us
    ppermute x3 -> x6, waiting for transfers between devices: 6.26 us -> 3.84 us  [fetch(): return lax.ppermute(x, both, pairs)]
    pallas_call x10 -> x9, Pallas kernels: 16.6 us -> 15.2 us  [the longest x2 4.02 us: local(): out, *errors = call(kernel, outs, 'group')(*held, *ahead)]
  transfers between devices with their start and end apart: 14 -> 17, of which waited for: 3 -> 4; matrix products, arithmetic and copies ran while one was open for 0% -> 0% of each run, Pallas kernels for 5% -> 4%
where the time goes in v6:
time: 117 us; the launch traced here: 116 us
  starting transfers between devices  88.6 us (76%)
  Pallas kernels  16.1 us (14%)
  waiting for transfers between devices  9.48 us (8%)
    all_to_all x1, starting transfers between devices, local(): parts = lax.all_to_all(out.reshape(n, share_rows, rank), 'split', 0, 0)  67.3 us
    ppermute x6, starting transfers between devices, fetch(): return lax.ppermute(x, both, pairs)  8.92 us
    ppermute x1, starting transfers between devices, local(): lax.ppermute(share, 'blk', [((b + 1) % blocks, b) for b in range(blocks)])  5.69 us
    pallas_call x2, Pallas kernels, local(): out, *errors = call(kernel, outs, 'group')(*held, *ahead)  4.02 us
    ppermute x6, waiting for transfers between devices, fetch(): return lax.ppermute(x, both, pairs)  3.84 us
    pallas_call x1, Pallas kernels, local(): call(kernel, [((slab, rank), f32)] + [factors] * chunks, 'last')  3.5 us
    pallas_call x2, Pallas kernels, local(): call(kernel, [factors, *ready] * chunks, 'users')  3.43 us
    pallas_call x1, Pallas kernels, local(): call(first_kernel, [((slab, rank), f32), ((rows, rank), f32)], 'first', p...  3.25 us
  transfers between devices with their start and end apart: 17, of which 4 were waited for; matrix products, arithmetic and copies ran while one was open for 0% of the time, Pallas kernels for 4%

profile of v6, /device:TPU:6, one launch (start us, length us, event | category | flops | bytes accessed | tf_op | source)
XLA Modules:
  0.0 116.0 jit_solution(12486203537904659612)
XLA Ops:
  0.6 3.3 %first.1 = (f32[128,512]{1,0:T(8,128)}, f32[288,512]{1,0:T(8,128)}) custom-call(f32[256,512]{1,0:T(8,128)} %user_hbm.1, f32[128,512]{1,0:T(8,128)} %held_hbm.1, s32[4,8,256]{2,1,0:T(8,128)} %bitcast.3, s32[4,8,256]{2,1,0:T(8,128)} %bitcast.4), custom_call_target="tpu_custom_call" | custom-call | tf_op jit(solution)/shard_map/first/pallas_call | solution.py:209
  3.9 3.5 %collective-permute-start.2 = (f32[128,512]{1,0:T(8,128)}, f32[128,512]{1,0:T(8,128)S(1)}, u32[]{:S(2)}, u32[]{:S(2)}) collective-permute-start(f32[128,512]{1,0:T(8,128)} %get-tuple-element.83.refs_0_), channel_id=1, source_target_pairs={{3,2},{6,7},{10,11},{15,14},{19,18},{22,23},{26,27},{31,30},{35,34... | collective-permute-start | bytes 786440 | tf_op jit(solution)/shard_map/ppermute | solution.py:194
  8.8 2.7 %collective-permute-start.7 = (f32[288,512]{1,0:T(8,128)}, f32[288,512]{1,0:T(8,128)S(1)}, u32[]{:S(2)}, u32[]{:S(2)}) collective-permute-start(f32[288,512]{1,0:T(8,128)} %get-tuple-element.84.refs_0_.refs_10_.refs_14_), channel_id=1, source_target_pairs={{3,2},{6,7},{10,11},{15,14},{19,18},{22,23},{26,27},{31,30},{35,34... | collective-permute-start | bytes 1769480 | tf_op jit(solution)/shard_map/ppermute | solution.py:194
  11.5 0.7 collective-permute-start.6
  12.2 0.7 collective-permute-start.5
  12.9 0.9 copy-done.1
  13.9 0.7 collective-permute-start.3
  15.3 3.8 %collective-permute-done.7.refs_3_.refs_13_.refs_17_ = f32[288,512]{1,0:T(8,128)S(1)} collective-permute-done((f32[288,512]{1,0:T(8,128)}, f32[288,512]{1,0:T(8,128)S(1)}, u32[]{:S(2)}, u32[]{:S(2)}) %collective-permute-start.7) | collective-permute-done | bytes 589856 | tf_op jit(solution)/shard_map/ppermute | solution.py:194
  19.1 1.0 prepare.1
  20.1 2.0 %group.2 = (f32[128,512]{1,0:T(8,128)S(1)}, bf16[128,256]{1,0:T(8,128)(2,1)S(1)}, bf16[128,256]{1,0:T(8,128)(2,1)S(1)}, bf16[128,256]{1,0:T(8,128)(2,1)S(1)}, bf...) custom-call(f32[128,512]{1,0:T(8,128)S(1)} %collective-permute-done., ...), custom_call_target="tpu_custom_call" | custom-call | tf_op jit(solution)/shard_map/group/pallas_call | solution.py:233
  22.8 0.7 collective-permute-start.9
  23.5 1.7 %users.2 = (f32[256,512]{1,0:T(8,128)S(1)}, bf16[256,512]{1,0:T(8,128)(2,1)S(1)}, bf16[256,512]{1,0:T(8,128)(2,1)S(1)}, f32[128,256]{1,0:T(8,128)S(1)}, f32[128,...) custom-call(f32[128,512]{1,0:T(8,128)S(1)} %collective-permute-done., ...), custom_call_target="tpu_custom_call" | custom-call | tf_op jit(solution)/shard_map/users/pallas_call | solution.py:236
  25.3 2.0 %group.3 = (f32[128,512]{1,0:T(8,128)S(1)}, bf16[128,256]{1,0:T(8,128)(2,1)S(1)}, bf16[128,256]{1,0:T(8,128)(2,1)S(1)}, bf16[128,256]{1,0:T(8,128)(2,1)S(1)}, bf...) custom-call(f32[128,512]{1,0:T(8,128)S(1)} %collective-permute-done., ...), custom_call_target="tpu_custom_call" | custom-call | tf_op jit(solution)/shard_map/group/pallas_call | solution.py:233
  28.7 1.7 %users.3 = (f32[256,512]{1,0:T(8,128)S(1)}, bf16[256,512]{1,0:T(8,128)(2,1)S(1)}, bf16[256,512]{1,0:T(8,128)(2,1)S(1)}, f32[128,256]{1,0:T(8,128)S(1)}, f32[128,...) custom-call(f32[128,512]{1,0:T(8,128)S(1)} %collective-permute-done., ...), custom_call_target="tpu_custom_call" | custom-call | tf_op jit(solution)/shard_map/users/pallas_call | solution.py:236
  30.4 3.5 %last.1 = (f32[128,512]{1,0:T(8,128)}, f32[256,512]{1,0:T(8,128)S(1)}, f32[256,512]{1,0:T(8,128)}, f32[256,512]{1,0:T(8,128)S(1)}, f32[256,512]{1,0:T(8,128)S(1)}) custom-call(f32[128,512]{1,0:T(8,128)S(1)} %collective-permute-done.10.refs_0_, f32[128,512]{1,0:T(8,128)S(1)} %collective-permute-done.11.refs_1_, ...), custom_call_target="tpu_custom_call" | custom-call | tf_op jit(solution)/shard_map/last/pallas_call | solution.py:241
  33.9 67.3 %all-to-all-start = ((f32[8,16,512]{2,1,0:T(8,128)}), f32[8,16,512]{2,1,0:T(8,128)S(1)}, u32[]{:S(2)}, u32[]{:S(2)}) async-start(f32[8,16,512]{2,1,0:T(8,128)} %bitcast.2), calls=%async_computation | async-start | bytes 524288 | tf_op jit(solution)/shard_map/all_to_all | solution.py:242
  101.2 0.7 collective-permute-start.13
  101.9 0.7 collective-permute-start.14
  102.6 1.3 %collective-permute-start.15 = (f32[256,512]{1,0:T(8,128)S(1)}, f32[256,512]{1,0:T(8,128)S(1)}, u32[]{:S(2)}, u32[]{:S(2)}) collective-permute-start(f32[256,512]{1,0:T(8,128)S(1)} %get-tuple-element.163), channel_id=1, source_target_pairs={{2,3},{7,6},{11,10},{14,15},{18,19},{23,22},{27,26},{30,31},{34,35... | collective-permute-start | bytes 1572872 | tf_op jit(solution)/shard_map/ppermute | solution.py:198
  103.9 3.1 %all-to-all-done.parts_ref = f32[8,16,512]{2,1,0:T(8,128)S(1)} async-done(((f32[8,16,512]{2,1,0:T(8,128)}), f32[8,16,512]{2,1,0:T(8,128)S(1)}, u32[]{:S(2)}, u32[]{:S(2)}) %all-to-all-start) | async-done | bytes 262176 | tf_op jit(solution)/shard_map/all_to_all | solution.py:242
  107.0 5.7 %collective-permute-start.12 = (f32[16,512]{1,0:T(8,128)S(1)}, f32[16,512]{1,0:T(8,128)S(1)}, u32[]{:S(2)}, u32[]{:S(2)}) collective-permute-start(f32[16,512]{1,0:T(8,128)S(1)} %share.1), channel_id=1, source_target_pairs={{8,0},{16,8},{24,16},{32,24},{40,32},{48,40},{56,48},{64,56},{72,6... | collective-permute-start | bytes 98312 | tf_op jit(solution)/shard_map/ppermute | solution.py:245
  112.7 1.6 %collective-permute-done.12.share_ref = f32[16,512]{1,0:T(8,128)S(1)} collective-permute-done((f32[16,512]{1,0:T(8,128)S(1)}, f32[16,512]{1,0:T(8,128)S(1)}, u32[]{:S(2)}, u32[]{:S(2)}) %collective-permute-start.12) | collective-permute-done | bytes 32800 | tf_op jit(solution)/shard_map/ppermute | solution.py:245
  114.3 0.9 collective-permute-done.15.c_ref
  115.2 0.8 home.1
  (24 shorter events, 4.2 us)
Async XLA Ops:
  3.9 8.3 %collective-permute-start.2 = (f32[128,512]{1,0:T(8,128)}, f32[128,512]{1,0:T(8,128)S(1)}, u32[]{:S(2)}, u32[]{:S(2)}) collective-permute-start(f32[128,512]{1,0:T(8,128)} %get-tuple-element.83.refs_0_), channel_id=1, source_target_pairs={{3,2},{6,7},{10,11},{15,14},{19,18},{22,23},{26,27},{31,30},{35,34... | collective-permute-start | bytes 786440 | tf_op jit(solution)/shard_map/ppermute | solution.py:194
  7.4 5.5 %collective-permute-start.1 = (f32[128,512]{1,0:T(8,128)}, f32[128,512]{1,0:T(8,128)S(1)}, u32[]{:S(2)}, u32[]{:S(2)}) collective-permute-start(f32[128,512]{1,0:T(8,128)} %get-tuple-element.83.refs_0_), channel_id=1, source_target_pairs={{4,2},{1,7},{13,11},{8,14},{20,18},{17,23},{29,27},{24,30},{36,34}... | collective-permute-start | bytes 786440 | tf_op jit(solution)/shard_map/ppermute | solution.py:194
  8.1 4.8 %collective-permute-start = (f32[128,512]{1,0:T(8,128)}, f32[128,512]{1,0:T(8,128)S(1)}, u32[]{:S(2)}, u32[]{:S(2)}) collective-permute-start(f32[128,512]{1,0:T(8,128)} %get-tuple-element.83.refs_0_), channel_id=1, source_target_pairs={{0,2},{5,7},{9,11},{12,14},{16,18},{21,23},{25,27},{28,30},{32,34}... | collective-permute-start | bytes 786440 | tf_op jit(solution)/shard_map/ppermute | solution.py:194
  8.8 10.4 %copy-start = (f32[288,512]{1,0:T(8,128)S(1)}, f32[288,512]{1,0:T(8,128)}, u32[]{:S(2)}) copy-start(f32[288,512]{1,0:T(8,128)} %get-tuple-element.84.refs_0_.refs_10_.refs_14_) | copy-start | bytes 1769476
  8.8 10.3 %collective-permute-start.7 = (f32[288,512]{1,0:T(8,128)}, f32[288,512]{1,0:T(8,128)S(1)}, u32[]{:S(2)}, u32[]{:S(2)}) collective-permute-start(f32[288,512]{1,0:T(8,128)} %get-tuple-element.84.refs_0_.refs_10_.refs_14_), channel_id=1, source_target_pairs={{3,2},{6,7},{10,11},{15,14},{19,18},{22,23},{26,27},{31,30},{35,34... | collective-permute-start | bytes 1769480 | tf_op jit(solution)/shard_map/ppermute | solution.py:194
  11.5 7.7 %collective-permute-start.6 = (f32[288,512]{1,0:T(8,128)}, f32[288,512]{1,0:T(8,128)S(1)}, u32[]{:S(2)}, u32[]{:S(2)}) collective-permute-start(f32[288,512]{1,0:T(8,128)} %get-tuple-element.84.refs_0_.refs_10_.refs_14_), channel_id=1, source_target_pairs={{4,2},{1,7},{13,11},{8,14},{20,18},{17,23},{29,27},{24,30},{36,34}... | collective-permute-start | bytes 1769480 | tf_op jit(solution)/shard_map/ppermute | solution.py:194
  12.2 7.0 %collective-permute-start.5 = (f32[288,512]{1,0:T(8,128)}, f32[288,512]{1,0:T(8,128)S(1)}, u32[]{:S(2)}, u32[]{:S(2)}) collective-permute-start(f32[288,512]{1,0:T(8,128)} %get-tuple-element.84.refs_0_.refs_10_.refs_14_), channel_id=1, source_target_pairs={{0,2},{5,7},{9,11},{12,14},{16,18},{21,23},{25,27},{28,30},{32,34}... | collective-permute-start | bytes 1769480 | tf_op jit(solution)/shard_map/ppermute | solution.py:194
  12.9 1.0 copy-start.1
  13.9 0.7 collective-permute-start.3
  14.6 5.5 %collective-permute-start.4 = (f32[128,512]{1,0:T(8,128)S(1)}, f32[128,512]{1,0:T(8,128)S(1)}, u32[]{:S(2)}, u32[]{:S(2)}) collective-permute-start(f32[128,512]{1,0:T(8,128)S(1)} %collective-permute-done.3.refs_0_), channel_id=1, source_target_pairs={{2,7},{7,2},{11,14},{14,11},{18,23},{23,18},{27,30},{30,27},{34,39... | collective-permute-start | bytes 786440 | tf_op jit(solution)/shard_map/ppermute | solution.py:204
  22.1 0.7 collective-permute-start.8
  22.8 2.4 %collective-permute-start.9 = (f32[128,512]{1,0:T(8,128)S(1)}, f32[128,512]{1,0:T(8,128)S(1)}, u32[]{:S(2)}, u32[]{:S(2)}) collective-permute-start(f32[128,512]{1,0:T(8,128)S(1)} %collective-permute-done.8.refs_0_), channel_id=1, source_target_pairs={{2,7},{7,2},{11,14},{14,11},{18,23},{23,18},{27,30},{30,27},{34,39... | collective-permute-start | bytes 786440 | tf_op jit(solution)/shard_map/ppermute | solution.py:204
  27.3 0.7 collective-permute-start.10
  28.0 2.4 %collective-permute-start.11 = (f32[128,512]{1,0:T(8,128)S(1)}, f32[128,512]{1,0:T(8,128)S(1)}, u32[]{:S(2)}, u32[]{:S(2)}) collective-permute-start(f32[128,512]{1,0:T(8,128)S(1)} %collective-permute-done.10.refs_0_), channel_id=1, source_target_pairs={{2,7},{7,2},{11,14},{14,11},{18,23},{23,18},{27,30},{30,27},{34,39... | collective-permute-start | bytes 786440 | tf_op jit(solution)/shard_map/ppermute | solution.py:204
  33.9 73.1 %all-to-all-start = ((f32[8,16,512]{2,1,0:T(8,128)}), f32[8,16,512]{2,1,0:T(8,128)S(1)}, u32[]{:S(2)}, u32[]{:S(2)}) async-start(f32[8,16,512]{2,1,0:T(8,128)} %bitcast.2), calls=%async_computation | async-start | bytes 524288 | tf_op jit(solution)/shard_map/all_to_all | solution.py:242
  101.2 13.1 %collective-permute-start.13 = (f32[256,512]{1,0:T(8,128)}, f32[256,512]{1,0:T(8,128)S(1)}, u32[]{:S(2)}, u32[]{:S(2)}) collective-permute-start(f32[256,512]{1,0:T(8,128)} %get-tuple-element.161), channel_id=1, source_target_pairs={{2,0},{7,5},{11,9},{14,12},{18,16},{23,21},{27,25},{30,28},{34,32}... | collective-permute-start | bytes 1572872 | tf_op jit(solution)/shard_map/ppermute | solution.py:198
  101.9 12.4 %collective-permute-start.14 = (f32[256,512]{1,0:T(8,128)S(1)}, f32[256,512]{1,0:T(8,128)S(1)}, u32[]{:S(2)}, u32[]{:S(2)}) collective-permute-start(f32[256,512]{1,0:T(8,128)S(1)} %get-tuple-element.162), channel_id=1, source_target_pairs={{2,4},{7,1},{11,13},{14,8},{18,20},{23,17},{27,29},{30,24},{34,36}... | collective-permute-start | bytes 1572872 | tf_op jit(solution)/shard_map/ppermute | solution.py:198
  102.6 12.6 %collective-permute-start.15 = (f32[256,512]{1,0:T(8,128)S(1)}, f32[256,512]{1,0:T(8,128)S(1)}, u32[]{:S(2)}, u32[]{:S(2)}) collective-permute-start(f32[256,512]{1,0:T(8,128)S(1)} %get-tuple-element.163), channel_id=1, source_target_pairs={{2,3},{7,6},{11,10},{14,15},{18,19},{23,22},{27,26},{30,31},{34,35... | collective-permute-start | bytes 1572872 | tf_op jit(solution)/shard_map/ppermute | solution.py:198
  107.0 7.3 %collective-permute-start.12 = (f32[16,512]{1,0:T(8,128)S(1)}, f32[16,512]{1,0:T(8,128)S(1)}, u32[]{:S(2)}, u32[]{:S(2)}) collective-permute-start(f32[16,512]{1,0:T(8,128)S(1)} %share.1), channel_id=1, source_target_pairs={{8,0},{16,8},{24,16},{32,24},{40,32},{48,40},{56,48},{64,56},{72,6... | collective-permute-start | bytes 98312 | tf_op jit(solution)/shard_map/ppermute | solution.py:245

commit v7 on v6

--- a/solution.py
+++ b/solution.py
@@ -198,12 +198,16 @@
         return lax.ppermute(x, both, pairs)
 
     def onward(x):
-        pairs = [(at((b + 1) % blocks, w), at(b, w)) for b in range(blocks) for w in (FIRST, SECOND)]
-        same = lax.ppermute(x, both, pairs)
-        pairs = [(at(b, w), at(b, v)) for b in range(blocks) for w, v in ((FIRST, SECOND), (SECOND, FIRST))]
-        return [same, lax.ppermute(same, both, pairs)]
+        same, cross = [], []
+        for b in range(blocks):
+            for w, v in ((FIRST, SECOND), (SECOND, FIRST)):
+                source = at((b + 1) % blocks, w)
+                same.append((source, at(b, w)))
+                cross.append((source, at(b, v)))
+        return [lax.ppermute(x, both, same), lax.ppermute(x, both, cross)]
 
     f32, bf16 = jnp.float32, jnp.bfloat16
+    early = pl.CostEstimate(flops=1 << 36, bytes_accessed=1 << 20, transcendentals=0)
     hbm = pl.BlockSpec(memory_space=pltpu.HBM)
     rows = users + steps * obs
     part, pack = call(
@@ -219,7 +223,7 @@
     )(user_factors, item_factors, items, conf)
     arrived = [part] + [fetch(part, helpers) for helpers in HELPERS]
     packs = [pack] + [fetch(pack, helpers) for helpers in HELPERS]
-    (out,) = call(sum_kernel, [((slab, rank), f32)], "sum")(*arrived)
+    (out,) = call(sum_kernel, [((slab, rank), f32)], "sum", cost_estimate=early)(*arrived)
     held = onward(out)
     factors, half, square = ((users, rank), f32), ((users, rank), bf16), ((slab, users), f32)
     pieces = len(held)
@@ -240,7 +244,6 @@
     kernel = functools.partial(last_kernel, pieces, chunks)
     out, *user = call(kernel, [((slab, rank), f32)] + [factors] * chunks, "last")(*held, *ahead, *user)
     parts = lax.all_to_all(out.reshape(n, share_rows, rank), "split", 0, 0)
-    early = pl.CostEstimate(flops=1 << 36, bytes_accessed=1 << 20, transcendentals=0)
     (share,) = call(share_kernel, [((share_rows, rank), f32)], "share", cost_estimate=early)(parts)
     share = lax.ppermute(share, "blk", [((b + 1) % blocks, b) for b in range(blocks)])
     home = [give(u, helpers) for u, helpers in zip(user[1:], HELPERS)]

time: 117 us -> 101 us (0.86)
  starting transfers between devices: 88.6 us -> 74.7 us
  waiting for transfers between devices: 9.48 us -> 7.76 us
    all_to_all x1, starting transfers between devices: 67.3 us -> 51.3 us  [local(): parts = lax.all_to_all(out.reshape(n, share_rows, rank), 'split', 0, 0)]
    ppermute x1, starting transfers between devices: 5.69 us -> 7.77 us  [local(): lax.ppermute(share, 'blk', [((b + 1) % blocks, b) for b in range(blocks)])]
where the time goes in v7:
time: 101 us; the launch traced here: 100 us
  starting transfers between devices  74.7 us (74%)
  Pallas kernels  16.1 us (16%)
  waiting for transfers between devices  7.76 us (8%)
    all_to_all x1, starting transfers between devices, local(): parts = lax.all_to_all(out.reshape(n, share_rows, rank), 'split', 0, 0)  51.3 us
    ppermute x6, starting transfers between devices, fetch(): return lax.ppermute(x, both, pairs)  8.92 us
    ppermute x1, starting transfers between devices, local(): lax.ppermute(share, 'blk', [((b + 1) % blocks, b) for b in range(blocks)])  7.77 us
    ppermute x6, starting transfers between devices, onward(): return [lax.ppermute(x, both, same), lax.ppermute(x, both, cross)]  4.06 us
    pallas_call x2, Pallas kernels, local(): out, *errors = call(kernel, outs, 'group')(*held, *ahead)  4.02 us
    ppermute x6, waiting for transfers between devices, fetch(): return lax.ppermute(x, both, pairs)  3.86 us
    pallas_call x1, Pallas kernels, local(): call(kernel, [((slab, rank), f32)] + [factors] * chunks, 'last')  3.5 us
    pallas_call x2, Pallas kernels, local(): call(kernel, [factors, *ready] * chunks, 'users')  3.43 us
  transfers between devices with their start and end apart: 17, of which 4 were waited for; matrix products, arithmetic and copies ran while one was open for 0% of the time, Pallas kernels for 4%

profile of v7, /device:TPU:6, one launch (start us, length us, event | category | flops | bytes accessed | tf_op | source)
XLA Modules:
  0.0 100.4 jit_solution(5392941081851706729)
XLA Ops:
  0.6 3.3 %first.1 = (f32[128,512]{1,0:T(8,128)}, f32[288,512]{1,0:T(8,128)}) custom-call(f32[256,512]{1,0:T(8,128)} %user_hbm.1, f32[128,512]{1,0:T(8,128)} %held_hbm.1, s32[4,8,256]{2,1,0:T(8,128)} %bitcast.3, s32[4,8,256]{2,1,0:T(8,128)} %bitcast.4), custom_call_target="tpu_custom_call" | custom-call | tf_op jit(solution)/shard_map/first/pallas_call | solution.py:213
  3.9 3.5 %collective-permute-start.2 = (f32[128,512]{1,0:T(8,128)}, f32[128,512]{1,0:T(8,128)S(1)}, u32[]{:S(2)}, u32[]{:S(2)}) collective-permute-start(f32[128,512]{1,0:T(8,128)} %get-tuple-element.83.refs_0_), channel_id=1, source_target_pairs={{3,2},{6,7},{10,11},{15,14},{19,18},{22,23},{26,27},{31,30},{35,34... | collective-permute-start | bytes 786440 | tf_op jit(solution)/shard_map/ppermute | solution.py:194
  8.8 2.7 %collective-permute-start.7 = (f32[288,512]{1,0:T(8,128)}, f32[288,512]{1,0:T(8,128)S(1)}, u32[]{:S(2)}, u32[]{:S(2)}) collective-permute-start(f32[288,512]{1,0:T(8,128)} %get-tuple-element.84.refs_0_.refs_10_.refs_14_), channel_id=1, source_target_pairs={{3,2},{6,7},{10,11},{15,14},{19,18},{22,23},{26,27},{31,30},{35,34... | collective-permute-start | bytes 1769480 | tf_op jit(solution)/shard_map/ppermute | solution.py:194
  11.5 0.7 collective-permute-start.6
  12.2 0.7 collective-permute-start.5
  12.9 0.9 copy-done.1
  13.9 0.7 collective-permute-start.4
  14.6 0.7 collective-permute-start.3
  15.3 3.8 %collective-permute-done.7.refs_3_.refs_13_.refs_17_ = f32[288,512]{1,0:T(8,128)S(1)} collective-permute-done((f32[288,512]{1,0:T(8,128)}, f32[288,512]{1,0:T(8,128)S(1)}, u32[]{:S(2)}, u32[]{:S(2)}) %collective-permute-start.7) | collective-permute-done | bytes 589856 | tf_op jit(solution)/shard_map/ppermute | solution.py:194
  19.1 1.0 prepare.1
  20.1 2.0 %group.2 = (f32[128,512]{1,0:T(8,128)S(1)}, bf16[128,256]{1,0:T(8,128)(2,1)S(1)}, bf16[128,256]{1,0:T(8,128)(2,1)S(1)}, bf16[128,256]{1,0:T(8,128)(2,1)S(1)}, bf...) custom-call(f32[128,512]{1,0:T(8,128)S(1)} %collective-permute-done., ...), custom_call_target="tpu_custom_call" | custom-call | tf_op jit(solution)/shard_map/group/pallas_call | solution.py:237
  23.5 1.7 %users.2 = (f32[256,512]{1,0:T(8,128)S(1)}, bf16[256,512]{1,0:T(8,128)(2,1)S(1)}, bf16[256,512]{1,0:T(8,128)(2,1)S(1)}, f32[128,256]{1,0:T(8,128)S(1)}, f32[128,...) custom-call(f32[128,512]{1,0:T(8,128)S(1)} %collective-permute-done., ...), custom_call_target="tpu_custom_call" | custom-call | tf_op jit(solution)/shard_map/users/pallas_call | solution.py:240
  25.3 2.0 %group.3 = (f32[128,512]{1,0:T(8,128)S(1)}, bf16[128,256]{1,0:T(8,128)(2,1)S(1)}, bf16[128,256]{1,0:T(8,128)(2,1)S(1)}, bf16[128,256]{1,0:T(8,128)(2,1)S(1)}, bf...) custom-call(f32[128,512]{1,0:T(8,128)S(1)} %collective-permute-done., ...), custom_call_target="tpu_custom_call" | custom-call | tf_op jit(solution)/shard_map/group/pallas_call | solution.py:237
  27.3 0.7 collective-permute-start.11
  28.7 1.7 %users.3 = (f32[256,512]{1,0:T(8,128)S(1)}, bf16[256,512]{1,0:T(8,128)(2,1)S(1)}, bf16[256,512]{1,0:T(8,128)(2,1)S(1)}, f32[128,256]{1,0:T(8,128)S(1)}, f32[128,...) custom-call(f32[128,512]{1,0:T(8,128)S(1)} %collective-permute-done., ...), custom_call_target="tpu_custom_call" | custom-call | tf_op jit(solution)/shard_map/users/pallas_call | solution.py:240
  30.4 3.5 %last.1 = (f32[128,512]{1,0:T(8,128)}, f32[256,512]{1,0:T(8,128)S(1)}, f32[256,512]{1,0:T(8,128)}, f32[256,512]{1,0:T(8,128)S(1)}, f32[256,512]{1,0:T(8,128)S(1)}) custom-call(f32[128,512]{1,0:T(8,128)S(1)} %collective-permute-done.10.refs_0_, f32[128,512]{1,0:T(8,128)S(1)} %collective-permute-done.11.refs_1_, ...), custom_call_target="tpu_custom_call" | custom-call | tf_op jit(solution)/shard_map/last/pallas_call | solution.py:245
  33.9 51.3 %all-to-all-start = ((f32[8,16,512]{2,1,0:T(8,128)}), f32[8,16,512]{2,1,0:T(8,128)S(1)}, u32[]{:S(2)}, u32[]{:S(2)}) async-start(f32[8,16,512]{2,1,0:T(8,128)} %bitcast.2), calls=%async_computation | async-start | bytes 524288 | tf_op jit(solution)/shard_map/all_to_all | solution.py:246
  85.2 0.7 collective-permute-start.13
  85.9 0.7 collective-permute-start.14
  86.6 1.3 %collective-permute-start.15 = (f32[256,512]{1,0:T(8,128)S(1)}, f32[256,512]{1,0:T(8,128)S(1)}, u32[]{:S(2)}, u32[]{:S(2)}) collective-permute-start(f32[256,512]{1,0:T(8,128)S(1)} %get-tuple-element.163), channel_id=1, source_target_pairs={{2,3},{7,6},{11,10},{14,15},{18,19},{23,22},{27,26},{30,31},{34,35... | collective-permute-start | bytes 1572872 | tf_op jit(solution)/shard_map/ppermute | solution.py:198
  87.9 2.2 %all-to-all-done.parts_ref = f32[8,16,512]{2,1,0:T(8,128)S(1)} async-done(((f32[8,16,512]{2,1,0:T(8,128)}), f32[8,16,512]{2,1,0:T(8,128)S(1)}, u32[]{:S(2)}, u32[]{:S(2)}) %all-to-all-start) | async-done | bytes 262176 | tf_op jit(solution)/shard_map/all_to_all | solution.py:246
  90.1 7.8 %collective-permute-start.12 = (f32[16,512]{1,0:T(8,128)S(1)}, f32[16,512]{1,0:T(8,128)S(1)}, u32[]{:S(2)}, u32[]{:S(2)}) collective-permute-start(f32[16,512]{1,0:T(8,128)S(1)} %share.1), channel_id=1, source_target_pairs={{8,0},{16,8},{24,16},{32,24},{40,32},{48,40},{56,48},{64,56},{72,6... | collective-permute-start | bytes 98312 | tf_op jit(solution)/shard_map/ppermute | solution.py:248
  97.9 1.6 %collective-permute-done.12.share_ref = f32[16,512]{1,0:T(8,128)S(1)} collective-permute-done((f32[16,512]{1,0:T(8,128)S(1)}, f32[16,512]{1,0:T(8,128)S(1)}, u32[]{:S(2)}, u32[]{:S(2)}) %collective-permute-start.12) | collective-permute-done | bytes 32800 | tf_op jit(solution)/shard_map/ppermute | solution.py:248
  99.6 0.8 home.1
  (24 shorter events, 3.6 us)
Async XLA Ops:
  3.9 8.3 %collective-permute-start.2 = (f32[128,512]{1,0:T(8,128)}, f32[128,512]{1,0:T(8,128)S(1)}, u32[]{:S(2)}, u32[]{:S(2)}) collective-permute-start(f32[128,512]{1,0:T(8,128)} %get-tuple-element.83.refs_0_), channel_id=1, source_target_pairs={{3,2},{6,7},{10,11},{15,14},{19,18},{22,23},{26,27},{31,30},{35,34... | collective-permute-start | bytes 786440 | tf_op jit(solution)/shard_map/ppermute | solution.py:194
  7.4 5.5 %collective-permute-start.1 = (f32[128,512]{1,0:T(8,128)}, f32[128,512]{1,0:T(8,128)S(1)}, u32[]{:S(2)}, u32[]{:S(2)}) collective-permute-start(f32[128,512]{1,0:T(8,128)} %get-tuple-element.83.refs_0_), channel_id=1, source_target_pairs={{4,2},{1,7},{13,11},{8,14},{20,18},{17,23},{29,27},{24,30},{36,34}... | collective-permute-start | bytes 786440 | tf_op jit(solution)/shard_map/ppermute | solution.py:194
  8.1 4.8 %collective-permute-start = (f32[128,512]{1,0:T(8,128)}, f32[128,512]{1,0:T(8,128)S(1)}, u32[]{:S(2)}, u32[]{:S(2)}) collective-permute-start(f32[128,512]{1,0:T(8,128)} %get-tuple-element.83.refs_0_), channel_id=1, source_target_pairs={{0,2},{5,7},{9,11},{12,14},{16,18},{21,23},{25,27},{28,30},{32,34}... | collective-permute-start | bytes 786440 | tf_op jit(solution)/shard_map/ppermute | solution.py:194
  8.8 10.4 %copy-start = (f32[288,512]{1,0:T(8,128)S(1)}, f32[288,512]{1,0:T(8,128)}, u32[]{:S(2)}) copy-start(f32[288,512]{1,0:T(8,128)} %get-tuple-element.84.refs_0_.refs_10_.refs_14_) | copy-start | bytes 1769476
  8.8 10.3 %collective-permute-start.7 = (f32[288,512]{1,0:T(8,128)}, f32[288,512]{1,0:T(8,128)S(1)}, u32[]{:S(2)}, u32[]{:S(2)}) collective-permute-start(f32[288,512]{1,0:T(8,128)} %get-tuple-element.84.refs_0_.refs_10_.refs_14_), channel_id=1, source_target_pairs={{3,2},{6,7},{10,11},{15,14},{19,18},{22,23},{26,27},{31,30},{35,34... | collective-permute-start | bytes 1769480 | tf_op jit(solution)/shard_map/ppermute | solution.py:194
  11.5 7.7 %collective-permute-start.6 = (f32[288,512]{1,0:T(8,128)}, f32[288,512]{1,0:T(8,128)S(1)}, u32[]{:S(2)}, u32[]{:S(2)}) collective-permute-start(f32[288,512]{1,0:T(8,128)} %get-tuple-element.84.refs_0_.refs_10_.refs_14_), channel_id=1, source_target_pairs={{4,2},{1,7},{13,11},{8,14},{20,18},{17,23},{29,27},{24,30},{36,34}... | collective-permute-start | bytes 1769480 | tf_op jit(solution)/shard_map/ppermute | solution.py:194
  12.2 7.0 %collective-permute-start.5 = (f32[288,512]{1,0:T(8,128)}, f32[288,512]{1,0:T(8,128)S(1)}, u32[]{:S(2)}, u32[]{:S(2)}) collective-permute-start(f32[288,512]{1,0:T(8,128)} %get-tuple-element.84.refs_0_.refs_10_.refs_14_), channel_id=1, source_target_pairs={{0,2},{5,7},{9,11},{12,14},{16,18},{21,23},{25,27},{28,30},{32,34}... | collective-permute-start | bytes 1769480 | tf_op jit(solution)/shard_map/ppermute | solution.py:194
  12.9 1.0 copy-start.1
  13.9 6.2 %collective-permute-start.4 = (f32[128,512]{1,0:T(8,128)S(1)}, f32[128,512]{1,0:T(8,128)S(1)}, u32[]{:S(2)}, u32[]{:S(2)}) collective-permute-start(f32[128,512]{1,0:T(8,128)S(1)} %sum.1), channel_id=1, source_target_pairs={{11,7},{14,2},{18,14},{23,11},{27,23},{30,18},{34,30},{39,27},{43,... | collective-permute-start | bytes 786440 | tf_op jit(solution)/shard_map/ppermute | solution.py:207
  14.6 5.5 %collective-permute-start.3 = (f32[128,512]{1,0:T(8,128)S(1)}, f32[128,512]{1,0:T(8,128)S(1)}, u32[]{:S(2)}, u32[]{:S(2)}) collective-permute-start(f32[128,512]{1,0:T(8,128)S(1)} %sum.1), channel_id=1, source_target_pairs={{11,2},{14,7},{18,11},{23,14},{27,18},{30,23},{34,27},{39,30},{43,... | collective-permute-start | bytes 786440 | tf_op jit(solution)/shard_map/ppermute | solution.py:207
  22.2 3.1 %collective-permute-start.9 = (f32[128,512]{1,0:T(8,128)S(1)}, f32[128,512]{1,0:T(8,128)S(1)}, u32[]{:S(2)}, u32[]{:S(2)}) collective-permute-start(f32[128,512]{1,0:T(8,128)S(1)} %get-tuple-element.101), channel_id=1, source_target_pairs={{11,7},{14,2},{18,14},{23,11},{27,23},{30,18},{34,30},{39,27},{43,... | collective-permute-start | bytes 786440 | tf_op jit(solution)/shard_map/ppermute | solution.py:207
  22.8 2.4 %collective-permute-start.8 = (f32[128,512]{1,0:T(8,128)S(1)}, f32[128,512]{1,0:T(8,128)S(1)}, u32[]{:S(2)}, u32[]{:S(2)}) collective-permute-start(f32[128,512]{1,0:T(8,128)S(1)} %get-tuple-element.101), channel_id=1, source_target_pairs={{11,2},{14,7},{18,11},{23,14},{27,18},{30,23},{34,27},{39,30},{43,... | collective-permute-start | bytes 786440 | tf_op jit(solution)/shard_map/ppermute | solution.py:207
  27.3 3.1 %collective-permute-start.11 = (f32[128,512]{1,0:T(8,128)S(1)}, f32[128,512]{1,0:T(8,128)S(1)}, u32[]{:S(2)}, u32[]{:S(2)}) collective-permute-start(f32[128,512]{1,0:T(8,128)S(1)} %get-tuple-element.126), channel_id=1, source_target_pairs={{11,7},{14,2},{18,14},{23,11},{27,23},{30,18},{34,30},{39,27},{43,... | collective-permute-start | bytes 786440 | tf_op jit(solution)/shard_map/ppermute | solution.py:207
  28.0 2.4 %collective-permute-start.10 = (f32[128,512]{1,0:T(8,128)S(1)}, f32[128,512]{1,0:T(8,128)S(1)}, u32[]{:S(2)}, u32[]{:S(2)}) collective-permute-start(f32[128,512]{1,0:T(8,128)S(1)} %get-tuple-element.126), channel_id=1, source_target_pairs={{11,2},{14,7},{18,11},{23,14},{27,18},{30,23},{34,27},{39,30},{43,... | collective-permute-start | bytes 786440 | tf_op jit(solution)/shard_map/ppermute | solution.py:207
  33.9 56.2 %all-to-all-start = ((f32[8,16,512]{2,1,0:T(8,128)}), f32[8,16,512]{2,1,0:T(8,128)S(1)}, u32[]{:S(2)}, u32[]{:S(2)}) async-start(f32[8,16,512]{2,1,0:T(8,128)} %bitcast.2), calls=%async_computation | async-start | bytes 524288 | tf_op jit(solution)/shard_map/all_to_all | solution.py:246
  85.2 14.3 %collective-permute-start.13 = (f32[256,512]{1,0:T(8,128)}, f32[256,512]{1,0:T(8,128)S(1)}, u32[]{:S(2)}, u32[]{:S(2)}) collective-permute-start(f32[256,512]{1,0:T(8,128)} %get-tuple-element.161), channel_id=1, source_target_pairs={{2,0},{7,5},{11,9},{14,12},{18,16},{23,21},{27,25},{30,28},{34,32}... | collective-permute-start | bytes 1572872 | tf_op jit(solution)/shard_map/ppermute | solution.py:198
  85.9 13.6 %collective-permute-start.14 = (f32[256,512]{1,0:T(8,128)S(1)}, f32[256,512]{1,0:T(8,128)S(1)}, u32[]{:S(2)}, u32[]{:S(2)}) collective-permute-start(f32[256,512]{1,0:T(8,128)S(1)} %get-tuple-element.162), channel_id=1, source_target_pairs={{2,4},{7,1},{11,13},{14,8},{18,20},{23,17},{27,29},{30,24},{34,36}... | collective-permute-start | bytes 1572872 | tf_op jit(solution)/shard_map/ppermute | solution.py:198
  86.6 13.0 %collective-permute-start.15 = (f32[256,512]{1,0:T(8,128)S(1)}, f32[256,512]{1,0:T(8,128)S(1)}, u32[]{:S(2)}, u32[]{:S(2)}) collective-permute-start(f32[256,512]{1,0:T(8,128)S(1)} %get-tuple-element.163), channel_id=1, source_target_pairs={{2,3},{7,6},{11,10},{14,15},{18,19},{23,22},{27,26},{30,31},{34,35... | collective-permute-start | bytes 1572872 | tf_op jit(solution)/shard_map/ppermute | solution.py:198
  90.1 9.4 %collective-permute-start.12 = (f32[16,512]{1,0:T(8,128)S(1)}, f32[16,512]{1,0:T(8,128)S(1)}, u32[]{:S(2)}, u32[]{:S(2)}) collective-permute-start(f32[16,512]{1,0:T(8,128)S(1)} %share.1), channel_id=1, source_target_pairs={{8,0},{16,8},{24,16},{32,24},{40,32},{48,40},{56,48},{64,56},{72,6... | collective-permute-start | bytes 98312 | tf_op jit(solution)/shard_map/ppermute | solution.py:248

commit v8 on v7

--- a/solution.py
+++ b/solution.py
@@ -73,7 +73,7 @@
     return jnp.where((lax.axis_index("split") ^ parity()) == FIRST, DECAY, 0.0)
 
 
-def first_kernel(user_hbm, held_hbm, items_hbm, conf_hbm, part_hbm, pack_hbm, user_ref, held_ref, items, conf, part, pack, sems):
+def first_kernel(user_hbm, held_hbm, items_hbm, conf_hbm, part, pack, user_ref, held_ref, items, conf, sems):
     users = user_ref.shape[0]
     slab = held_ref.shape[0]
     steps, obs, _ = items.shape
@@ -95,13 +95,7 @@
     user = halves(user_ref[...])
     errors = halves(weights * product(held_halves, user, NT) - targets)
     part[...] = kept() * held - LEARN_RATE * product(errors, user, NN)
-    send_part = pltpu.make_async_copy(part, part_hbm, sems.at[4])
-    send_part.start()
     pack[:users, :] = DECAY * user_ref[...] - LEARN_RATE * product(errors, held_halves, TN)
-    send_pack = pltpu.make_async_copy(pack, pack_hbm, sems.at[5])
-    send_pack.start()
-    send_part.wait()
-    send_pack.wait()
 
 
 def sum_kernel(*refs):
@@ -204,7 +198,7 @@
                 source = at((b + 1) % blocks, w)
                 same.append((source, at(b, w)))
                 cross.append((source, at(b, v)))
-        return [lax.ppermute(x, both, same), lax.ppermute(x, both, cross)]
+        return [lax.ppermute(x, both, cross), lax.ppermute(x, both, same)]
 
     f32, bf16 = jnp.float32, jnp.bfloat16
     early = pl.CostEstimate(flops=1 << 36, bytes_accessed=1 << 20, transcendentals=0)
@@ -214,13 +208,11 @@
         first_kernel,
         [((slab, rank), f32), ((rows, rank), f32)],
         "first",
-        params=None,
         in_specs=[hbm] * 4,
-        out_specs=[hbm] * 2,
         scratch_shapes=[pltpu.VMEM(user_factors.shape, f32), pltpu.VMEM(item_factors.shape, f32)]
         + [pltpu.VMEM(items.shape, jnp.int32)] * 2
-        + [pltpu.VMEM((slab, rank), f32), pltpu.VMEM((rows, rank), f32), pltpu.SemaphoreType.DMA((6,))],
-    )(user_factors, item_factors, items, conf)
+        + [pltpu.SemaphoreType.DMA((4,))],
+    )(*[pltpu.with_memory_space_constraint(x, pltpu.HBM) for x in (user_factors, item_factors, items, conf)])
     arrived = [part] + [fetch(part, helpers) for helpers in HELPERS]
     packs = [pack] + [fetch(pack, helpers) for helpers in HELPERS]
     (out,) = call(sum_kernel, [((slab, rank), f32)], "sum", cost_estimate=early)(*arrived)

time: 101 us -> 99.1 us (0.981)
  starting transfers between devices: 74.7 us -> 72.6 us
  waiting for transfers between devices: 7.76 us -> 9.83 us
    ppermute x1, starting transfers between devices: 7.77 us -> 5.98 us  [local(): lax.ppermute(share, 'blk', [((b + 1) % blocks, b) for b in range(blocks)])]
    ppermute x3, waiting for transfers between devices: 0.1 us -> 1.54 us  [give(): return lax.ppermute(x, both, pairs)]
  transfers between devices with their start and end apart: 17 -> 17, of which waited for: 4 -> 4; matrix products, arithmetic and copies ran while one was open for 0% -> 0% of each run, Pallas kernels for 4% -> 5%
where the time goes in v8:
time: 99.1 us; the launch traced here: 98.5 us
  starting transfers between devices  72.6 us (73%)
  Pallas kernels  15.2 us (15%)
  waiting for transfers between devices  9.83 us (10%)
    all_to_all x1, starting transfers between devices, local(): parts = lax.all_to_all(out.reshape(n, share_rows, rank), 'split', 0, 0)  51.1 us
    ppermute x6, starting transfers between devices, fetch(): return lax.ppermute(x, both, pairs)  8.79 us
    ppermute x1, starting transfers between devices, local(): lax.ppermute(share, 'blk', [((b + 1) % blocks, b) for b in range(blocks)])  5.98 us
    ppermute x6, waiting for transfers between devices, fetch(): return lax.ppermute(x, both, pairs)  4.49 us
    ppermute x6, starting transfers between devices, onward(): return [lax.ppermute(x, both, cross), lax.ppermute(x, both, same)]  4.06 us
    pallas_call x2, Pallas kernels, local(): out, *errors = call(kernel, outs, 'group')(*held, *ahead)  4.02 us
    pallas_call x1, Pallas kernels, local(): call(kernel, [((slab, rank), f32)] + [factors] * chunks, 'last')  3.51 us
    pallas_call x2, Pallas kernels, local(): call(kernel, [factors, *ready] * chunks, 'users')  3.43 us
  transfers between devices with their start and end apart: 17, of which 4 were waited for; matrix products, arithmetic and copies ran while one was open for 0% of the time, Pallas kernels for 5%

profile of v8, /device:TPU:6, one launch (start us, length us, event | category | flops | bytes accessed | tf_op | source)
XLA Modules:
  0.0 98.5 jit_solution(6330321482465595525)
XLA Ops:
  0.6 2.4 %first.1 = (f32[128,512]{1,0:T(8,128)S(1)}, f32[288,512]{1,0:T(8,128)S(1)}) custom-call(f32[256,512]{1,0:T(8,128)} %user_hbm.1, f32[128,512]{1,0:T(8,128)} %held_hbm.1, s32[4,8,256]{2,1,0:T(8,128)} %bitcast.3, s32[4,8,256]{2,1,0:T(8,128)} %bitcast.4), custom_call_target="tpu_custom_call" | custom-call | tf_op jit(solution)/shard_map/first/pallas_call | solution.py:207
  3.0 3.5 %collective-permute-start.2 = (f32[128,512]{1,0:T(8,128)S(1)}, f32[128,512]{1,0:T(8,128)S(1)}, u32[]{:S(2)}, u32[]{:S(2)}) collective-permute-start(f32[128,512]{1,0:T(8,128)S(1)} %get-tuple-element.83.refs_0_), channel_id=1, source_target_pairs={{3,2},{6,7},{10,11},{15,14},{19,18},{22,23},{26,27},{31,30},{35,34... | collective-permute-start | bytes 786440 | tf_op jit(solution)/shard_map/ppermute | solution.py:188
  7.9 2.5 %collective-permute-start.7 = (f32[288,512]{1,0:T(8,128)S(1)}, f32[288,512]{1,0:T(8,128)S(1)}, u32[]{:S(2)}, u32[]{:S(2)}) collective-permute-start(f32[288,512]{1,0:T(8,128)S(1)} %get-tuple-element.84.refs_0_.refs_10_.refs_14_), channel_id=1, source_target_pairs={{3,2},{6,7},{10,11},{15,14},{19,18},{22,23},{26,27},{31,30},{35,34... | collective-permute-start | bytes 1769480 | tf_op jit(solution)/shard_map/ppermute | solution.py:188
  10.4 0.7 collective-permute-start.6
  11.2 0.7 collective-permute-start.5
  11.9 0.7 collective-permute-start.4
  12.6 0.7 collective-permute-start.3
  13.3 4.5 %collective-permute-done.7.refs_3_.refs_13_.refs_17_ = f32[288,512]{1,0:T(8,128)S(1)} collective-permute-done((f32[288,512]{1,0:T(8,128)S(1)}, f32[288,512]{1,0:T(8,128)S(1)}, u32[]{:S(2)}, u32[]{:S(2)}) %collective-permute-start.7) | collective-permute-done | bytes 589856 | tf_op jit(solution)/shard_map/ppermute | solution.py:188
  17.8 1.0 prepare.1
  18.8 2.0 %group.2 = (f32[128,512]{1,0:T(8,128)S(1)}, bf16[128,256]{1,0:T(8,128)(2,1)S(1)}, bf16[128,256]{1,0:T(8,128)(2,1)S(1)}, bf16[128,256]{1,0:T(8,128)(2,1)S(1)}, bf...) custom-call(f32[128,512]{1,0:T(8,128)S(1)} %collective-permute-done., ...), custom_call_target="tpu_custom_call" | custom-call | tf_op jit(solution)/shard_map/group/pallas_call | solution.py:229
  21.5 0.7 collective-permute-start.8
  22.2 1.7 %users.2 = (f32[256,512]{1,0:T(8,128)S(1)}, bf16[256,512]{1,0:T(8,128)(2,1)S(1)}, bf16[256,512]{1,0:T(8,128)(2,1)S(1)}, f32[128,256]{1,0:T(8,128)S(1)}, f32[128,...) custom-call(f32[128,512]{1,0:T(8,128)S(1)} %collective-permute-done., ...), custom_call_target="tpu_custom_call" | custom-call | tf_op jit(solution)/shard_map/users/pallas_call | solution.py:232
  23.9 2.0 %group.3 = (f32[128,512]{1,0:T(8,128)S(1)}, bf16[128,256]{1,0:T(8,128)(2,1)S(1)}, bf16[128,256]{1,0:T(8,128)(2,1)S(1)}, bf16[128,256]{1,0:T(8,128)(2,1)S(1)}, bf...) custom-call(f32[128,512]{1,0:T(8,128)S(1)} %collective-permute-done., ...), custom_call_target="tpu_custom_call" | custom-call | tf_op jit(solution)/shard_map/group/pallas_call | solution.py:229
  27.3 1.7 %users.3 = (f32[256,512]{1,0:T(8,128)S(1)}, bf16[256,512]{1,0:T(8,128)(2,1)S(1)}, bf16[256,512]{1,0:T(8,128)(2,1)S(1)}, f32[128,256]{1,0:T(8,128)S(1)}, f32[128,...) custom-call(f32[128,512]{1,0:T(8,128)S(1)} %collective-permute-done., ...), custom_call_target="tpu_custom_call" | custom-call | tf_op jit(solution)/shard_map/users/pallas_call | solution.py:232
  29.1 3.5 %last.1 = (f32[128,512]{1,0:T(8,128)}, f32[256,512]{1,0:T(8,128)S(1)}, f32[256,512]{1,0:T(8,128)}, f32[256,512]{1,0:T(8,128)S(1)}, f32[256,512]{1,0:T(8,128)S(1)}) custom-call(f32[128,512]{1,0:T(8,128)S(1)} %collective-permute-done.10.refs_0_, f32[128,512]{1,0:T(8,128)S(1)} %collective-permute-done.11.refs_1_, ...), custom_call_target="tpu_custom_call" | custom-call | tf_op jit(solution)/shard_map/last/pallas_call | solution.py:237
  32.6 51.1 %all-to-all-start = ((f32[8,16,512]{2,1,0:T(8,128)}), f32[8,16,512]{2,1,0:T(8,128)S(1)}, u32[]{:S(2)}, u32[]{:S(2)}) async-start(f32[8,16,512]{2,1,0:T(8,128)} %bitcast.2), calls=%async_computation | async-start | bytes 524288 | tf_op jit(solution)/shard_map/all_to_all | solution.py:238
  83.7 0.7 collective-permute-start.13
  84.4 0.7 collective-permute-start.14
  85.1 1.3 %collective-permute-start.15 = (f32[256,512]{1,0:T(8,128)S(1)}, f32[256,512]{1,0:T(8,128)S(1)}, u32[]{:S(2)}, u32[]{:S(2)}) collective-permute-start(f32[256,512]{1,0:T(8,128)S(1)} %get-tuple-element.163), channel_id=1, source_target_pairs={{2,3},{7,6},{11,10},{14,15},{18,19},{23,22},{27,26},{30,31},{34,35... | collective-permute-start | bytes 1572872 | tf_op jit(solution)/shard_map/ppermute | solution.py:192
  86.4 2.2 %all-to-all-done.parts_ref = f32[8,16,512]{2,1,0:T(8,128)S(1)} async-done(((f32[8,16,512]{2,1,0:T(8,128)}), f32[8,16,512]{2,1,0:T(8,128)S(1)}, u32[]{:S(2)}, u32[]{:S(2)}) %all-to-all-start) | async-done | bytes 262176 | tf_op jit(solution)/shard_map/all_to_all | solution.py:238
  88.6 6.0 %collective-permute-start.12 = (f32[16,512]{1,0:T(8,128)S(1)}, f32[16,512]{1,0:T(8,128)S(1)}, u32[]{:S(2)}, u32[]{:S(2)}) collective-permute-start(f32[16,512]{1,0:T(8,128)S(1)} %share.1), channel_id=1, source_target_pairs={{8,0},{16,8},{24,16},{32,24},{40,32},{48,40},{56,48},{64,56},{72,6... | collective-permute-start | bytes 98312 | tf_op jit(solution)/shard_map/ppermute | solution.py:240
  94.6 1.6 %collective-permute-done.12.share_ref = f32[16,512]{1,0:T(8,128)S(1)} collective-permute-done((f32[16,512]{1,0:T(8,128)S(1)}, f32[16,512]{1,0:T(8,128)S(1)}, u32[]{:S(2)}, u32[]{:S(2)}) %collective-permute-start.12) | collective-permute-done | bytes 32800 | tf_op jit(solution)/shard_map/ppermute | solution.py:240
  96.2 1.5 %collective-permute-done.15.c_ref = f32[256,512]{1,0:T(8,128)S(1)} collective-permute-done((f32[256,512]{1,0:T(8,128)S(1)}, f32[256,512]{1,0:T(8,128)S(1)}, u32[]{:S(2)}, u32[]{:S(2)}) %collective-permute-start.15) | collective-permute-done | bytes 524320 | tf_op jit(solution)/shard_map/ppermute | solution.py:192
  97.7 0.8 home.1
  (20 shorter events, 3.5 us)
Async XLA Ops:
  3.0 8.1 %collective-permute-start.2 = (f32[128,512]{1,0:T(8,128)S(1)}, f32[128,512]{1,0:T(8,128)S(1)}, u32[]{:S(2)}, u32[]{:S(2)}) collective-permute-start(f32[128,512]{1,0:T(8,128)S(1)} %get-tuple-element.83.refs_0_), channel_id=1, source_target_pairs={{3,2},{6,7},{10,11},{15,14},{19,18},{22,23},{26,27},{31,30},{35,34... | collective-permute-start | bytes 786440 | tf_op jit(solution)/shard_map/ppermute | solution.py:188
  6.5 5.3 %collective-permute-start.1 = (f32[128,512]{1,0:T(8,128)S(1)}, f32[128,512]{1,0:T(8,128)S(1)}, u32[]{:S(2)}, u32[]{:S(2)}) collective-permute-start(f32[128,512]{1,0:T(8,128)S(1)} %get-tuple-element.83.refs_0_), channel_id=1, source_target_pairs={{4,2},{1,7},{13,11},{8,14},{20,18},{17,23},{29,27},{24,30},{36,34}... | collective-permute-start | bytes 786440 | tf_op jit(solution)/shard_map/ppermute | solution.py:188
  7.2 4.7 %collective-permute-start = (f32[128,512]{1,0:T(8,128)S(1)}, f32[128,512]{1,0:T(8,128)S(1)}, u32[]{:S(2)}, u32[]{:S(2)}) collective-permute-start(f32[128,512]{1,0:T(8,128)S(1)} %get-tuple-element.83.refs_0_), channel_id=1, source_target_pairs={{0,2},{5,7},{9,11},{12,14},{16,18},{21,23},{25,27},{28,30},{32,34}... | collective-permute-start | bytes 786440 | tf_op jit(solution)/shard_map/ppermute | solution.py:188
  7.9 9.9 %collective-permute-start.7 = (f32[288,512]{1,0:T(8,128)S(1)}, f32[288,512]{1,0:T(8,128)S(1)}, u32[]{:S(2)}, u32[]{:S(2)}) collective-permute-start(f32[288,512]{1,0:T(8,128)S(1)} %get-tuple-element.84.refs_0_.refs_10_.refs_14_), channel_id=1, source_target_pairs={{3,2},{6,7},{10,11},{15,14},{19,18},{22,23},{26,27},{31,30},{35,34... | collective-permute-start | bytes 1769480 | tf_op jit(solution)/shard_map/ppermute | solution.py:188
  10.4 7.3 %collective-permute-start.6 = (f32[288,512]{1,0:T(8,128)S(1)}, f32[288,512]{1,0:T(8,128)S(1)}, u32[]{:S(2)}, u32[]{:S(2)}) collective-permute-start(f32[288,512]{1,0:T(8,128)S(1)} %get-tuple-element.84.refs_0_.refs_10_.refs_14_), channel_id=1, source_target_pairs={{4,2},{1,7},{13,11},{8,14},{20,18},{17,23},{29,27},{24,30},{36,34}... | collective-permute-start | bytes 1769480 | tf_op jit(solution)/shard_map/ppermute | solution.py:188
  11.2 6.6 %collective-permute-start.5 = (f32[288,512]{1,0:T(8,128)S(1)}, f32[288,512]{1,0:T(8,128)S(1)}, u32[]{:S(2)}, u32[]{:S(2)}) collective-permute-start(f32[288,512]{1,0:T(8,128)S(1)} %get-tuple-element.84.refs_0_.refs_10_.refs_14_), channel_id=1, source_target_pairs={{0,2},{5,7},{9,11},{12,14},{16,18},{21,23},{25,27},{28,30},{32,34}... | collective-permute-start | bytes 1769480 | tf_op jit(solution)/shard_map/ppermute | solution.py:188
  11.9 6.8 %collective-permute-start.4 = (f32[128,512]{1,0:T(8,128)S(1)}, f32[128,512]{1,0:T(8,128)S(1)}, u32[]{:S(2)}, u32[]{:S(2)}) collective-permute-start(f32[128,512]{1,0:T(8,128)S(1)} %sum.1), channel_id=1, source_target_pairs={{11,2},{14,7},{18,11},{23,14},{27,18},{30,23},{34,27},{39,30},{43,... | collective-permute-start | bytes 786440 | tf_op jit(solution)/shard_map/ppermute | solution.py:201
  12.6 6.2 %collective-permute-start.3 = (f32[128,512]{1,0:T(8,128)S(1)}, f32[128,512]{1,0:T(8,128)S(1)}, u32[]{:S(2)}, u32[]{:S(2)}) collective-permute-start(f32[128,512]{1,0:T(8,128)S(1)} %sum.1), channel_id=1, source_target_pairs={{11,7},{14,2},{18,14},{23,11},{27,23},{30,18},{34,30},{39,27},{43,... | collective-permute-start | bytes 786440 | tf_op jit(solution)/shard_map/ppermute | solution.py:201
  20.8 3.1 %collective-permute-start.9 = (f32[128,512]{1,0:T(8,128)S(1)}, f32[128,512]{1,0:T(8,128)S(1)}, u32[]{:S(2)}, u32[]{:S(2)}) collective-permute-start(f32[128,512]{1,0:T(8,128)S(1)} %get-tuple-element.101), channel_id=1, source_target_pairs={{11,2},{14,7},{18,11},{23,14},{27,18},{30,23},{34,27},{39,30},{43,... | collective-permute-start | bytes 786440 | tf_op jit(solution)/shard_map/ppermute | solution.py:201
  21.5 2.4 %collective-permute-start.8 = (f32[128,512]{1,0:T(8,128)S(1)}, f32[128,512]{1,0:T(8,128)S(1)}, u32[]{:S(2)}, u32[]{:S(2)}) collective-permute-start(f32[128,512]{1,0:T(8,128)S(1)} %get-tuple-element.101), channel_id=1, source_target_pairs={{11,7},{14,2},{18,14},{23,11},{27,23},{30,18},{34,30},{39,27},{43,... | collective-permute-start | bytes 786440 | tf_op jit(solution)/shard_map/ppermute | solution.py:201
  25.9 3.1 %collective-permute-start.11 = (f32[128,512]{1,0:T(8,128)S(1)}, f32[128,512]{1,0:T(8,128)S(1)}, u32[]{:S(2)}, u32[]{:S(2)}) collective-permute-start(f32[128,512]{1,0:T(8,128)S(1)} %get-tuple-element.126), channel_id=1, source_target_pairs={{11,2},{14,7},{18,11},{23,14},{27,18},{30,23},{34,27},{39,30},{43,... | collective-permute-start | bytes 786440 | tf_op jit(solution)/shard_map/ppermute | solution.py:201
  26.6 2.4 %collective-permute-start.10 = (f32[128,512]{1,0:T(8,128)S(1)}, f32[128,512]{1,0:T(8,128)S(1)}, u32[]{:S(2)}, u32[]{:S(2)}) collective-permute-start(f32[128,512]{1,0:T(8,128)S(1)} %get-tuple-element.126), channel_id=1, source_target_pairs={{11,7},{14,2},{18,14},{23,11},{27,23},{30,18},{34,30},{39,27},{43,... | collective-permute-start | bytes 786440 | tf_op jit(solution)/shard_map/ppermute | solution.py:201
  32.6 56.0 %all-to-all-start = ((f32[8,16,512]{2,1,0:T(8,128)}), f32[8,16,512]{2,1,0:T(8,128)S(1)}, u32[]{:S(2)}, u32[]{:S(2)}) async-start(f32[8,16,512]{2,1,0:T(8,128)} %bitcast.2), calls=%async_computation | async-start | bytes 524288 | tf_op jit(solution)/shard_map/all_to_all | solution.py:238
  83.7 12.5 %collective-permute-start.13 = (f32[256,512]{1,0:T(8,128)}, f32[256,512]{1,0:T(8,128)S(1)}, u32[]{:S(2)}, u32[]{:S(2)}) collective-permute-start(f32[256,512]{1,0:T(8,128)} %get-tuple-element.161), channel_id=1, source_target_pairs={{2,0},{7,5},{11,9},{14,12},{18,16},{23,21},{27,25},{30,28},{34,32}... | collective-permute-start | bytes 1572872 | tf_op jit(solution)/shard_map/ppermute | solution.py:192
  84.4 11.8 %collective-permute-start.14 = (f32[256,512]{1,0:T(8,128)S(1)}, f32[256,512]{1,0:T(8,128)S(1)}, u32[]{:S(2)}, u32[]{:S(2)}) collective-permute-start(f32[256,512]{1,0:T(8,128)S(1)} %get-tuple-element.162), channel_id=1, source_target_pairs={{2,4},{7,1},{11,13},{14,8},{18,20},{23,17},{27,29},{30,24},{34,36}... | collective-permute-start | bytes 1572872 | tf_op jit(solution)/shard_map/ppermute | solution.py:192
  85.1 12.6 %collective-permute-start.15 = (f32[256,512]{1,0:T(8,128)S(1)}, f32[256,512]{1,0:T(8,128)S(1)}, u32[]{:S(2)}, u32[]{:S(2)}) collective-permute-start(f32[256,512]{1,0:T(8,128)S(1)} %get-tuple-element.163), channel_id=1, source_target_pairs={{2,3},{7,6},{11,10},{14,15},{18,19},{23,22},{27,26},{30,31},{34,35... | collective-permute-start | bytes 1572872 | tf_op jit(solution)/shard_map/ppermute | solution.py:192
  88.6 7.6 %collective-permute-start.12 = (f32[16,512]{1,0:T(8,128)S(1)}, f32[16,512]{1,0:T(8,128)S(1)}, u32[]{:S(2)}, u32[]{:S(2)}) collective-permute-start(f32[16,512]{1,0:T(8,128)S(1)} %share.1), channel_id=1, source_target_pairs={{8,0},{16,8},{24,16},{32,24},{40,32},{48,40},{56,48},{64,56},{72,6... | collective-permute-start | bytes 98312 | tf_op jit(solution)/shard_map/ppermute | solution.py:240

commit v9 on v8

--- a/solution.py
+++ b/solution.py
@@ -31,7 +31,11 @@
     def one(p, q):
         return lax.dot_general(p, q, dims, preferred_element_type=jnp.float32)
 
-    return one(a[0], b[0]) + (one(a[0], b[1]) + one(a[1], b[0]))
+    if dims == TN:
+        return one(a[0], b[0]) + (one(a[0], b[1]) + one(a[1], b[0]))
+    rows = a[0].shape[0]
+    stacked = one(jnp.concatenate(a, axis=0), b[0])
+    return stacked[:rows] + (stacked[rows:] + one(a[0], b[1]))
 
 
 def weigh(items, conf, slab):

time: 99.1 us -> 98.3 us (level)
  no operation moved by 1% of the time
where the time goes in v9:
time: 98.3 us; the launch traced here: 97.7 us
  starting transfers between devices  72.6 us (74%)
  Pallas kernels  14.4 us (15%)
  waiting for transfers between devices  9.83 us (10%)
    all_to_all x1, starting transfers between devices, local(): parts = lax.all_to_all(out.reshape(n, share_rows, rank), 'split', 0, 0)  51.1 us
    ppermute x6, starting transfers between devices, fetch(): return lax.ppermute(x, both, pairs)  8.79 us
    ppermute x1, starting transfers between devices, local(): lax.ppermute(share, 'blk', [((b + 1) % blocks, b) for b in range(blocks)])  5.98 us
    ppermute x6, waiting for transfers between devices, fetch(): return lax.ppermute(x, both, pairs)  4.49 us
    ppermute x6, starting transfers between devices, onward(): return [lax.ppermute(x, both, cross), lax.ppermute(x, both, same)]  4.06 us
    pallas_call x1, Pallas kernels, local(): call(kernel, [((slab, rank), f32)] + [factors] * chunks, 'last')  3.78 us
    pallas_call x2, Pallas kernels, local(): call(kernel, [factors, *ready] * chunks, 'users')  3.44 us
    pallas_call x2, Pallas kernels, local(): out, *errors = call(kernel, outs, 'group')(*held, *ahead)  3.17 us
  transfers between devices with their start and end apart: 17, of which 4 were waited for; matrix products, arithmetic and copies ran while one was open for 0% of the time, Pallas kernels for 5%

profile of v9, /device:TPU:6, one launch (start us, length us, event | category | flops | bytes accessed | tf_op | source)
XLA Modules:
  0.0 97.7 jit_solution(3774322534950325690)
XLA Ops:
  0.6 2.2 %first.1 = (f32[128,512]{1,0:T(8,128)S(1)}, f32[288,512]{1,0:T(8,128)S(1)}) custom-call(f32[256,512]{1,0:T(8,128)} %user_hbm.1, f32[128,512]{1,0:T(8,128)} %held_hbm.1, s32[4,8,256]{2,1,0:T(8,128)} %bitcast.3, s32[4,8,256]{2,1,0:T(8,128)} %bitcast.4), custom_call_target="tpu_custom_call" | custom-call | tf_op jit(solution)/shard_map/first/pallas_call | solution.py:211
  2.8 3.5 %collective-permute-start.2 = (f32[128,512]{1,0:T(8,128)S(1)}, f32[128,512]{1,0:T(8,128)S(1)}, u32[]{:S(2)}, u32[]{:S(2)}) collective-permute-start(f32[128,512]{1,0:T(8,128)S(1)} %get-tuple-element.83.refs_0_), channel_id=1, source_target_pairs={{3,2},{6,7},{10,11},{15,14},{19,18},{22,23},{26,27},{31,30},{35,34... | collective-permute-start | bytes 786440 | tf_op jit(solution)/shard_map/ppermute | solution.py:192
  7.7 2.5 %collective-permute-start.7 = (f32[288,512]{1,0:T(8,128)S(1)}, f32[288,512]{1,0:T(8,128)S(1)}, u32[]{:S(2)}, u32[]{:S(2)}) collective-permute-start(f32[288,512]{1,0:T(8,128)S(1)} %get-tuple-element.84.refs_0_.refs_10_.refs_14_), channel_id=1, source_target_pairs={{3,2},{6,7},{10,11},{15,14},{19,18},{22,23},{26,27},{31,30},{35,34... | collective-permute-start | bytes 1769480 | tf_op jit(solution)/shard_map/ppermute | solution.py:192
  10.2 0.7 collective-permute-start.6
  10.9 0.7 collective-permute-start.5
  11.7 0.7 collective-permute-start.4
  12.4 0.7 collective-permute-start.3
  13.1 4.5 %collective-permute-done.7.refs_3_.refs_13_.refs_17_ = f32[288,512]{1,0:T(8,128)S(1)} collective-permute-done((f32[288,512]{1,0:T(8,128)S(1)}, f32[288,512]{1,0:T(8,128)S(1)}, u32[]{:S(2)}, u32[]{:S(2)}) %collective-permute-start.7) | collective-permute-done | bytes 589856 | tf_op jit(solution)/shard_map/ppermute | solution.py:192
  17.6 1.0 prepare.1
  18.6 1.6 %group.2 = (f32[128,512]{1,0:T(8,128)S(1)}, bf16[128,256]{1,0:T(8,128)(2,1)S(1)}, bf16[128,256]{1,0:T(8,128)(2,1)S(1)}, bf16[128,256]{1,0:T(8,128)(2,1)S(1)}, bf...) custom-call(f32[128,512]{1,0:T(8,128)S(1)} %collective-permute-done., ...), custom_call_target="tpu_custom_call" | custom-call | tf_op jit(solution)/shard_map/group/pallas_call | solution.py:233
  21.5 1.7 %users.2 = (f32[256,512]{1,0:T(8,128)S(1)}, bf16[256,512]{1,0:T(8,128)(2,1)S(1)}, bf16[256,512]{1,0:T(8,128)(2,1)S(1)}, f32[128,256]{1,0:T(8,128)S(1)}, f32[128,...) custom-call(f32[128,512]{1,0:T(8,128)S(1)} %collective-permute-done., ...), custom_call_target="tpu_custom_call" | custom-call | tf_op jit(solution)/shard_map/users/pallas_call | solution.py:236
  23.3 1.6 %group.3 = (f32[128,512]{1,0:T(8,128)S(1)}, bf16[128,256]{1,0:T(8,128)(2,1)S(1)}, bf16[128,256]{1,0:T(8,128)(2,1)S(1)}, bf16[128,256]{1,0:T(8,128)(2,1)S(1)}, bf...) custom-call(f32[128,512]{1,0:T(8,128)S(1)} %collective-permute-done., ...), custom_call_target="tpu_custom_call" | custom-call | tf_op jit(solution)/shard_map/group/pallas_call | solution.py:233
  24.9 0.7 collective-permute-start.11
  26.2 1.7 %users.3 = (f32[256,512]{1,0:T(8,128)S(1)}, bf16[256,512]{1,0:T(8,128)(2,1)S(1)}, bf16[256,512]{1,0:T(8,128)(2,1)S(1)}, f32[128,256]{1,0:T(8,128)S(1)}, f32[128,...) custom-call(f32[128,512]{1,0:T(8,128)S(1)} %collective-permute-done., ...), custom_call_target="tpu_custom_call" | custom-call | tf_op jit(solution)/shard_map/users/pallas_call | solution.py:236
  28.0 3.8 %last.1 = (f32[128,512]{1,0:T(8,128)}, f32[256,512]{1,0:T(8,128)S(1)}, f32[256,512]{1,0:T(8,128)}, f32[256,512]{1,0:T(8,128)S(1)}, f32[256,512]{1,0:T(8,128)S(1)}) custom-call(f32[128,512]{1,0:T(8,128)S(1)} %collective-permute-done.10.refs_0_, f32[128,512]{1,0:T(8,128)S(1)} %collective-permute-done.11.refs_1_, ...), custom_call_target="tpu_custom_call" | custom-call | tf_op jit(solution)/shard_map/last/pallas_call | solution.py:241
  31.8 51.1 %all-to-all-start = ((f32[8,16,512]{2,1,0:T(8,128)}), f32[8,16,512]{2,1,0:T(8,128)S(1)}, u32[]{:S(2)}, u32[]{:S(2)}) async-start(f32[8,16,512]{2,1,0:T(8,128)} %bitcast.2), calls=%async_computation | async-start | bytes 524288 | tf_op jit(solution)/shard_map/all_to_all | solution.py:242
  82.9 0.7 collective-permute-start.13
  83.6 0.7 collective-permute-start.14
  84.3 1.3 %collective-permute-start.15 = (f32[256,512]{1,0:T(8,128)S(1)}, f32[256,512]{1,0:T(8,128)S(1)}, u32[]{:S(2)}, u32[]{:S(2)}) collective-permute-start(f32[256,512]{1,0:T(8,128)S(1)} %get-tuple-element.163), channel_id=1, source_target_pairs={{2,3},{7,6},{11,10},{14,15},{18,19},{23,22},{27,26},{30,31},{34,35... | collective-permute-start | bytes 1572872 | tf_op jit(solution)/shard_map/ppermute | solution.py:196
  85.6 2.2 %all-to-all-done.parts_ref = f32[8,16,512]{2,1,0:T(8,128)S(1)} async-done(((f32[8,16,512]{2,1,0:T(8,128)}), f32[8,16,512]{2,1,0:T(8,128)S(1)}, u32[]{:S(2)}, u32[]{:S(2)}) %all-to-all-start) | async-done | bytes 262176 | tf_op jit(solution)/shard_map/all_to_all | solution.py:242
  87.8 6.0 %collective-permute-start.12 = (f32[16,512]{1,0:T(8,128)S(1)}, f32[16,512]{1,0:T(8,128)S(1)}, u32[]{:S(2)}, u32[]{:S(2)}) collective-permute-start(f32[16,512]{1,0:T(8,128)S(1)} %share.1), channel_id=1, source_target_pairs={{8,0},{16,8},{24,16},{32,24},{40,32},{48,40},{56,48},{64,56},{72,6... | collective-permute-start | bytes 98312 | tf_op jit(solution)/shard_map/ppermute | solution.py:244
  93.8 1.6 %collective-permute-done.12.share_ref = f32[16,512]{1,0:T(8,128)S(1)} collective-permute-done((f32[16,512]{1,0:T(8,128)S(1)}, f32[16,512]{1,0:T(8,128)S(1)}, u32[]{:S(2)}, u32[]{:S(2)}) %collective-permute-start.12) | collective-permute-done | bytes 32800 | tf_op jit(solution)/shard_map/ppermute | solution.py:244
  95.4 1.5 %collective-permute-done.15.c_ref = f32[256,512]{1,0:T(8,128)S(1)} collective-permute-done((f32[256,512]{1,0:T(8,128)S(1)}, f32[256,512]{1,0:T(8,128)S(1)}, u32[]{:S(2)}, u32[]{:S(2)}) %collective-permute-start.15) | collective-permute-done | bytes 524320 | tf_op jit(solution)/shard_map/ppermute | solution.py:196
  96.9 0.8 home.1
  (20 shorter events, 3.5 us)
Async XLA Ops:
  2.8 8.1 %collective-permute-start.2 = (f32[128,512]{1,0:T(8,128)S(1)}, f32[128,512]{1,0:T(8,128)S(1)}, u32[]{:S(2)}, u32[]{:S(2)}) collective-permute-start(f32[128,512]{1,0:T(8,128)S(1)} %get-tuple-element.83.refs_0_), channel_id=1, source_target_pairs={{3,2},{6,7},{10,11},{15,14},{19,18},{22,23},{26,27},{31,30},{35,34... | collective-permute-start | bytes 786440 | tf_op jit(solution)/shard_map/ppermute | solution.py:192
  6.3 5.3 %collective-permute-start.1 = (f32[128,512]{1,0:T(8,128)S(1)}, f32[128,512]{1,0:T(8,128)S(1)}, u32[]{:S(2)}, u32[]{:S(2)}) collective-permute-start(f32[128,512]{1,0:T(8,128)S(1)} %get-tuple-element.83.refs_0_), channel_id=1, source_target_pairs={{4,2},{1,7},{13,11},{8,14},{20,18},{17,23},{29,27},{24,30},{36,34}... | collective-permute-start | bytes 786440 | tf_op jit(solution)/shard_map/ppermute | solution.py:192
  7.0 4.7 %collective-permute-start = (f32[128,512]{1,0:T(8,128)S(1)}, f32[128,512]{1,0:T(8,128)S(1)}, u32[]{:S(2)}, u32[]{:S(2)}) collective-permute-start(f32[128,512]{1,0:T(8,128)S(1)} %get-tuple-element.83.refs_0_), channel_id=1, source_target_pairs={{0,2},{5,7},{9,11},{12,14},{16,18},{21,23},{25,27},{28,30},{32,34}... | collective-permute-start | bytes 786440 | tf_op jit(solution)/shard_map/ppermute | solution.py:192
  7.7 9.9 %collective-permute-start.7 = (f32[288,512]{1,0:T(8,128)S(1)}, f32[288,512]{1,0:T(8,128)S(1)}, u32[]{:S(2)}, u32[]{:S(2)}) collective-permute-start(f32[288,512]{1,0:T(8,128)S(1)} %get-tuple-element.84.refs_0_.refs_10_.refs_14_), channel_id=1, source_target_pairs={{3,2},{6,7},{10,11},{15,14},{19,18},{22,23},{26,27},{31,30},{35,34... | collective-permute-start | bytes 1769480 | tf_op jit(solution)/shard_map/ppermute | solution.py:192
  10.2 7.3 %collective-permute-start.6 = (f32[288,512]{1,0:T(8,128)S(1)}, f32[288,512]{1,0:T(8,128)S(1)}, u32[]{:S(2)}, u32[]{:S(2)}) collective-permute-start(f32[288,512]{1,0:T(8,128)S(1)} %get-tuple-element.84.refs_0_.refs_10_.refs_14_), channel_id=1, source_target_pairs={{4,2},{1,7},{13,11},{8,14},{20,18},{17,23},{29,27},{24,30},{36,34}... | collective-permute-start | bytes 1769480 | tf_op jit(solution)/shard_map/ppermute | solution.py:192
  10.9 6.6 %collective-permute-start.5 = (f32[288,512]{1,0:T(8,128)S(1)}, f32[288,512]{1,0:T(8,128)S(1)}, u32[]{:S(2)}, u32[]{:S(2)}) collective-permute-start(f32[288,512]{1,0:T(8,128)S(1)} %get-tuple-element.84.refs_0_.refs_10_.refs_14_), channel_id=1, source_target_pairs={{0,2},{5,7},{9,11},{12,14},{16,18},{21,23},{25,27},{28,30},{32,34}... | collective-permute-start | bytes 1769480 | tf_op jit(solution)/shard_map/ppermute | solution.py:192
  11.7 6.8 %collective-permute-start.4 = (f32[128,512]{1,0:T(8,128)S(1)}, f32[128,512]{1,0:T(8,128)S(1)}, u32[]{:S(2)}, u32[]{:S(2)}) collective-permute-start(f32[128,512]{1,0:T(8,128)S(1)} %sum.1), channel_id=1, source_target_pairs={{11,2},{14,7},{18,11},{23,14},{27,18},{30,23},{34,27},{39,30},{43,... | collective-permute-start | bytes 786440 | tf_op jit(solution)/shard_map/ppermute | solution.py:205
  12.4 6.2 %collective-permute-start.3 = (f32[128,512]{1,0:T(8,128)S(1)}, f32[128,512]{1,0:T(8,128)S(1)}, u32[]{:S(2)}, u32[]{:S(2)}) collective-permute-start(f32[128,512]{1,0:T(8,128)S(1)} %sum.1), channel_id=1, source_target_pairs={{11,7},{14,2},{18,14},{23,11},{27,23},{30,18},{34,30},{39,27},{43,... | collective-permute-start | bytes 786440 | tf_op jit(solution)/shard_map/ppermute | solution.py:205
  20.2 3.1 %collective-permute-start.9 = (f32[128,512]{1,0:T(8,128)S(1)}, f32[128,512]{1,0:T(8,128)S(1)}, u32[]{:S(2)}, u32[]{:S(2)}) collective-permute-start(f32[128,512]{1,0:T(8,128)S(1)} %get-tuple-element.101), channel_id=1, source_target_pairs={{11,2},{14,7},{18,11},{23,14},{27,18},{30,23},{34,27},{39,30},{43,... | collective-permute-start | bytes 786440 | tf_op jit(solution)/shard_map/ppermute | solution.py:205
  20.8 2.4 %collective-permute-start.8 = (f32[128,512]{1,0:T(8,128)S(1)}, f32[128,512]{1,0:T(8,128)S(1)}, u32[]{:S(2)}, u32[]{:S(2)}) collective-permute-start(f32[128,512]{1,0:T(8,128)S(1)} %get-tuple-element.101), channel_id=1, source_target_pairs={{11,7},{14,2},{18,14},{23,11},{27,23},{30,18},{34,30},{39,27},{43,... | collective-permute-start | bytes 786440 | tf_op jit(solution)/shard_map/ppermute | solution.py:205
  24.9 3.1 %collective-permute-start.11 = (f32[128,512]{1,0:T(8,128)S(1)}, f32[128,512]{1,0:T(8,128)S(1)}, u32[]{:S(2)}, u32[]{:S(2)}) collective-permute-start(f32[128,512]{1,0:T(8,128)S(1)} %get-tuple-element.126), channel_id=1, source_target_pairs={{11,2},{14,7},{18,11},{23,14},{27,18},{30,23},{34,27},{39,30},{43,... | collective-permute-start | bytes 786440 | tf_op jit(solution)/shard_map/ppermute | solution.py:205
  25.6 2.4 %collective-permute-start.10 = (f32[128,512]{1,0:T(8,128)S(1)}, f32[128,512]{1,0:T(8,128)S(1)}, u32[]{:S(2)}, u32[]{:S(2)}) collective-permute-start(f32[128,512]{1,0:T(8,128)S(1)} %get-tuple-element.126), channel_id=1, source_target_pairs={{11,7},{14,2},{18,14},{23,11},{27,23},{30,18},{34,30},{39,27},{43,... | collective-permute-start | bytes 786440 | tf_op jit(solution)/shard_map/ppermute | solution.py:205
  31.8 56.0 %all-to-all-start = ((f32[8,16,512]{2,1,0:T(8,128)}), f32[8,16,512]{2,1,0:T(8,128)S(1)}, u32[]{:S(2)}, u32[]{:S(2)}) async-start(f32[8,16,512]{2,1,0:T(8,128)} %bitcast.2), calls=%async_computation | async-start | bytes 524288 | tf_op jit(solution)/shard_map/all_to_all | solution.py:242
  82.9 12.5 %collective-permute-start.13 = (f32[256,512]{1,0:T(8,128)}, f32[256,512]{1,0:T(8,128)S(1)}, u32[]{:S(2)}, u32[]{:S(2)}) collective-permute-start(f32[256,512]{1,0:T(8,128)} %get-tuple-element.161), channel_id=1, source_target_pairs={{2,0},{7,5},{11,9},{14,12},{18,16},{23,21},{27,25},{30,28},{34,32}... | collective-permute-start | bytes 1572872 | tf_op jit(solution)/shard_map/ppermute | solution.py:196
  83.6 11.8 %collective-permute-start.14 = (f32[256,512]{1,0:T(8,128)S(1)}, f32[256,512]{1,0:T(8,128)S(1)}, u32[]{:S(2)}, u32[]{:S(2)}) collective-permute-start(f32[256,512]{1,0:T(8,128)S(1)} %get-tuple-element.162), channel_id=1, source_target_pairs={{2,4},{7,1},{11,13},{14,8},{18,20},{23,17},{27,29},{30,24},{34,36}... | collective-permute-start | bytes 1572872 | tf_op jit(solution)/shard_map/ppermute | solution.py:196
  84.3 12.6 %collective-permute-start.15 = (f32[256,512]{1,0:T(8,128)S(1)}, f32[256,512]{1,0:T(8,128)S(1)}, u32[]{:S(2)}, u32[]{:S(2)}) collective-permute-start(f32[256,512]{1,0:T(8,128)S(1)} %get-tuple-element.163), channel_id=1, source_target_pairs={{2,3},{7,6},{11,10},{14,15},{18,19},{23,22},{27,26},{30,31},{34,35... | collective-permute-start | bytes 1572872 | tf_op jit(solution)/shard_map/ppermute | solution.py:196
  87.8 7.6 %collective-permute-start.12 = (f32[16,512]{1,0:T(8,128)S(1)}, f32[16,512]{1,0:T(8,128)S(1)}, u32[]{:S(2)}, u32[]{:S(2)}) collective-permute-start(f32[16,512]{1,0:T(8,128)S(1)} %share.1), channel_id=1, source_target_pairs={{8,0},{16,8},{24,16},{32,24},{40,32},{48,40},{56,48},{64,56},{72,6... | collective-permute-start | bytes 98312 | tf_op jit(solution)/shard_map/ppermute | solution.py:244

commit v10 on v9

--- a/solution.py
+++ b/solution.py
@@ -145,7 +145,8 @@
 
 def last_kernel(pieces, chunks, *refs):
     held_refs, ready_refs, refs = refs[:pieces], refs[pieces : pieces + 4 * chunks], refs[pieces + 4 * chunks :]
-    user_refs, out_ref, new_refs = refs[:chunks], refs[chunks], refs[chunks + 1 :]
+    user_refs, out_hbm, own_ref, new_hbm = refs[:chunks], refs[chunks], refs[chunks + 1], refs[chunks + 2 : 2 * chunks + 1]
+    out, new, errors_ref, sems = refs[2 * chunks + 1 :]
     held = slab_of(held_refs)
     held_halves = halves(held)
     total = jnp.zeros(held.shape, jnp.float32)
@@ -153,9 +154,22 @@
         high_ref, low_ref, weights_ref, targets_ref = ready_refs[4 * i : 4 * i + 4]
         user = high_ref[...], low_ref[...]
         errors = halves(weights_ref[...] * product(held_halves, user, NT) - targets_ref[...])
+        errors_ref[2 * i], errors_ref[2 * i + 1] = errors
         total += product(errors, user, NN)
-        new_refs[i][...] = DECAY * user_refs[i][...] - LEARN_RATE * product(errors, held_halves, TN)
-    out_ref[...] = kept() * held - LEARN_RATE * total
+    out[...] = kept() * held - LEARN_RATE * total
+    sends = [pltpu.make_async_copy(out, out_hbm, sems.at[0])]
+    sends[0].start()
+    for i in (*range(1, chunks), 0):
+        move = product((errors_ref[2 * i], errors_ref[2 * i + 1]), held_halves, TN)
+        moved = DECAY * user_refs[i][...] - LEARN_RATE * move
+        if i == 0:
+            own_ref[...] = moved
+        else:
+            new[i - 1] = moved
+            sends.append(pltpu.make_async_copy(new.at[i - 1], new_hbm[i - 1], sems.at[i]))
+            sends[-1].start()
+    for send in sends:
+        send.wait()
 
 
 def share_kernel(parts_ref, out_ref):
@@ -238,7 +252,15 @@
         ahead = [x for i, x in enumerate(outs) if i % 5]
         held = sent
     kernel = functools.partial(last_kernel, pieces, chunks)
-    out, *user = call(kernel, [((slab, rank), f32)] + [factors] * chunks, "last")(*held, *ahead, *user)
+    vmem = pl.BlockSpec(memory_space=pltpu.VMEM)
+    out, *user = call(
+        kernel,
+        [((slab, rank), f32)] + [factors] * chunks,
+        "last",
+        out_specs=[hbm, vmem] + [hbm] * (chunks - 1),
+        scratch_shapes=[pltpu.VMEM((slab, rank), f32), pltpu.VMEM((chunks - 1, users, rank), f32)]
+        + [pltpu.VMEM((2 * chunks, slab, users), bf16), pltpu.SemaphoreType.DMA((chunks,))],
+    )(*held, *ahead, *user)
     parts = lax.all_to_all(out.reshape(n, share_rows, rank), "split", 0, 0)
     (share,) = call(share_kernel, [((share_rows, rank), f32)], "share", cost_estimate=early)(parts)
     share = lax.ppermute(share, "blk", [((b + 1) % blocks, b) for b in range(blocks)])

time: 98.3 us -> 97.8 us (level)
  no operation moved by 1% of the time
where the time goes in v10:
time: 97.8 us; the launch traced here: 97.2 us
  starting transfers between devices  72.6 us (74%)
  Pallas kernels  13.9 us (14%)
  waiting for transfers between devices  9.83 us (10%)
    all_to_all x1, starting transfers between devices, local(): parts = lax.all_to_all(out.reshape(n, share_rows, rank), 'split', 0, 0)  51.1 us
    ppermute x6, starting transfers between devices, fetch(): return lax.ppermute(x, both, pairs)  8.79 us
    ppermute x1, starting transfers between devices, local(): lax.ppermute(share, 'blk', [((b + 1) % blocks, b) for b in range(blocks)])  5.98 us
    ppermute x6, waiting for transfers between devices, fetch(): return lax.ppermute(x, both, pairs)  4.49 us
    ppermute x6, starting transfers between devices, onward(): return [lax.ppermute(x, both, cross), lax.ppermute(x, both, same)]  4.06 us
    pallas_call x2, Pallas kernels, local(): call(kernel, [factors, *ready] * chunks, 'users')  3.44 us
    pallas_call x1, Pallas kernels, local(): call(kernel, [((slab, rank), f32)] + [factors] * chunks, 'last', out_spec...  3.26 us
    pallas_call x2, Pallas kernels, local(): out, *errors = call(kernel, outs, 'group')(*held, *ahead)  3.17 us
  transfers between devices with their start and end apart: 17, of which 4 were waited for; matrix products, arithmetic and copies ran while one was open for 0% of the time, Pallas kernels for 5%

profile of v10, /device:TPU:6, one launch (start us, length us, event | category | flops | bytes accessed | tf_op | source)
XLA Modules:
  0.0 97.2 jit_solution(4271148594529847297)
XLA Ops:
  0.6 2.2 %first.1 = (f32[128,512]{1,0:T(8,128)S(1)}, f32[288,512]{1,0:T(8,128)S(1)}) custom-call(f32[256,512]{1,0:T(8,128)} %user_hbm.1, f32[128,512]{1,0:T(8,128)} %held_hbm.1, s32[4,8,256]{2,1,0:T(8,128)} %bitcast.3, s32[4,8,256]{2,1,0:T(8,128)} %bitcast.4), custom_call_target="tpu_custom_call" | custom-call | tf_op jit(solution)/shard_map/first/pallas_call | solution.py:225
  2.8 3.5 %collective-permute-start.2 = (f32[128,512]{1,0:T(8,128)S(1)}, f32[128,512]{1,0:T(8,128)S(1)}, u32[]{:S(2)}, u32[]{:S(2)}) collective-permute-start(f32[128,512]{1,0:T(8,128)S(1)} %get-tuple-element.83.refs_0_), channel_id=1, source_target_pairs={{3,2},{6,7},{10,11},{15,14},{19,18},{22,23},{26,27},{31,30},{35,34... | collective-permute-start | bytes 786440 | tf_op jit(solution)/shard_map/ppermute | solution.py:206
  7.7 2.5 %collective-permute-start.7 = (f32[288,512]{1,0:T(8,128)S(1)}, f32[288,512]{1,0:T(8,128)S(1)}, u32[]{:S(2)}, u32[]{:S(2)}) collective-permute-start(f32[288,512]{1,0:T(8,128)S(1)} %get-tuple-element.84.refs_0_.refs_10_.refs_14_), channel_id=1, source_target_pairs={{3,2},{6,7},{10,11},{15,14},{19,18},{22,23},{26,27},{31,30},{35,34... | collective-permute-start | bytes 1769480 | tf_op jit(solution)/shard_map/ppermute | solution.py:206
  10.2 0.7 collective-permute-start.6
  10.9 0.7 collective-permute-start.5
  11.7 0.7 collective-permute-start.4
  12.4 0.7 collective-permute-start.3
  13.1 4.5 %collective-permute-done.7.refs_3_.refs_13_.refs_17_ = f32[288,512]{1,0:T(8,128)S(1)} collective-permute-done((f32[288,512]{1,0:T(8,128)S(1)}, f32[288,512]{1,0:T(8,128)S(1)}, u32[]{:S(2)}, u32[]{:S(2)}) %collective-permute-start.7) | collective-permute-done | bytes 589856 | tf_op jit(solution)/shard_map/ppermute | solution.py:206
  17.6 1.0 prepare.1
  18.6 1.6 %group.2 = (f32[128,512]{1,0:T(8,128)S(1)}, bf16[128,256]{1,0:T(8,128)(2,1)S(1)}, bf16[128,256]{1,0:T(8,128)(2,1)S(1)}, bf16[128,256]{1,0:T(8,128)(2,1)S(1)}, bf...) custom-call(f32[128,512]{1,0:T(8,128)S(1)} %collective-permute-done., ...), custom_call_target="tpu_custom_call" | custom-call | tf_op jit(solution)/shard_map/group/pallas_call | solution.py:247
  21.5 1.7 %users.2 = (f32[256,512]{1,0:T(8,128)S(1)}, bf16[256,512]{1,0:T(8,128)(2,1)S(1)}, bf16[256,512]{1,0:T(8,128)(2,1)S(1)}, f32[128,256]{1,0:T(8,128)S(1)}, f32[128,...) custom-call(f32[128,512]{1,0:T(8,128)S(1)} %collective-permute-done., ...), custom_call_target="tpu_custom_call" | custom-call | tf_op jit(solution)/shard_map/users/pallas_call | solution.py:250
  23.3 1.6 %group.3 = (f32[128,512]{1,0:T(8,128)S(1)}, bf16[128,256]{1,0:T(8,128)(2,1)S(1)}, bf16[128,256]{1,0:T(8,128)(2,1)S(1)}, bf16[128,256]{1,0:T(8,128)(2,1)S(1)}, bf...) custom-call(f32[128,512]{1,0:T(8,128)S(1)} %collective-permute-done., ...), custom_call_target="tpu_custom_call" | custom-call | tf_op jit(solution)/shard_map/group/pallas_call | solution.py:247
  24.9 0.7 collective-permute-start.11
  26.2 1.7 %users.3 = (f32[256,512]{1,0:T(8,128)S(1)}, bf16[256,512]{1,0:T(8,128)(2,1)S(1)}, bf16[256,512]{1,0:T(8,128)(2,1)S(1)}, f32[128,256]{1,0:T(8,128)S(1)}, f32[128,...) custom-call(f32[128,512]{1,0:T(8,128)S(1)} %collective-permute-done., ...), custom_call_target="tpu_custom_call" | custom-call | tf_op jit(solution)/shard_map/users/pallas_call | solution.py:250
  28.0 3.3 %last.1 = (f32[128,512]{1,0:T(8,128)}, f32[256,512]{1,0:T(8,128)S(1)}, f32[256,512]{1,0:T(8,128)}, f32[256,512]{1,0:T(8,128)S(1)}, f32[256,512]{1,0:T(8,128)S(1)}) custom-call(f32[128,512]{1,0:T(8,128)S(1)} %collective-permute-done.10.refs_0_, f32[128,512]{1,0:T(8,128)S(1)} %collective-permute-done.11.refs_1_, ...), custom_call_target="tpu_custom_call" | custom-call | tf_op jit(solution)/shard_map/last/pallas_call | solution.py:256
  31.3 51.1 %all-to-all-start = ((f32[8,16,512]{2,1,0:T(8,128)}), f32[8,16,512]{2,1,0:T(8,128)S(1)}, u32[]{:S(2)}, u32[]{:S(2)}) async-start(f32[8,16,512]{2,1,0:T(8,128)} %bitcast.2), calls=%async_computation | async-start | bytes 524288 | tf_op jit(solution)/shard_map/all_to_all | solution.py:264
  82.4 0.7 collective-permute-start.13
  83.1 0.7 collective-permute-start.14
  83.8 1.3 %collective-permute-start.15 = (f32[256,512]{1,0:T(8,128)S(1)}, f32[256,512]{1,0:T(8,128)S(1)}, u32[]{:S(2)}, u32[]{:S(2)}) collective-permute-start(f32[256,512]{1,0:T(8,128)S(1)} %get-tuple-element.163), channel_id=1, source_target_pairs={{2,3},{7,6},{11,10},{14,15},{18,19},{23,22},{27,26},{30,31},{34,35... | collective-permute-start | bytes 1572872 | tf_op jit(solution)/shard_map/ppermute | solution.py:210
  85.1 2.2 %all-to-all-done.parts_ref = f32[8,16,512]{2,1,0:T(8,128)S(1)} async-done(((f32[8,16,512]{2,1,0:T(8,128)}), f32[8,16,512]{2,1,0:T(8,128)S(1)}, u32[]{:S(2)}, u32[]{:S(2)}) %all-to-all-start) | async-done | bytes 262176 | tf_op jit(solution)/shard_map/all_to_all | solution.py:264
  87.3 6.0 %collective-permute-start.12 = (f32[16,512]{1,0:T(8,128)S(1)}, f32[16,512]{1,0:T(8,128)S(1)}, u32[]{:S(2)}, u32[]{:S(2)}) collective-permute-start(f32[16,512]{1,0:T(8,128)S(1)} %share.1), channel_id=1, source_target_pairs={{8,0},{16,8},{24,16},{32,24},{40,32},{48,40},{56,48},{64,56},{72,6... | collective-permute-start | bytes 98312 | tf_op jit(solution)/shard_map/ppermute | solution.py:266
  93.3 1.6 %collective-permute-done.12.share_ref = f32[16,512]{1,0:T(8,128)S(1)} collective-permute-done((f32[16,512]{1,0:T(8,128)S(1)}, f32[16,512]{1,0:T(8,128)S(1)}, u32[]{:S(2)}, u32[]{:S(2)}) %collective-permute-start.12) | collective-permute-done | bytes 32800 | tf_op jit(solution)/shard_map/ppermute | solution.py:266
  94.9 1.5 %collective-permute-done.15.c_ref = f32[256,512]{1,0:T(8,128)S(1)} collective-permute-done((f32[256,512]{1,0:T(8,128)S(1)}, f32[256,512]{1,0:T(8,128)S(1)}, u32[]{:S(2)}, u32[]{:S(2)}) %collective-permute-start.15) | collective-permute-done | bytes 524320 | tf_op jit(solution)/shard_map/ppermute | solution.py:210
  96.4 0.8 home.1
  (20 shorter events, 3.5 us)
Async XLA Ops:
  2.8 8.1 %collective-permute-start.2 = (f32[128,512]{1,0:T(8,128)S(1)}, f32[128,512]{1,0:T(8,128)S(1)}, u32[]{:S(2)}, u32[]{:S(2)}) collective-permute-start(f32[128,512]{1,0:T(8,128)S(1)} %get-tuple-element.83.refs_0_), channel_id=1, source_target_pairs={{3,2},{6,7},{10,11},{15,14},{19,18},{22,23},{26,27},{31,30},{35,34... | collective-permute-start | bytes 786440 | tf_op jit(solution)/shard_map/ppermute | solution.py:206
  6.3 5.3 %collective-permute-start.1 = (f32[128,512]{1,0:T(8,128)S(1)}, f32[128,512]{1,0:T(8,128)S(1)}, u32[]{:S(2)}, u32[]{:S(2)}) collective-permute-start(f32[128,512]{1,0:T(8,128)S(1)} %get-tuple-element.83.refs_0_), channel_id=1, source_target_pairs={{4,2},{1,7},{13,11},{8,14},{20,18},{17,23},{29,27},{24,30},{36,34}... | collective-permute-start | bytes 786440 | tf_op jit(solution)/shard_map/ppermute | solution.py:206
  7.0 4.7 %collective-permute-start = (f32[128,512]{1,0:T(8,128)S(1)}, f32[128,512]{1,0:T(8,128)S(1)}, u32[]{:S(2)}, u32[]{:S(2)}) collective-permute-start(f32[128,512]{1,0:T(8,128)S(1)} %get-tuple-element.83.refs_0_), channel_id=1, source_target_pairs={{0,2},{5,7},{9,11},{12,14},{16,18},{21,23},{25,27},{28,30},{32,34}... | collective-permute-start | bytes 786440 | tf_op jit(solution)/shard_map/ppermute | solution.py:206
  7.7 9.9 %collective-permute-start.7 = (f32[288,512]{1,0:T(8,128)S(1)}, f32[288,512]{1,0:T(8,128)S(1)}, u32[]{:S(2)}, u32[]{:S(2)}) collective-permute-start(f32[288,512]{1,0:T(8,128)S(1)} %get-tuple-element.84.refs_0_.refs_10_.refs_14_), channel_id=1, source_target_pairs={{3,2},{6,7},{10,11},{15,14},{19,18},{22,23},{26,27},{31,30},{35,34... | collective-permute-start | bytes 1769480 | tf_op jit(solution)/shard_map/ppermute | solution.py:206
  10.2 7.3 %collective-permute-start.6 = (f32[288,512]{1,0:T(8,128)S(1)}, f32[288,512]{1,0:T(8,128)S(1)}, u32[]{:S(2)}, u32[]{:S(2)}) collective-permute-start(f32[288,512]{1,0:T(8,128)S(1)} %get-tuple-element.84.refs_0_.refs_10_.refs_14_), channel_id=1, source_target_pairs={{4,2},{1,7},{13,11},{8,14},{20,18},{17,23},{29,27},{24,30},{36,34}... | collective-permute-start | bytes 1769480 | tf_op jit(solution)/shard_map/ppermute | solution.py:206
  10.9 6.6 %collective-permute-start.5 = (f32[288,512]{1,0:T(8,128)S(1)}, f32[288,512]{1,0:T(8,128)S(1)}, u32[]{:S(2)}, u32[]{:S(2)}) collective-permute-start(f32[288,512]{1,0:T(8,128)S(1)} %get-tuple-element.84.refs_0_.refs_10_.refs_14_), channel_id=1, source_target_pairs={{0,2},{5,7},{9,11},{12,14},{16,18},{21,23},{25,27},{28,30},{32,34}... | collective-permute-start | bytes 1769480 | tf_op jit(solution)/shard_map/ppermute | solution.py:206
  11.7 6.8 %collective-permute-start.4 = (f32[128,512]{1,0:T(8,128)S(1)}, f32[128,512]{1,0:T(8,128)S(1)}, u32[]{:S(2)}, u32[]{:S(2)}) collective-permute-start(f32[128,512]{1,0:T(8,128)S(1)} %sum.1), channel_id=1, source_target_pairs={{11,2},{14,7},{18,11},{23,14},{27,18},{30,23},{34,27},{39,30},{43,... | collective-permute-start | bytes 786440 | tf_op jit(solution)/shard_map/ppermute | solution.py:219
  12.4 6.2 %collective-permute-start.3 = (f32[128,512]{1,0:T(8,128)S(1)}, f32[128,512]{1,0:T(8,128)S(1)}, u32[]{:S(2)}, u32[]{:S(2)}) collective-permute-start(f32[128,512]{1,0:T(8,128)S(1)} %sum.1), channel_id=1, source_target_pairs={{11,7},{14,2},{18,14},{23,11},{27,23},{30,18},{34,30},{39,27},{43,... | collective-permute-start | bytes 786440 | tf_op jit(solution)/shard_map/ppermute | solution.py:219
  20.2 3.1 %collective-permute-start.9 = (f32[128,512]{1,0:T(8,128)S(1)}, f32[128,512]{1,0:T(8,128)S(1)}, u32[]{:S(2)}, u32[]{:S(2)}) collective-permute-start(f32[128,512]{1,0:T(8,128)S(1)} %get-tuple-element.101), channel_id=1, source_target_pairs={{11,2},{14,7},{18,11},{23,14},{27,18},{30,23},{34,27},{39,30},{43,... | collective-permute-start | bytes 786440 | tf_op jit(solution)/shard_map/ppermute | solution.py:219
  20.8 2.4 %collective-permute-start.8 = (f32[128,512]{1,0:T(8,128)S(1)}, f32[128,512]{1,0:T(8,128)S(1)}, u32[]{:S(2)}, u32[]{:S(2)}) collective-permute-start(f32[128,512]{1,0:T(8,128)S(1)} %get-tuple-element.101), channel_id=1, source_target_pairs={{11,7},{14,2},{18,14},{23,11},{27,23},{30,18},{34,30},{39,27},{43,... | collective-permute-start | bytes 786440 | tf_op jit(solution)/shard_map/ppermute | solution.py:219
  24.9 3.1 %collective-permute-start.11 = (f32[128,512]{1,0:T(8,128)S(1)}, f32[128,512]{1,0:T(8,128)S(1)}, u32[]{:S(2)}, u32[]{:S(2)}) collective-permute-start(f32[128,512]{1,0:T(8,128)S(1)} %get-tuple-element.126), channel_id=1, source_target_pairs={{11,2},{14,7},{18,11},{23,14},{27,18},{30,23},{34,27},{39,30},{43,... | collective-permute-start | bytes 786440 | tf_op jit(solution)/shard_map/ppermute | solution.py:219
  25.6 2.4 %collective-permute-start.10 = (f32[128,512]{1,0:T(8,128)S(1)}, f32[128,512]{1,0:T(8,128)S(1)}, u32[]{:S(2)}, u32[]{:S(2)}) collective-permute-start(f32[128,512]{1,0:T(8,128)S(1)} %get-tuple-element.126), channel_id=1, source_target_pairs={{11,7},{14,2},{18,14},{23,11},{27,23},{30,18},{34,30},{39,27},{43,... | collective-permute-start | bytes 786440 | tf_op jit(solution)/shard_map/ppermute | solution.py:219
  31.3 56.0 %all-to-all-start = ((f32[8,16,512]{2,1,0:T(8,128)}), f32[8,16,512]{2,1,0:T(8,128)S(1)}, u32[]{:S(2)}, u32[]{:S(2)}) async-start(f32[8,16,512]{2,1,0:T(8,128)} %bitcast.2), calls=%async_computation | async-start | bytes 524288 | tf_op jit(solution)/shard_map/all_to_all | solution.py:264
  82.4 12.5 %collective-permute-start.13 = (f32[256,512]{1,0:T(8,128)}, f32[256,512]{1,0:T(8,128)S(1)}, u32[]{:S(2)}, u32[]{:S(2)}) collective-permute-start(f32[256,512]{1,0:T(8,128)} %get-tuple-element.161), channel_id=1, source_target_pairs={{2,0},{7,5},{11,9},{14,12},{18,16},{23,21},{27,25},{30,28},{34,32}... | collective-permute-start | bytes 1572872 | tf_op jit(solution)/shard_map/ppermute | solution.py:210
  83.1 11.8 %collective-permute-start.14 = (f32[256,512]{1,0:T(8,128)S(1)}, f32[256,512]{1,0:T(8,128)S(1)}, u32[]{:S(2)}, u32[]{:S(2)}) collective-permute-start(f32[256,512]{1,0:T(8,128)S(1)} %get-tuple-element.162), channel_id=1, source_target_pairs={{2,4},{7,1},{11,13},{14,8},{18,20},{23,17},{27,29},{30,24},{34,36}... | collective-permute-start | bytes 1572872 | tf_op jit(solution)/shard_map/ppermute | solution.py:210
  83.8 12.6 %collective-permute-start.15 = (f32[256,512]{1,0:T(8,128)S(1)}, f32[256,512]{1,0:T(8,128)S(1)}, u32[]{:S(2)}, u32[]{:S(2)}) collective-permute-start(f32[256,512]{1,0:T(8,128)S(1)} %get-tuple-element.163), channel_id=1, source_target_pairs={{2,3},{7,6},{11,10},{14,15},{18,19},{23,22},{27,26},{30,31},{34,35... | collective-permute-start | bytes 1572872 | tf_op jit(solution)/shard_map/ppermute | solution.py:210
  87.3 7.6 %collective-permute-start.12 = (f32[16,512]{1,0:T(8,128)S(1)}, f32[16,512]{1,0:T(8,128)S(1)}, u32[]{:S(2)}, u32[]{:S(2)}) collective-permute-start(f32[16,512]{1,0:T(8,128)S(1)} %share.1), channel_id=1, source_target_pairs={{8,0},{16,8},{24,16},{32,24},{40,32},{48,40},{56,48},{64,56},{72,6... | collective-permute-start | bytes 98312 | tf_op jit(solution)/shard_map/ppermute | solution.py:266

commit v11 on v10

--- a/solution.py
+++ b/solution.py
@@ -77,11 +77,10 @@
     return jnp.where((lax.axis_index("split") ^ parity()) == FIRST, DECAY, 0.0)
 
 
-def first_kernel(user_hbm, held_hbm, items_hbm, conf_hbm, part, pack, user_ref, held_ref, items, conf, sems):
-    users = user_ref.shape[0]
-    slab = held_ref.shape[0]
-    steps, obs, _ = items.shape
-    pairs = ((items_hbm, items), (conf_hbm, conf), (held_hbm, held_ref), (user_hbm, user_ref))
+def first_kernel(user_hbm, held_hbm, items_hbm, conf_hbm, part, errors_ref, held_ref, raw, items, conf, sems):
+    slab, _ = held_ref.shape
+    steps, obs, users = items.shape
+    pairs = ((items_hbm, items), (conf_hbm, conf), (held_hbm, held_ref), (user_hbm, raw.at[pl.ds(0, users), :]))
     loads = [pltpu.make_async_copy(source, target, sems.at[i]) for i, (source, target) in enumerate(pairs)]
     for copy in loads:
         copy.start()
@@ -89,17 +88,23 @@
     loads[1].wait()
     for s in range(steps):
         at = users + s * obs
-        pack[at : at + obs, :users] = items[s].astype(jnp.float32)
-        pack[at : at + obs, users:] = conf[s].astype(jnp.float32)
+        raw[at : at + obs, :users] = items[s].astype(jnp.float32)
+        raw[at : at + obs, users:] = conf[s].astype(jnp.float32)
     weights, targets = weigh(items[0], conf[0].astype(jnp.float32), slab)
     loads[2].wait()
     loads[3].wait()
     held = held_ref[...]
-    held_halves = halves(held)
-    user = halves(user_ref[...])
-    errors = halves(weights * product(held_halves, user, NT) - targets)
+    user = halves(raw[:users, :])
+    errors = halves(weights * product(halves(held), user, NT) - targets)
+    errors_ref[0], errors_ref[1] = errors
     part[...] = kept() * held - LEARN_RATE * product(errors, user, NN)
-    pack[:users, :] = DECAY * user_ref[...] - LEARN_RATE * product(errors, held_halves, TN)
+
+
+def pack_kernel(raw, held_ref, errors_ref, pack):
+    users = errors_ref.shape[2]
+    move = product((errors_ref[0], errors_ref[1]), halves(held_ref[...]), TN)
+    pack[:users, :] = DECAY * raw[:users, :] - LEARN_RATE * move
+    pack[users:, :] = raw[users:, :]
 
 
 def sum_kernel(*refs):
@@ -222,15 +227,14 @@
     early = pl.CostEstimate(flops=1 << 36, bytes_accessed=1 << 20, transcendentals=0)
     hbm = pl.BlockSpec(memory_space=pltpu.HBM)
     rows = users + steps * obs
-    part, pack = call(
+    part, first_errors, slab_copy, raw = call(
         first_kernel,
-        [((slab, rank), f32), ((rows, rank), f32)],
+        [((slab, rank), f32), ((2, slab, users), bf16), ((slab, rank), f32), ((rows, rank), f32)],
         "first",
         in_specs=[hbm] * 4,
-        scratch_shapes=[pltpu.VMEM(user_factors.shape, f32), pltpu.VMEM(item_factors.shape, f32)]
-        + [pltpu.VMEM(items.shape, jnp.int32)] * 2
-        + [pltpu.SemaphoreType.DMA((4,))],
+        scratch_shapes=[pltpu.VMEM(items.shape, jnp.int32)] * 2 + [pltpu.SemaphoreType.DMA((4,))],
     )(*[pltpu.with_memory_space_constraint(x, pltpu.HBM) for x in (user_factors, item_factors, items, conf)])
+    (pack,) = call(pack_kernel, [((rows, rank), f32)], "pack")(raw, slab_copy, first_errors)
     arrived = [part] + [fetch(part, helpers) for helpers in HELPERS]
     packs = [pack] + [fetch(pack, helpers) for helpers in HELPERS]
     (out,) = call(sum_kernel, [((slab, rank), f32)], "sum", cost_estimate=early)(*arrived)

time: 97.8 us -> 97.6 us (level)
    pallas_call x1 -> x2, Pallas kernels: 2.15 us -> 2.3 us  [the longest x1 1.91 us: local(): call(first_kernel, [((slab, rank), f32), ((2, slab, users), bf16), ((slab...]
where the time goes in v11:
time: 97.6 us; the launch traced here: 97 us
  starting transfers between devices  72 us (74%)
  Pallas kernels  14 us (14%)
  waiting for transfers between devices  10 us (10%)
    all_to_all x1, starting transfers between devices, local(): parts = lax.all_to_all(out.reshape(n, share_rows, rank), 'split', 0, 0)  50.5 us
    ppermute x6, starting transfers between devices, fetch(): return lax.ppermute(x, both, pairs)  8.79 us
    ppermute x1, starting transfers between devices, local(): lax.ppermute(share, 'blk', [((b + 1) % blocks, b) for b in range(blocks)])  5.98 us
    ppermute x6, waiting for transfers between devices, fetch(): return lax.ppermute(x, both, pairs)  4.69 us
    ppermute x6, starting transfers between devices, onward(): return [lax.ppermute(x, both, cross), lax.ppermute(x, both, same)]  4.06 us
    pallas_call x2, Pallas kernels, local(): call(kernel, [factors, *ready] * chunks, 'users')  3.44 us
    pallas_call x1, Pallas kernels, local(): call(kernel, [((slab, rank), f32)] + [factors] * chunks, 'last', out_spec...  3.26 us
    pallas_call x2, Pallas kernels, local(): out, *errors = call(kernel, outs, 'group')(*held, *ahead)  3.17 us
  transfers between devices with their start and end apart: 17, of which 4 were waited for; matrix products, arithmetic and copies ran while one was open for 0% of the time, Pallas kernels for 5%

profile of v11, /device:TPU:6, one launch (start us, length us, event | category | flops | bytes accessed | tf_op | source)
XLA Modules:
  0.0 97.0 jit_solution(6358732354020617600)
XLA Ops:
  0.6 1.9 %first.1 = (f32[128,512]{1,0:T(8,128)S(1)}, bf16[2,128,256]{2,1,0:T(8,128)(2,1)S(1)}, f32[128,512]{1,0:T(8,128)S(1)}, f32[288,512]{1,0:T(8,128)S(1)}) custom-call(f32[256,512]{1,0:T(8,128)} %user_hbm.1, f32[128,512]{1,0:T(8,128)} %held_hbm.1, s32[4,8,256]{2,1,0:T(8,128)} %bitcast.3, s32[4,8,256]{2,1,0:T(8,128)} %bitcast.4), custom_call_target="tpu_custom_call" | custom-call | tf_op jit(solution)/shard_map/first/pallas_call | solution.py:230
  2.5 3.5 %collective-permute-start.2 = (f32[128,512]{1,0:T(8,128)S(1)}, f32[128,512]{1,0:T(8,128)S(1)}, u32[]{:S(2)}, u32[]{:S(2)}) collective-permute-start(f32[128,512]{1,0:T(8,128)S(1)} %get-tuple-element.85.refs_0_), channel_id=1, source_target_pairs={{3,2},{6,7},{10,11},{15,14},{19,18},{22,23},{26,27},{31,30},{35,34... | collective-permute-start | bytes 786440 | tf_op jit(solution)/shard_map/ppermute | solution.py:211
  6.1 0.7 collective-permute-start.1
  6.7 0.7 collective-permute-start
  7.8 2.5 %collective-permute-start.7 = (f32[288,512]{1,0:T(8,128)S(1)}, f32[288,512]{1,0:T(8,128)S(1)}, u32[]{:S(2)}, u32[]{:S(2)}) collective-permute-start(f32[288,512]{1,0:T(8,128)S(1)} %pack.1.refs_0_.refs_10_.refs_14_), channel_id=1, source_target_pairs={{3,2},{6,7},{10,11},{15,14},{19,18},{22,23},{26,27},{31,30},{35,34... | collective-permute-start | bytes 1769480 | tf_op jit(solution)/shard_map/ppermute | solution.py:211
  10.4 0.7 collective-permute-start.6
  11.1 0.7 collective-permute-start.5
  13.2 4.7 %collective-permute-done.7.refs_3_.refs_13_.refs_17_ = f32[288,512]{1,0:T(8,128)S(1)} collective-permute-done((f32[288,512]{1,0:T(8,128)S(1)}, f32[288,512]{1,0:T(8,128)S(1)}, u32[]{:S(2)}, u32[]{:S(2)}) %collective-permute-start.7) | collective-permute-done | bytes 589856 | tf_op jit(solution)/shard_map/ppermute | solution.py:211
  17.9 1.0 %prepare.1 = (bf16[256,512]{1,0:T(8,128)(2,1)S(1)}, bf16[256,512]{1,0:T(8,128)(2,1)S(1)}, f32[128,256]{1,0:T(8,128)S(1)}, f32[128,256]{1,0:T(8,128)S(1)}, bf16[2...) custom-call(f32[288,512]{1,0:T(8,128)S(1)} %pack.1.refs_0_.refs_10_., ...), custom_call_target="tpu_custom_call" | custom-call | tf_op jit(solution)/shard_map/prepare/pallas_call | solution.py:246
  18.9 1.6 %group.2 = (f32[128,512]{1,0:T(8,128)S(1)}, bf16[128,256]{1,0:T(8,128)(2,1)S(1)}, bf16[128,256]{1,0:T(8,128)(2,1)S(1)}, bf16[128,256]{1,0:T(8,128)(2,1)S(1)}, bf...) custom-call(f32[128,512]{1,0:T(8,128)S(1)} %collective-permute-done., ...), custom_call_target="tpu_custom_call" | custom-call | tf_op jit(solution)/shard_map/group/pallas_call | solution.py:251
  21.9 1.7 %users.2 = (f32[256,512]{1,0:T(8,128)S(1)}, bf16[256,512]{1,0:T(8,128)(2,1)S(1)}, bf16[256,512]{1,0:T(8,128)(2,1)S(1)}, f32[128,256]{1,0:T(8,128)S(1)}, f32[128,...) custom-call(f32[128,512]{1,0:T(8,128)S(1)} %collective-permute-done., ...), custom_call_target="tpu_custom_call" | custom-call | tf_op jit(solution)/shard_map/users/pallas_call | solution.py:254
  23.6 1.6 %group.3 = (f32[128,512]{1,0:T(8,128)S(1)}, bf16[128,256]{1,0:T(8,128)(2,1)S(1)}, bf16[128,256]{1,0:T(8,128)(2,1)S(1)}, bf16[128,256]{1,0:T(8,128)(2,1)S(1)}, bf...) custom-call(f32[128,512]{1,0:T(8,128)S(1)} %collective-permute-done., ...), custom_call_target="tpu_custom_call" | custom-call | tf_op jit(solution)/shard_map/group/pallas_call | solution.py:251
  25.9 0.7 collective-permute-start.10
  26.6 1.7 %users.3 = (f32[256,512]{1,0:T(8,128)S(1)}, bf16[256,512]{1,0:T(8,128)(2,1)S(1)}, bf16[256,512]{1,0:T(8,128)(2,1)S(1)}, f32[128,256]{1,0:T(8,128)S(1)}, f32[128,...) custom-call(f32[128,512]{1,0:T(8,128)S(1)} %collective-permute-done., ...), custom_call_target="tpu_custom_call" | custom-call | tf_op jit(solution)/shard_map/users/pallas_call | solution.py:254
  28.4 3.3 %last.1 = (f32[128,512]{1,0:T(8,128)}, f32[256,512]{1,0:T(8,128)S(1)}, f32[256,512]{1,0:T(8,128)}, f32[256,512]{1,0:T(8,128)S(1)}, f32[256,512]{1,0:T(8,128)S(1)}) custom-call(f32[128,512]{1,0:T(8,128)S(1)} %collective-permute-done.10.refs_0_, f32[128,512]{1,0:T(8,128)S(1)} %collective-permute-done.11.refs_1_, ...), custom_call_target="tpu_custom_call" | custom-call | tf_op jit(solution)/shard_map/last/pallas_call | solution.py:260
  31.6 50.5 %all-to-all-start = ((f32[8,16,512]{2,1,0:T(8,128)}), f32[8,16,512]{2,1,0:T(8,128)S(1)}, u32[]{:S(2)}, u32[]{:S(2)}) async-start(f32[8,16,512]{2,1,0:T(8,128)} %bitcast.2), calls=%async_computation | async-start | bytes 524288 | tf_op jit(solution)/shard_map/all_to_all | solution.py:268
  82.2 0.7 collective-permute-start.13
  82.9 0.7 collective-permute-start.14
  83.6 1.3 %collective-permute-start.15 = (f32[256,512]{1,0:T(8,128)S(1)}, f32[256,512]{1,0:T(8,128)S(1)}, u32[]{:S(2)}, u32[]{:S(2)}) collective-permute-start(f32[256,512]{1,0:T(8,128)S(1)} %get-tuple-element.167), channel_id=1, source_target_pairs={{2,3},{7,6},{11,10},{14,15},{18,19},{23,22},{27,26},{30,31},{34,35... | collective-permute-start | bytes 1572872 | tf_op jit(solution)/shard_map/ppermute | solution.py:215
  84.9 2.2 %all-to-all-done.parts_ref = f32[8,16,512]{2,1,0:T(8,128)S(1)} async-done(((f32[8,16,512]{2,1,0:T(8,128)}), f32[8,16,512]{2,1,0:T(8,128)S(1)}, u32[]{:S(2)}, u32[]{:S(2)}) %all-to-all-start) | async-done | bytes 262176 | tf_op jit(solution)/shard_map/all_to_all | solution.py:268
  87.1 6.0 %collective-permute-start.12 = (f32[16,512]{1,0:T(8,128)S(1)}, f32[16,512]{1,0:T(8,128)S(1)}, u32[]{:S(2)}, u32[]{:S(2)}) collective-permute-start(f32[16,512]{1,0:T(8,128)S(1)} %share.1), channel_id=1, source_target_pairs={{8,0},{16,8},{24,16},{32,24},{40,32},{48,40},{56,48},{64,56},{72,6... | collective-permute-start | bytes 98312 | tf_op jit(solution)/shard_map/ppermute | solution.py:270
  93.1 1.6 %collective-permute-done.12.share_ref = f32[16,512]{1,0:T(8,128)S(1)} collective-permute-done((f32[16,512]{1,0:T(8,128)S(1)}, f32[16,512]{1,0:T(8,128)S(1)}, u32[]{:S(2)}, u32[]{:S(2)}) %collective-permute-start.12) | collective-permute-done | bytes 32800 | tf_op jit(solution)/shard_map/ppermute | solution.py:270
  94.6 1.5 %collective-permute-done.15.c_ref = f32[256,512]{1,0:T(8,128)S(1)} collective-permute-done((f32[256,512]{1,0:T(8,128)S(1)}, f32[256,512]{1,0:T(8,128)S(1)}, u32[]{:S(2)}, u32[]{:S(2)}) %collective-permute-start.15) | collective-permute-done | bytes 524320 | tf_op jit(solution)/shard_map/ppermute | solution.py:215
  96.2 0.8 home.1
  (21 shorter events, 3.9 us)
Async XLA Ops:
  2.5 8.5 %collective-permute-start.2 = (f32[128,512]{1,0:T(8,128)S(1)}, f32[128,512]{1,0:T(8,128)S(1)}, u32[]{:S(2)}, u32[]{:S(2)}) collective-permute-start(f32[128,512]{1,0:T(8,128)S(1)} %get-tuple-element.85.refs_0_), channel_id=1, source_target_pairs={{3,2},{6,7},{10,11},{15,14},{19,18},{22,23},{26,27},{31,30},{35,34... | collective-permute-start | bytes 786440 | tf_op jit(solution)/shard_map/ppermute | solution.py:211
  6.1 5.7 %collective-permute-start.1 = (f32[128,512]{1,0:T(8,128)S(1)}, f32[128,512]{1,0:T(8,128)S(1)}, u32[]{:S(2)}, u32[]{:S(2)}) collective-permute-start(f32[128,512]{1,0:T(8,128)S(1)} %get-tuple-element.85.refs_0_), channel_id=1, source_target_pairs={{4,2},{1,7},{13,11},{8,14},{20,18},{17,23},{29,27},{24,30},{36,34}... | collective-permute-start | bytes 786440 | tf_op jit(solution)/shard_map/ppermute | solution.py:211
  6.7 5.1 %collective-permute-start = (f32[128,512]{1,0:T(8,128)S(1)}, f32[128,512]{1,0:T(8,128)S(1)}, u32[]{:S(2)}, u32[]{:S(2)}) collective-permute-start(f32[128,512]{1,0:T(8,128)S(1)} %get-tuple-element.85.refs_0_), channel_id=1, source_target_pairs={{0,2},{5,7},{9,11},{12,14},{16,18},{21,23},{25,27},{28,30},{32,34}... | collective-permute-start | bytes 786440 | tf_op jit(solution)/shard_map/ppermute | solution.py:211
  7.8 10.1 %collective-permute-start.7 = (f32[288,512]{1,0:T(8,128)S(1)}, f32[288,512]{1,0:T(8,128)S(1)}, u32[]{:S(2)}, u32[]{:S(2)}) collective-permute-start(f32[288,512]{1,0:T(8,128)S(1)} %pack.1.refs_0_.refs_10_.refs_14_), channel_id=1, source_target_pairs={{3,2},{6,7},{10,11},{15,14},{19,18},{22,23},{26,27},{31,30},{35,34... | collective-permute-start | bytes 1769480 | tf_op jit(solution)/shard_map/ppermute | solution.py:211
  10.4 7.6 %collective-permute-start.6 = (f32[288,512]{1,0:T(8,128)S(1)}, f32[288,512]{1,0:T(8,128)S(1)}, u32[]{:S(2)}, u32[]{:S(2)}) collective-permute-start(f32[288,512]{1,0:T(8,128)S(1)} %pack.1.refs_0_.refs_10_.refs_14_), channel_id=1, source_target_pairs={{4,2},{1,7},{13,11},{8,14},{20,18},{17,23},{29,27},{24,30},{36,34}... | collective-permute-start | bytes 1769480 | tf_op jit(solution)/shard_map/ppermute | solution.py:211
  11.1 6.8 %collective-permute-start.5 = (f32[288,512]{1,0:T(8,128)S(1)}, f32[288,512]{1,0:T(8,128)S(1)}, u32[]{:S(2)}, u32[]{:S(2)}) collective-permute-start(f32[288,512]{1,0:T(8,128)S(1)} %pack.1.refs_0_.refs_10_.refs_14_), channel_id=1, source_target_pairs={{0,2},{5,7},{9,11},{12,14},{16,18},{21,23},{25,27},{28,30},{32,34}... | collective-permute-start | bytes 1769480 | tf_op jit(solution)/shard_map/ppermute | solution.py:211
  11.9 7.0 %collective-permute-start.4 = (f32[128,512]{1,0:T(8,128)S(1)}, f32[128,512]{1,0:T(8,128)S(1)}, u32[]{:S(2)}, u32[]{:S(2)}) collective-permute-start(f32[128,512]{1,0:T(8,128)S(1)} %sum.1), channel_id=1, source_target_pairs={{11,2},{14,7},{18,11},{23,14},{27,18},{30,23},{34,27},{39,30},{43,... | collective-permute-start | bytes 786440 | tf_op jit(solution)/shard_map/ppermute | solution.py:224
  12.6 6.4 %collective-permute-start.3 = (f32[128,512]{1,0:T(8,128)S(1)}, f32[128,512]{1,0:T(8,128)S(1)}, u32[]{:S(2)}, u32[]{:S(2)}) collective-permute-start(f32[128,512]{1,0:T(8,128)S(1)} %sum.1), channel_id=1, source_target_pairs={{11,7},{14,2},{18,14},{23,11},{27,23},{30,18},{34,30},{39,27},{43,... | collective-permute-start | bytes 786440 | tf_op jit(solution)/shard_map/ppermute | solution.py:224
  20.5 3.1 %collective-permute-start.9 = (f32[128,512]{1,0:T(8,128)S(1)}, f32[128,512]{1,0:T(8,128)S(1)}, u32[]{:S(2)}, u32[]{:S(2)}) collective-permute-start(f32[128,512]{1,0:T(8,128)S(1)} %get-tuple-element.105), channel_id=1, source_target_pairs={{11,2},{14,7},{18,11},{23,14},{27,18},{30,23},{34,27},{39,30},{43,... | collective-permute-start | bytes 786440 | tf_op jit(solution)/shard_map/ppermute | solution.py:224
  21.2 2.4 %collective-permute-start.8 = (f32[128,512]{1,0:T(8,128)S(1)}, f32[128,512]{1,0:T(8,128)S(1)}, u32[]{:S(2)}, u32[]{:S(2)}) collective-permute-start(f32[128,512]{1,0:T(8,128)S(1)} %get-tuple-element.105), channel_id=1, source_target_pairs={{11,7},{14,2},{18,14},{23,11},{27,23},{30,18},{34,30},{39,27},{43,... | collective-permute-start | bytes 786440 | tf_op jit(solution)/shard_map/ppermute | solution.py:224
  25.2 3.1 %collective-permute-start.11 = (f32[128,512]{1,0:T(8,128)S(1)}, f32[128,512]{1,0:T(8,128)S(1)}, u32[]{:S(2)}, u32[]{:S(2)}) collective-permute-start(f32[128,512]{1,0:T(8,128)S(1)} %get-tuple-element.130), channel_id=1, source_target_pairs={{11,2},{14,7},{18,11},{23,14},{27,18},{30,23},{34,27},{39,30},{43,... | collective-permute-start | bytes 786440 | tf_op jit(solution)/shard_map/ppermute | solution.py:224
  25.9 2.4 %collective-permute-start.10 = (f32[128,512]{1,0:T(8,128)S(1)}, f32[128,512]{1,0:T(8,128)S(1)}, u32[]{:S(2)}, u32[]{:S(2)}) collective-permute-start(f32[128,512]{1,0:T(8,128)S(1)} %get-tuple-element.130), channel_id=1, source_target_pairs={{11,7},{14,2},{18,14},{23,11},{27,23},{30,18},{34,30},{39,27},{43,... | collective-permute-start | bytes 786440 | tf_op jit(solution)/shard_map/ppermute | solution.py:224
  31.6 55.4 %all-to-all-start = ((f32[8,16,512]{2,1,0:T(8,128)}), f32[8,16,512]{2,1,0:T(8,128)S(1)}, u32[]{:S(2)}, u32[]{:S(2)}) async-start(f32[8,16,512]{2,1,0:T(8,128)} %bitcast.2), calls=%async_computation | async-start | bytes 524288 | tf_op jit(solution)/shard_map/all_to_all | solution.py:268
  82.2 12.5 %collective-permute-start.13 = (f32[256,512]{1,0:T(8,128)}, f32[256,512]{1,0:T(8,128)S(1)}, u32[]{:S(2)}, u32[]{:S(2)}) collective-permute-start(f32[256,512]{1,0:T(8,128)} %get-tuple-element.165), channel_id=1, source_target_pairs={{2,0},{7,5},{11,9},{14,12},{18,16},{23,21},{27,25},{30,28},{34,32}... | collective-permute-start | bytes 1572872 | tf_op jit(solution)/shard_map/ppermute | solution.py:215
  82.9 11.8 %collective-permute-start.14 = (f32[256,512]{1,0:T(8,128)S(1)}, f32[256,512]{1,0:T(8,128)S(1)}, u32[]{:S(2)}, u32[]{:S(2)}) collective-permute-start(f32[256,512]{1,0:T(8,128)S(1)} %get-tuple-element.166), channel_id=1, source_target_pairs={{2,4},{7,1},{11,13},{14,8},{18,20},{23,17},{27,29},{30,24},{34,36}... | collective-permute-start | bytes 1572872 | tf_op jit(solution)/shard_map/ppermute | solution.py:215
  83.6 12.6 %collective-permute-start.15 = (f32[256,512]{1,0:T(8,128)S(1)}, f32[256,512]{1,0:T(8,128)S(1)}, u32[]{:S(2)}, u32[]{:S(2)}) collective-permute-start(f32[256,512]{1,0:T(8,128)S(1)} %get-tuple-element.167), channel_id=1, source_target_pairs={{2,3},{7,6},{11,10},{14,15},{18,19},{23,22},{27,26},{30,31},{34,35... | collective-permute-start | bytes 1572872 | tf_op jit(solution)/shard_map/ppermute | solution.py:215
  87.1 7.6 %collective-permute-start.12 = (f32[16,512]{1,0:T(8,128)S(1)}, f32[16,512]{1,0:T(8,128)S(1)}, u32[]{:S(2)}, u32[]{:S(2)}) collective-permute-start(f32[16,512]{1,0:T(8,128)S(1)} %share.1), channel_id=1, source_target_pairs={{8,0},{16,8},{24,16},{32,24},{40,32},{48,40},{56,48},{64,56},{72,6... | collective-permute-start | bytes 98312 | tf_op jit(solution)/shard_map/ppermute | solution.py:270

commit v12 on v11

--- a/solution.py
+++ b/solution.py
@@ -80,7 +80,10 @@
 def first_kernel(user_hbm, held_hbm, items_hbm, conf_hbm, part, errors_ref, held_ref, raw, items, conf, sems):
     slab, _ = held_ref.shape
     steps, obs, users = items.shape
-    pairs = ((items_hbm, items), (conf_hbm, conf), (held_hbm, held_ref), (user_hbm, raw.at[pl.ds(0, users), :]))
+    half = held_ref.shape[1] // 2
+    columns = [pl.ds(0, half), pl.ds(half, half)]
+    pairs = [(items_hbm, items), (conf_hbm, conf), (held_hbm, held_ref)]
+    pairs += [(user_hbm.at[:, c], raw.at[pl.ds(0, users), c]) for c in columns]
     loads = [pltpu.make_async_copy(source, target, sems.at[i]) for i, (source, target) in enumerate(pairs)]
     for copy in loads:
         copy.start()
@@ -92,12 +95,15 @@
         raw[at : at + obs, users:] = conf[s].astype(jnp.float32)
     weights, targets = weigh(items[0], conf[0].astype(jnp.float32), slab)
     loads[2].wait()
-    loads[3].wait()
-    held = held_ref[...]
-    user = halves(raw[:users, :])
-    errors = halves(weights * product(halves(held), user, NT) - targets)
+    scores, user = jnp.zeros((slab, users), jnp.float32), []
+    for c, load in zip(columns, loads[3:]):
+        load.wait()
+        user.append(halves(raw[:users, c]))
+        scores += product(halves(held_ref[:, c]), user[-1], NT)
+    errors = halves(weights * scores - targets)
     errors_ref[0], errors_ref[1] = errors
-    part[...] = kept() * held - LEARN_RATE * product(errors, user, NN)
+    for c, piece in zip(columns, user):
+        part[:, c] = kept() * held_ref[:, c] - LEARN_RATE * product(errors, piece, NN)
 
 
 def pack_kernel(raw, held_ref, errors_ref, pack):
@@ -232,7 +238,7 @@
         [((slab, rank), f32), ((2, slab, users), bf16), ((slab, rank), f32), ((rows, rank), f32)],
         "first",
         in_specs=[hbm] * 4,
-        scratch_shapes=[pltpu.VMEM(items.shape, jnp.int32)] * 2 + [pltpu.SemaphoreType.DMA((4,))],
+        scratch_shapes=[pltpu.VMEM(items.shape, jnp.int32)] * 2 + [pltpu.SemaphoreType.DMA((5,))],
     )(*[pltpu.with_memory_space_constraint(x, pltpu.HBM) for x in (user_factors, item_factors, items, conf)])
     (pack,) = call(pack_kernel, [((rows, rank), f32)], "pack")(raw, slab_copy, first_errors)
     arrived = [part] + [fetch(part, helpers) for helpers in HELPERS]

time: 97.6 us -> 97.5 us (level)
  no operation moved by 1% of the time
where the time goes in v12:
time: 97.5 us; the launch traced here: 97 us
  starting transfers between devices  72 us (74%)
  Pallas kernels  14 us (14%)
  waiting for transfers between devices  10 us (10%)
    all_to_all x1, starting transfers between devices, local(): parts = lax.all_to_all(out.reshape(n, share_rows, rank), 'split', 0, 0)  50.5 us
    ppermute x6, starting transfers between devices, fetch(): return lax.ppermute(x, both, pairs)  8.79 us
    ppermute x1, starting transfers between devices, local(): lax.ppermute(share, 'blk', [((b + 1) % blocks, b) for b in range(blocks)])  5.98 us
    ppermute x6, waiting for transfers between devices, fetch(): return lax.ppermute(x, both, pairs)  4.69 us
    ppermute x6, starting transfers between devices, onward(): return [lax.ppermute(x, both, cross), lax.ppermute(x, both, same)]  4.06 us
    pallas_call x2, Pallas kernels, local(): call(kernel, [factors, *ready] * chunks, 'users')  3.43 us
    pallas_call x1, Pallas kernels, local(): call(kernel, [((slab, rank), f32)] + [factors] * chunks, 'last', out_spec...  3.26 us
    pallas_call x2, Pallas kernels, local(): out, *errors = call(kernel, outs, 'group')(*held, *ahead)  3.17 us
  transfers between devices with their start and end apart: 17, of which 4 were waited for; matrix products, arithmetic and copies ran while one was open for 0% of the time, Pallas kernels for 5%

profile of v12, /device:TPU:6, one launch (start us, length us, event | category | flops | bytes accessed | tf_op | source)
XLA Modules:
  0.0 97.0 jit_solution(12739822564628324495)
XLA Ops:
  0.6 1.9 %first.1 = (f32[128,512]{1,0:T(8,128)S(1)}, bf16[2,128,256]{2,1,0:T(8,128)(2,1)S(1)}, f32[128,512]{1,0:T(8,128)S(1)}, f32[288,512]{1,0:T(8,128)S(1)}) custom-call(f32[256,512]{1,0:T(8,128)} %user_hbm.1, f32[128,512]{1,0:T(8,128)} %held_hbm.1, s32[4,8,256]{2,1,0:T(8,128)} %bitcast.3, s32[4,8,256]{2,1,0:T(8,128)} %bitcast.4), custom_call_target="tpu_custom_call" | custom-call | tf_op jit(solution)/shard_map/first/pallas_call | solution.py:236
  2.5 3.5 %collective-permute-start.2 = (f32[128,512]{1,0:T(8,128)S(1)}, f32[128,512]{1,0:T(8,128)S(1)}, u32[]{:S(2)}, u32[]{:S(2)}) collective-permute-start(f32[128,512]{1,0:T(8,128)S(1)} %get-tuple-element.85.refs_0_), channel_id=1, source_target_pairs={{3,2},{6,7},{10,11},{15,14},{19,18},{22,23},{26,27},{31,30},{35,34... | collective-permute-start | bytes 786440 | tf_op jit(solution)/shard_map/ppermute | solution.py:217
  6.0 0.7 collective-permute-start.1
  7.8 2.5 %collective-permute-start.7 = (f32[288,512]{1,0:T(8,128)S(1)}, f32[288,512]{1,0:T(8,128)S(1)}, u32[]{:S(2)}, u32[]{:S(2)}) collective-permute-start(f32[288,512]{1,0:T(8,128)S(1)} %pack.1.refs_0_.refs_10_.refs_14_), channel_id=1, source_target_pairs={{3,2},{6,7},{10,11},{15,14},{19,18},{22,23},{26,27},{31,30},{35,34... | collective-permute-start | bytes 1769480 | tf_op jit(solution)/shard_map/ppermute | solution.py:217
  10.3 0.7 collective-permute-start.6
  11.0 0.7 collective-permute-start.5
  11.8 0.7 collective-permute-start.4
  12.5 0.7 collective-permute-start.3
  13.2 4.7 %collective-permute-done.7.refs_3_.refs_13_.refs_17_ = f32[288,512]{1,0:T(8,128)S(1)} collective-permute-done((f32[288,512]{1,0:T(8,128)S(1)}, f32[288,512]{1,0:T(8,128)S(1)}, u32[]{:S(2)}, u32[]{:S(2)}) %collective-permute-start.7) | collective-permute-done | bytes 589856 | tf_op jit(solution)/shard_map/ppermute | solution.py:217
  17.9 1.0 %prepare.1 = (bf16[256,512]{1,0:T(8,128)(2,1)S(1)}, bf16[256,512]{1,0:T(8,128)(2,1)S(1)}, f32[128,256]{1,0:T(8,128)S(1)}, f32[128,256]{1,0:T(8,128)S(1)}, bf16[2...) custom-call(f32[288,512]{1,0:T(8,128)S(1)} %pack.1.refs_0_.refs_10_., ...), custom_call_target="tpu_custom_call" | custom-call | tf_op jit(solution)/shard_map/prepare/pallas_call | solution.py:252
  18.9 1.6 %group.2 = (f32[128,512]{1,0:T(8,128)S(1)}, bf16[128,256]{1,0:T(8,128)(2,1)S(1)}, bf16[128,256]{1,0:T(8,128)(2,1)S(1)}, bf16[128,256]{1,0:T(8,128)(2,1)S(1)}, bf...) custom-call(f32[128,512]{1,0:T(8,128)S(1)} %collective-permute-done., ...), custom_call_target="tpu_custom_call" | custom-call | tf_op jit(solution)/shard_map/group/pallas_call | solution.py:257
  21.8 1.7 %users.2 = (f32[256,512]{1,0:T(8,128)S(1)}, bf16[256,512]{1,0:T(8,128)(2,1)S(1)}, bf16[256,512]{1,0:T(8,128)(2,1)S(1)}, f32[128,256]{1,0:T(8,128)S(1)}, f32[128,...) custom-call(f32[128,512]{1,0:T(8,128)S(1)} %collective-permute-done., ...), custom_call_target="tpu_custom_call" | custom-call | tf_op jit(solution)/shard_map/users/pallas_call | solution.py:260
  23.6 1.6 %group.3 = (f32[128,512]{1,0:T(8,128)S(1)}, bf16[128,256]{1,0:T(8,128)(2,1)S(1)}, bf16[128,256]{1,0:T(8,128)(2,1)S(1)}, bf16[128,256]{1,0:T(8,128)(2,1)S(1)}, bf...) custom-call(f32[128,512]{1,0:T(8,128)S(1)} %collective-permute-done., ...), custom_call_target="tpu_custom_call" | custom-call | tf_op jit(solution)/shard_map/group/pallas_call | solution.py:257
  26.6 1.7 %users.3 = (f32[256,512]{1,0:T(8,128)S(1)}, bf16[256,512]{1,0:T(8,128)(2,1)S(1)}, bf16[256,512]{1,0:T(8,128)(2,1)S(1)}, f32[128,256]{1,0:T(8,128)S(1)}, f32[128,...) custom-call(f32[128,512]{1,0:T(8,128)S(1)} %collective-permute-done., ...), custom_call_target="tpu_custom_call" | custom-call | tf_op jit(solution)/shard_map/users/pallas_call | solution.py:260
  28.3 3.3 %last.1 = (f32[128,512]{1,0:T(8,128)}, f32[256,512]{1,0:T(8,128)S(1)}, f32[256,512]{1,0:T(8,128)}, f32[256,512]{1,0:T(8,128)S(1)}, f32[256,512]{1,0:T(8,128)S(1)}) custom-call(f32[128,512]{1,0:T(8,128)S(1)} %collective-permute-done.10.refs_0_, f32[128,512]{1,0:T(8,128)S(1)} %collective-permute-done.11.refs_1_, ...), custom_call_target="tpu_custom_call" | custom-call | tf_op jit(solution)/shard_map/last/pallas_call | solution.py:266
  31.6 50.5 %all-to-all-start = ((f32[8,16,512]{2,1,0:T(8,128)}), f32[8,16,512]{2,1,0:T(8,128)S(1)}, u32[]{:S(2)}, u32[]{:S(2)}) async-start(f32[8,16,512]{2,1,0:T(8,128)} %bitcast.2), calls=%async_computation | async-start | bytes 524288 | tf_op jit(solution)/shard_map/all_to_all | solution.py:274
  82.1 0.7 collective-permute-start.13
  82.8 0.7 collective-permute-start.14
  83.5 1.3 %collective-permute-start.15 = (f32[256,512]{1,0:T(8,128)S(1)}, f32[256,512]{1,0:T(8,128)S(1)}, u32[]{:S(2)}, u32[]{:S(2)}) collective-permute-start(f32[256,512]{1,0:T(8,128)S(1)} %get-tuple-element.167), channel_id=1, source_target_pairs={{2,3},{7,6},{11,10},{14,15},{18,19},{23,22},{27,26},{30,31},{34,35... | collective-permute-start | bytes 1572872 | tf_op jit(solution)/shard_map/ppermute | solution.py:221
  84.8 2.2 %all-to-all-done.parts_ref = f32[8,16,512]{2,1,0:T(8,128)S(1)} async-done(((f32[8,16,512]{2,1,0:T(8,128)}), f32[8,16,512]{2,1,0:T(8,128)S(1)}, u32[]{:S(2)}, u32[]{:S(2)}) %all-to-all-start) | async-done | bytes 262176 | tf_op jit(solution)/shard_map/all_to_all | solution.py:274
  87.0 6.0 %collective-permute-start.12 = (f32[16,512]{1,0:T(8,128)S(1)}, f32[16,512]{1,0:T(8,128)S(1)}, u32[]{:S(2)}, u32[]{:S(2)}) collective-permute-start(f32[16,512]{1,0:T(8,128)S(1)} %share.1), channel_id=1, source_target_pairs={{8,0},{16,8},{24,16},{32,24},{40,32},{48,40},{56,48},{64,56},{72,6... | collective-permute-start | bytes 98312 | tf_op jit(solution)/shard_map/ppermute | solution.py:276
  93.0 1.6 %collective-permute-done.12.share_ref = f32[16,512]{1,0:T(8,128)S(1)} collective-permute-done((f32[16,512]{1,0:T(8,128)S(1)}, f32[16,512]{1,0:T(8,128)S(1)}, u32[]{:S(2)}, u32[]{:S(2)}) %collective-permute-start.12) | collective-permute-done | bytes 32800 | tf_op jit(solution)/shard_map/ppermute | solution.py:276
  94.6 1.5 %collective-permute-done.15.c_ref = f32[256,512]{1,0:T(8,128)S(1)} collective-permute-done((f32[256,512]{1,0:T(8,128)S(1)}, f32[256,512]{1,0:T(8,128)S(1)}, u32[]{:S(2)}, u32[]{:S(2)}) %collective-permute-start.15) | collective-permute-done | bytes 524320 | tf_op jit(solution)/shard_map/ppermute | solution.py:221
  96.1 0.8 home.1
  (21 shorter events, 3.9 us)
Async XLA Ops:
  2.5 8.5 %collective-permute-start.2 = (f32[128,512]{1,0:T(8,128)S(1)}, f32[128,512]{1,0:T(8,128)S(1)}, u32[]{:S(2)}, u32[]{:S(2)}) collective-permute-start(f32[128,512]{1,0:T(8,128)S(1)} %get-tuple-element.85.refs_0_), channel_id=1, source_target_pairs={{3,2},{6,7},{10,11},{15,14},{19,18},{22,23},{26,27},{31,30},{35,34... | collective-permute-start | bytes 786440 | tf_op jit(solution)/shard_map/ppermute | solution.py:217
  6.0 5.7 %collective-permute-start.1 = (f32[128,512]{1,0:T(8,128)S(1)}, f32[128,512]{1,0:T(8,128)S(1)}, u32[]{:S(2)}, u32[]{:S(2)}) collective-permute-start(f32[128,512]{1,0:T(8,128)S(1)} %get-tuple-element.85.refs_0_), channel_id=1, source_target_pairs={{4,2},{1,7},{13,11},{8,14},{20,18},{17,23},{29,27},{24,30},{36,34}... | collective-permute-start | bytes 786440 | tf_op jit(solution)/shard_map/ppermute | solution.py:217
  6.7 5.1 %collective-permute-start = (f32[128,512]{1,0:T(8,128)S(1)}, f32[128,512]{1,0:T(8,128)S(1)}, u32[]{:S(2)}, u32[]{:S(2)}) collective-permute-start(f32[128,512]{1,0:T(8,128)S(1)} %get-tuple-element.85.refs_0_), channel_id=1, source_target_pairs={{0,2},{5,7},{9,11},{12,14},{16,18},{21,23},{25,27},{28,30},{32,34}... | collective-permute-start | bytes 786440 | tf_op jit(solution)/shard_map/ppermute | solution.py:217
  7.8 10.1 %collective-permute-start.7 = (f32[288,512]{1,0:T(8,128)S(1)}, f32[288,512]{1,0:T(8,128)S(1)}, u32[]{:S(2)}, u32[]{:S(2)}) collective-permute-start(f32[288,512]{1,0:T(8,128)S(1)} %pack.1.refs_0_.refs_10_.refs_14_), channel_id=1, source_target_pairs={{3,2},{6,7},{10,11},{15,14},{19,18},{22,23},{26,27},{31,30},{35,34... | collective-permute-start | bytes 1769480 | tf_op jit(solution)/shard_map/ppermute | solution.py:217
  10.3 7.6 %collective-permute-start.6 = (f32[288,512]{1,0:T(8,128)S(1)}, f32[288,512]{1,0:T(8,128)S(1)}, u32[]{:S(2)}, u32[]{:S(2)}) collective-permute-start(f32[288,512]{1,0:T(8,128)S(1)} %pack.1.refs_0_.refs_10_.refs_14_), channel_id=1, source_target_pairs={{4,2},{1,7},{13,11},{8,14},{20,18},{17,23},{29,27},{24,30},{36,34}... | collective-permute-start | bytes 1769480 | tf_op jit(solution)/shard_map/ppermute | solution.py:217
  11.0 6.8 %collective-permute-start.5 = (f32[288,512]{1,0:T(8,128)S(1)}, f32[288,512]{1,0:T(8,128)S(1)}, u32[]{:S(2)}, u32[]{:S(2)}) collective-permute-start(f32[288,512]{1,0:T(8,128)S(1)} %pack.1.refs_0_.refs_10_.refs_14_), channel_id=1, source_target_pairs={{0,2},{5,7},{9,11},{12,14},{16,18},{21,23},{25,27},{28,30},{32,34}... | collective-permute-start | bytes 1769480 | tf_op jit(solution)/shard_map/ppermute | solution.py:217
  11.8 7.0 %collective-permute-start.4 = (f32[128,512]{1,0:T(8,128)S(1)}, f32[128,512]{1,0:T(8,128)S(1)}, u32[]{:S(2)}, u32[]{:S(2)}) collective-permute-start(f32[128,512]{1,0:T(8,128)S(1)} %sum.1), channel_id=1, source_target_pairs={{11,2},{14,7},{18,11},{23,14},{27,18},{30,23},{34,27},{39,30},{43,... | collective-permute-start | bytes 786440 | tf_op jit(solution)/shard_map/ppermute | solution.py:230
  12.5 6.4 %collective-permute-start.3 = (f32[128,512]{1,0:T(8,128)S(1)}, f32[128,512]{1,0:T(8,128)S(1)}, u32[]{:S(2)}, u32[]{:S(2)}) collective-permute-start(f32[128,512]{1,0:T(8,128)S(1)} %sum.1), channel_id=1, source_target_pairs={{11,7},{14,2},{18,14},{23,11},{27,23},{30,18},{34,30},{39,27},{43,... | collective-permute-start | bytes 786440 | tf_op jit(solution)/shard_map/ppermute | solution.py:230
  20.5 3.1 %collective-permute-start.9 = (f32[128,512]{1,0:T(8,128)S(1)}, f32[128,512]{1,0:T(8,128)S(1)}, u32[]{:S(2)}, u32[]{:S(2)}) collective-permute-start(f32[128,512]{1,0:T(8,128)S(1)} %get-tuple-element.105), channel_id=1, source_target_pairs={{11,2},{14,7},{18,11},{23,14},{27,18},{30,23},{34,27},{39,30},{43,... | collective-permute-start | bytes 786440 | tf_op jit(solution)/shard_map/ppermute | solution.py:230
  21.2 2.4 %collective-permute-start.8 = (f32[128,512]{1,0:T(8,128)S(1)}, f32[128,512]{1,0:T(8,128)S(1)}, u32[]{:S(2)}, u32[]{:S(2)}) collective-permute-start(f32[128,512]{1,0:T(8,128)S(1)} %get-tuple-element.105), channel_id=1, source_target_pairs={{11,7},{14,2},{18,14},{23,11},{27,23},{30,18},{34,30},{39,27},{43,... | collective-permute-start | bytes 786440 | tf_op jit(solution)/shard_map/ppermute | solution.py:230
  25.2 3.1 %collective-permute-start.11 = (f32[128,512]{1,0:T(8,128)S(1)}, f32[128,512]{1,0:T(8,128)S(1)}, u32[]{:S(2)}, u32[]{:S(2)}) collective-permute-start(f32[128,512]{1,0:T(8,128)S(1)} %get-tuple-element.130), channel_id=1, source_target_pairs={{11,2},{14,7},{18,11},{23,14},{27,18},{30,23},{34,27},{39,30},{43,... | collective-permute-start | bytes 786440 | tf_op jit(solution)/shard_map/ppermute | solution.py:230
  25.9 2.4 %collective-permute-start.10 = (f32[128,512]{1,0:T(8,128)S(1)}, f32[128,512]{1,0:T(8,128)S(1)}, u32[]{:S(2)}, u32[]{:S(2)}) collective-permute-start(f32[128,512]{1,0:T(8,128)S(1)} %get-tuple-element.130), channel_id=1, source_target_pairs={{11,7},{14,2},{18,14},{23,11},{27,23},{30,18},{34,30},{39,27},{43,... | collective-permute-start | bytes 786440 | tf_op jit(solution)/shard_map/ppermute | solution.py:230
  31.6 55.5 %all-to-all-start = ((f32[8,16,512]{2,1,0:T(8,128)}), f32[8,16,512]{2,1,0:T(8,128)S(1)}, u32[]{:S(2)}, u32[]{:S(2)}) async-start(f32[8,16,512]{2,1,0:T(8,128)} %bitcast.2), calls=%async_computation | async-start | bytes 524288 | tf_op jit(solution)/shard_map/all_to_all | solution.py:274
  82.1 12.5 %collective-permute-start.13 = (f32[256,512]{1,0:T(8,128)}, f32[256,512]{1,0:T(8,128)S(1)}, u32[]{:S(2)}, u32[]{:S(2)}) collective-permute-start(f32[256,512]{1,0:T(8,128)} %get-tuple-element.165), channel_id=1, source_target_pairs={{2,0},{7,5},{11,9},{14,12},{18,16},{23,21},{27,25},{30,28},{34,32}... | collective-permute-start | bytes 1572872 | tf_op jit(solution)/shard_map/ppermute | solution.py:221
  82.8 11.8 %collective-permute-start.14 = (f32[256,512]{1,0:T(8,128)S(1)}, f32[256,512]{1,0:T(8,128)S(1)}, u32[]{:S(2)}, u32[]{:S(2)}) collective-permute-start(f32[256,512]{1,0:T(8,128)S(1)} %get-tuple-element.166), channel_id=1, source_target_pairs={{2,4},{7,1},{11,13},{14,8},{18,20},{23,17},{27,29},{30,24},{34,36}... | collective-permute-start | bytes 1572872 | tf_op jit(solution)/shard_map/ppermute | solution.py:221
  83.5 12.6 %collective-permute-start.15 = (f32[256,512]{1,0:T(8,128)S(1)}, f32[256,512]{1,0:T(8,128)S(1)}, u32[]{:S(2)}, u32[]{:S(2)}) collective-permute-start(f32[256,512]{1,0:T(8,128)S(1)} %get-tuple-element.167), channel_id=1, source_target_pairs={{2,3},{7,6},{11,10},{14,15},{18,19},{23,22},{27,26},{30,31},{34,35... | collective-permute-start | bytes 1572872 | tf_op jit(solution)/shard_map/ppermute | solution.py:221
  87.0 7.6 %collective-permute-start.12 = (f32[16,512]{1,0:T(8,128)S(1)}, f32[16,512]{1,0:T(8,128)S(1)}, u32[]{:S(2)}, u32[]{:S(2)}) collective-permute-start(f32[16,512]{1,0:T(8,128)S(1)} %share.1), channel_id=1, source_target_pairs={{8,0},{16,8},{24,16},{32,24},{40,32},{48,40},{56,48},{64,56},{72,6... | collective-permute-start | bytes 98312 | tf_op jit(solution)/shard_map/ppermute | solution.py:276
